TPU v7x, 256 devices: a whole 4x4x8 slice. The times are simulated.
256 devices in a mesh: row: 16 (over z_hi, x, core), col: 16 (over z_lo, y).
Axes of the slice: x: 4, y: 4, z: 8 (z_hi: 2, z_lo: 4; z = z_hi * 4 + z_lo), core: 2. Of those that a mesh axis runs over, the one named last changes fastest.
Arguments:
- orbitals: bfloat16 [1024, 16384], P(('row', 'col')), may hold values from -0.09375 to 0.09375
- gradient: bfloat16 [1024, 16384], P(('row', 'col')), may hold values from -6 to 6
- stored: float32 [16384, 16384], P('row', 'col'), as said below
Outputs:
- projected: bfloat16 [1024, 16384], P(('row', 'col'))
Inputs may be any that keep to these rules, and one draw needn't show every extreme that they name: stored is exactly symmetric: stored[i, j] equals stored[j, i].
All inputs are finite; a program needn't handle non-finite values.
Results may differ from a plain program's by a relative error of at most 0.0034.
Values may be sent and summed in bfloat16 or wider, within the bound.
No kernel may reach another device: no remote copies, remote signals or barrier semaphores. Data moves between devices by JAX's collectives and lax.ppermute only.
A program may use at most 64 MiB of HBM per device.

v0:
```python
import jax
import jax.numpy as jnp
from jax import lax
from jax.experimental import pallas as pl
from jax.experimental.pallas import tpu as pltpu
from jax.sharding import Mesh, PartitionSpec as P

AXES = ("zh", "x", "core", "zl", "y")
SIZES = {"zh": 2, "x": 4, "core": 2, "zl": 4, "y": 4}
F32, BF16 = jnp.float32, jnp.bfloat16


def shift(value, axis, step):
    n = SIZES[axis]
    return lax.ppermute(value, axis, [(i, (i + step) % n) for i in range(n)])


def pick(value, index, dim=0):
    return lax.dynamic_index_in_dim(value, index, dim, keepdims=False)


def exchange(pieces, axis, dim):
    n = SIZES[axis]
    me = lax.axis_index(axis)
    sent = [pick(pieces, (me + d) % n, dim) for d in range(n)]
    return jnp.stack([sent[0]] + [shift(sent[d], axis, d) for d in range(1, n)])


def gather(block, axis):
    return [block] + [shift(block, axis, d) for d in range(1, SIZES[axis])]


def gather_ring(block, axis):
    half = block.shape[0] // 2
    left, right = shift(block, axis, 1), shift(block, axis, -1)
    return block, left, shift(left[:half], axis, 1), shift(right[half:], axis, -1), right


def dot(left, right, dims):
    return lax.dot_general(left, right, (dims, ((), ())), preferred_element_type=F32)


def early_kernel(a0, a1, a3, cols, out):
    total = None
    for a, j in ((a0, 0), (a1, 1), (a3, 3)):
        term = dot(flat(a[...]), flat(cols[j]), ((0,), (0,)))
        total = term if total is None else total + term
    out[...] = total


def share_kernel(a0, a1, a2, a2b, a3, e0, e1, e2, e3, cols, early, kept, out):
    wa = early.shape[0]
    rows = a0.shape[1] // 2
    main = early[...]
    main += dot(flat(a2[...]), flat(cols[2, :2]), ((0,), (0,)))
    main += dot(flat(a2b[...]), flat(cols[2, 2:]), ((0,), (0,)))
    main = (0.5 * main + kept[:wa]).astype(BF16)
    side = None
    for d, e in enumerate((e0, e1, e2, e3)):
        term = dot(flat(e[...]), flat(cols[:, d]), ((0,), (0,)))
        side = term if side is None else side + term
    side = (0.5 * side + kept[wa:]).astype(BF16)
    for a, j, lo in ((a0, 0, 0), (a1, 1, 0), (a2, 2, 0), (a2b, 2, 2), (a3, 3, 0)):
        n = a.shape[0]
        upper = dot(flat(a[:, :rows]), main, ((1,), (0,)))
        for z in range(n):
            e = (e0, e1, e2, e3)[lo + z]
            out[j, lo + z] = upper[z * rows : (z + 1) * rows] + dot(e[j, :rows], side, ((1,), (0,)))


def flat(value):
    return value.reshape(-1, value.shape[-1])


def call(kernel, shape, flops, *args):
    spec = pl.BlockSpec(memory_space=pltpu.VMEM)
    size = sum(a.size * a.dtype.itemsize for a in args)
    return pl.pallas_call(
        kernel,
        out_shape=jax.ShapeDtypeStruct(shape, F32),
        in_specs=[spec] * len(args),
        out_specs=spec,
        compiler_params=pltpu.CompilerParams(vmem_limit_bytes=48 << 20),
        cost_estimate=pl.CostEstimate(flops=flops, bytes_accessed=size, transcendentals=0),
    )(*args)


def body(orbitals, gradient, stored):
    k, n = orbitals.shape
    rows, w, hw = 2 * k, n // 16, n // 32
    wa = 3 * w // 4
    core, zl, y = (lax.axis_index(a) for a in ("core", "zl", "y"))

    own = jnp.stack([orbitals, gradient])
    sibling = shift(own, "core", 1)
    both = jnp.where(core == 0, jnp.concatenate([own, sibling], 1), jnp.concatenate([sibling, own], 1))

    to_r = pick(both.reshape(2, rows, 2, 4, 2, w), core, 4).transpose(3, 2, 0, 1, 4)
    to_c = pick(both[::-1].reshape(2, rows, 4, 4, 2, hw), core, 4).transpose(2, 3, 0, 1, 4)

    part_r = exchange(to_r, "x", 0)
    part_r = exchange(part_r, "zh", 1).transpose(2, 0, 1, 3, 4).reshape(16 * rows, w)
    part_c = exchange(to_c, "zl", 0)
    part_c = jnp.stack(gather(part_c, "zh"))
    part_c = exchange(part_c, "y", 2)

    near = jnp.stack(gather(part_r[:, :wa], "zl"))
    edge = jnp.stack(gather(part_r[:, wa:], "y"))
    a0, a1, a2, a2b, a3 = gather_ring(near, "y")
    edges = gather(edge, "zl")

    c0, c1, c2, c2b, c3 = gather_ring(part_c, "x")
    panel = jnp.stack([c0, c1, jnp.concatenate([c2, c2b]), c3])
    panel = panel.transpose(1, 3, 4, 2, 0, 5, 6).reshape(4, 4, 16 * rows, hw)
    other = shift(panel, "core", 1)

    def share(cols, which):
        kept = lax.dynamic_slice_in_dim(stored, which * hw, hw, 1)
        early = call(early_kernel, (wa, hw), 2 * 192 * rows * wa * hw, a0, a1, a3, cols)
        flops = 2 * 64 * rows * (wa + 4 * (w - wa)) * hw + 2 * 128 * rows * w * hw
        return call(share_kernel, (4, 4, 8 * rows, hw), flops, a0, a1, a2, a2b, a3, *edges, cols, early, kept)

    away = shift(share(other, 1 - core), "core", 1)
    total = (share(panel, core) + away).reshape(16, 2, 4, rows, hw)

    got = [shift(total[:, :, 4 - d].astype(BF16), "x", d) for d in range(1, 4)]
    total = total[:, :, 0] + sum(g.astype(F32) for g in got)
    total = total[:, 0] + shift(total[:, 1].astype(BF16), "zh", 1).astype(F32)

    mine = part_c[:, 0, :, 0].reshape(16, rows, hw).astype(F32)
    result = (mine - total).astype(BF16).reshape(4, 4, rows, hw)
    back = result[::-1, ::-1]
    back = lax.dynamic_slice_in_dim(jnp.concatenate([back, back], 0), 3 - y, 4, 0)
    back = lax.dynamic_slice_in_dim(jnp.concatenate([back, back], 1), 3 - zl, 4, 1)
    result = lax.all_to_all(
        back.transpose(1, 0, 2, 3).reshape(16, rows, hw), ("zl", "y"), split_axis=0, concat_axis=0, tiled=True
    )
    result = result.reshape(16, 2, k, hw)
    kept, got = pick(result, core, 1), shift(pick(result, 1 - core, 1), "core", 1)
    halves = jnp.where(core == 0, jnp.stack([kept, got]), jnp.stack([got, kept]))
    return halves.transpose(2, 1, 0, 3).reshape(k, n)


def solution(mesh):
    fine = Mesh(mesh.devices.reshape(tuple(SIZES.values())), AXES)
    return jax.shard_map(
        body,
        mesh=fine,
        in_specs=(P(AXES, None), P(AXES, None), P(("zh", "x", "core"), ("zl", "y"))),
        out_specs=P(AXES, None),
        check_vma=False,
    )
```

profile of v0, /device:TPU:2, one launch (start us, length us, event | category | flops | bytes accessed | tf_op | source)
XLA Modules:
  0.0 219.4 jit_solution(16706091273688667946)
XLA Ops:
  0.0 1.2 pad_maximum_fusion.2
  1.3 1.4 collective-permute-done
  2.8 1.6 maximum_select_fusion
  4.5 4.7 %collective-permute-start.3 = (bf16[4,2,8,512]{3,2,0,1:T(8,128)(2,1)S(1)}, bf16[4,2,8,512]{3,2,0,1:T(8,128)(2,1)S(1)}, u32[]{:S(2)}, u32[]{:S(2)}) collective-permute-start(bf16[4,2,8,512]{3,2,0,1:T(8,128)(2,1)S(1)} %get-tuple-element.17), channel_id=1, source_target_pairs={{0,12},{4,0},{8,4},{12,8},{1,13},{5,1},{9,5},{13,9},{2,14},{6,2},{... | collective-permute-start | bytes 196616 | tf_op jit(solution)/shard_map/ppermute | solution.py:15
  9.2 0.7 collective-permute-start.1
  9.8 1.8 collective-permute-done.3
  11.7 4.1 %collective-permute-done.2 = bf16[4,2,8,512]{3,2,0,1:T(8,128)(2,1)S(1)} collective-permute-done((bf16[4,2,8,512]{3,2,0,1:T(8,128)(2,1)S(1)}, bf16[4,2,8,512]{3,2,0,1:T(8,128)(2,1)S(1)}, u32[]{:S(2)}, u32[]{:S(2)}) %collective-permute-start.2) | collective-permute-done | bytes 65568 | tf_op jit(solution)/shard_map/ppermute | solution.py:15
  15.8 5.3 %collective-permute-start.4 = (bf16[4,4,2,8,512]{4,3,1,0,2:T(8,128)(2,1)S(1)}, bf16[4,4,2,8,512]{4,3,1,0,2:T(8,128)(2,1)S(1)}, u32[]{:S(2)}, u32[]{:S(2)}) collective-permute-start(bf16[4,4,2,8,512]{4,3,1,0,2:T(8,128)(2,1)S(1)} %get-tuple-element.24), channel_id=1, source_target_pairs={{0,128},{128,0},{1,129},{129,1},{2,130},{130,2},{3,131},{131,3},{4... | collective-permute-start | bytes 786440 | tf_op jit(solution)/shard_map/ppermute | solution.py:15
  21.1 7.5 %collective-permute-done.4 = bf16[4,4,2,8,512]{4,3,1,0,2:T(8,128)(2,1)S(1)} collective-permute-done((bf16[4,4,2,8,512]{4,3,1,0,2:T(8,128)(2,1)S(1)}, bf16[4,4,2,8,512]{4,3,1,0,2:T(8,128)(2,1)S(1)}, u32[]{:S(2)}, u32[]{:S(2)}) %collective-permute-start.4) | collective-permute-done | bytes 262176 | tf_op jit(solution)/shard_map/ppermute | solution.py:15
  28.7 3.1 %collective-permute-start.7 = (bf16[2,4,2,8,512]{4,3,2,1,0:T(8,128)(2,1)S(1)}, bf16[2,4,2,8,512]{4,3,2,1,0:T(8,128)(2,1)S(1)}, u32[]{:S(2)}, u32[]{:S(2)}) collective-permute-start(bf16[2,4,2,8,512]{4,3,2,1,0:T(8,128)(2,1)S(1)} %bitcast.177), channel_id=1, source_target_pairs={{0,3},{1,0},{2,1},{3,2},{4,7},{5,4},{6,5},{7,6},{8,11},{9,8},{10,9... | collective-permute-start | bytes 393224 | tf_op jit(solution)/shard_map/ppermute | solution.py:15
  31.8 0.7 collective-permute-start.6
  32.6 1.0 collective-permute-start.5
  33.6 0.9 collective-permute-done.7
  34.5 4.0 %collective-permute-done.6 = bf16[2,4,2,8,512]{4,3,2,1,0:T(8,128)(2,1)S(1)} collective-permute-done((bf16[2,4,2,8,512]{4,3,2,1,0:T(8,128)(2,1)S(1)}, bf16[2,4,2,8,512]{4,3,2,1,0:T(8,128)(2,1)S(1)}, u32[]{:S(2)}, u32[]{:S(2)}) %collective-permute-start.6) | collective-permute-done | bytes 131104 | tf_op jit(solution)/shard_map/ppermute | solution.py:15
  38.5 1.3 collective-permute-done.5
  39.9 0.6 collective-permute-start.27
  40.5 1.5 collective-permute-start.25
  42.0 10.0 %collective-permute-done.27 = bf16[4,2,4,2,8,512]{5,4,3,2,1,0:T(8,128)(2,1)S(1)} collective-permute-done((bf16[4,2,4,2,8,512]{5,4,3,2,1,0:T(8,128)(2,1)S(1)}, bf16[4,2,4,2,8,512]{5,4,3,2,1,0:T(8,128)(2,1)S(1)}, u32[]{:S(2)}, u32[]{:S(2)}) %collective-permute-start.27) | collective-permute-done | bytes 524320 | tf_op jit(solution)/shard_map/ppermute | solution.py:15
  52.0 0.3 collective-permute-start.28
  52.3 1.8 collective-permute-start.26
  54.2 0.5 maximum_select_fusion.1
  54.7 3.8 %collective-permute-done.28 = bf16[2,2,4,2,8,512]{5,4,3,2,1,0:T(8,128)(2,1)S(1)} collective-permute-done((bf16[2,2,4,2,8,512]{5,4,3,2,1,0:T(8,128)(2,1)S(1)}, bf16[2,2,4,2,8,512]{5,4,3,2,1,0:T(8,128)(2,1)S(1)}, u32[]{:S(2)}, u32[]{:S(2)}) %collective-permute-start.28) | collective-permute-done | bytes 262176 | tf_op jit(solution)/shard_map/ppermute | solution.py:15
  58.4 1.5 collective-permute-done.26
  59.9 1.0 maximum_bitcast_fusion.1
  61.6 3.3 %collective-permute-start.10 = (bf16[2,2,8,1024]{3,2,0,1:T(8,128)(2,1)S(1)}, bf16[2,2,8,1024]{3,2,0,1:T(8,128)(2,1)S(1)}, u32[]{:S(2)}, u32[]{:S(2)}) collective-permute-start(bf16[2,2,8,1024]{3,2,0,1:T(8,128)(2,1)S(1)} %get-tuple-element.21), channel_id=1, source_target_pairs={{0,96},{32,0},{64,32},{96,64},{1,97},{33,1},{65,33},{97,65},{2,98}... | collective-permute-start | bytes 196616 | tf_op jit(solution)/shard_map/ppermute | solution.py:15
  65.0 1.7 collective-permute-start.8
  66.7 0.7 collective-permute-done.10
  67.4 3.3 %collective-permute-done.9 = bf16[2,2,8,1024]{3,2,0,1:T(8,128)(2,1)S(1)} collective-permute-done((bf16[2,2,8,1024]{3,2,0,1:T(8,128)(2,1)S(1)}, bf16[2,2,8,1024]{3,2,0,1:T(8,128)(2,1)S(1)}, u32[]{:S(2)}, u32[]{:S(2)}) %collective-permute-start.9) | collective-permute-done | bytes 65568 | tf_op jit(solution)/shard_map/ppermute | solution.py:15
  70.8 8.1 %collective-permute-start.11 = (bf16[4,2,8,1024]{3,2,0,1:T(8,128)(2,1)S(1)}, bf16[4,2,8,1024]{3,2,0,1:T(8,128)(2,1)S(1)}, u32[]{:S(2)}, u32[]{:S(2)}) collective-permute-start(bf16[4,2,8,1024]{3,2,0,1:T(8,128)(2,1)S(1)} %get-tuple-element.31), channel_id=1, source_target_pairs={{0,128},{128,0},{1,129},{129,1},{2,130},{130,2},{3,131},{131,3},{4... | collective-permute-start | bytes 393224 | tf_op jit(solution)/shard_map/ppermute | solution.py:15
  78.9 3.2 %collective-permute-done.11 = bf16[4,2,8,1024]{3,2,0,1:T(8,128)(2,1)S(1)} collective-permute-done((bf16[4,2,8,1024]{3,2,0,1:T(8,128)(2,1)S(1)}, bf16[4,2,8,1024]{3,2,0,1:T(8,128)(2,1)S(1)}, u32[]{:S(2)}, u32[]{:S(2)}) %collective-permute-start.11) | collective-permute-done | bytes 131104 | tf_op jit(solution)/shard_map/ppermute | solution.py:15
  82.4 9.7 %collective-permute-start.13 = (bf16[128,768]{1,0:T(8,128)(2,1)S(1)}, bf16[128,768]{1,0:T(8,128)(2,1)S(1)}, u32[]{:S(2)}, u32[]{:S(2)}) collective-permute-start(bf16[128,768]{1,0:T(8,128)(2,1)S(1)} %get-tuple-element.29), channel_id=1, source_target_pairs={{0,8},{4,12},{8,0},{12,4},{1,9},{5,13},{9,1},{13,5},{2,10},{6,14},... | collective-permute-start | bytes 589832 | tf_op jit(solution)/shard_map/ppermute | solution.py:15
  92.1 1.9 collective-permute-start.12
  94.1 11.5 %collective-permute-done.13 = bf16[128,768]{1,0:T(8,128)(2,1)S(1)} collective-permute-done((bf16[128,768]{1,0:T(8,128)(2,1)S(1)}, bf16[128,768]{1,0:T(8,128)(2,1)S(1)}, u32[]{:S(2)}, u32[]{:S(2)}) %collective-permute-start.13) | collective-permute-done | bytes 196640 | tf_op jit(solution)/shard_map/ppermute | solution.py:15
  105.8 3.2 %collective-permute-start.17 = (bf16[4,128,768]{2,1,0:T(8,128)(2,1)S(1)}, bf16[4,128,768]{2,1,0:T(8,128)(2,1)}, u32[]{:S(2)}, u32[]{:S(2)}) collective-permute-start(bf16[4,128,768]{2,1,0:T(8,128)(2,1)S(1)} %pad_maximum_fusion.a0), channel_id=1, source_target_pairs={{0,3},{1,0},{2,1},{3,2},{4,7},{5,4},{6,5},{7,6},{8,11},{9,8},{10,9... | collective-permute-start | bytes 2359304 | tf_op jit(solution)/shard_map/ppermute | solution.py:15
  109.1 0.9 collective-permute-start.20
  110.0 11.3 %collective-permute-done.15.a1 = bf16[4,128,768]{2,1,0:T(8,128)(2,1)S(1)} collective-permute-done((bf16[4,128,768]{2,1,0:T(8,128)(2,1)S(1)}, bf16[4,128,768]{2,1,0:T(8,128)(2,1)S(1)}, u32[]{:S(2)}, u32[]{:S(2)}) %collective-permute-start.15) | collective-permute-done | bytes 786464 | tf_op jit(solution)/shard_map/ppermute | solution.py:15
  121.3 0.9 copy-done.1
  122.4 1.0 slice.58
  123.4 2.4 %collective-permute-start.16 = (bf16[2,128,768]{2,1,0:T(8,128)(2,1)S(1)}, bf16[2,128,768]{2,1,0:T(8,128)(2,1)S(1)}, u32[]{:S(2)}, u32[]{:S(2)}) collective-permute-start(bf16[2,128,768]{2,1,0:T(8,128)(2,1)S(1)} %slice.58), channel_id=1, source_target_pairs={{0,1},{1,2},{2,3},{3,0},{4,5},{5,6},{6,7},{7,4},{8,9},{9,10},{10,1... | collective-permute-start | bytes 1179656 | tf_op jit(solution)/shard_map/ppermute | solution.py:15
  125.8 1.0 slice.59
  126.9 0.9 collective-permute-start.18
  128.0 0.9 pad_maximum_fusion.6.e0
  129.0 0.7 collective-permute-start.22
  129.6 1.3 collective-permute-start.23
  130.9 2.8 %collective-permute-start.24 = (bf16[4,128,256]{2,1,0:T(8,128)(2,1)S(1)}, bf16[4,128,256]{2,1,0:T(8,128)(2,1)S(1)}, u32[]{:S(2)}, u32[]{:S(2)}) collective-permute-start(bf16[4,128,256]{2,1,0:T(8,128)(2,1)S(1)} %pad_maximum_fusion.6.e0), channel_id=1, source_target_pairs={{0,12},{4,0},{8,4},{12,8},{1,13},{5,1},{9,5},{13,9},{2,14},{6,2},{... | collective-permute-start | bytes 786440 | tf_op jit(solution)/shard_map/ppermute | solution.py:15
  133.7 4.7 %constant_dynamic-slice_fusion.2 = (f32[1024,512]{1,0:T(8,128)}, f32[1024,512]{1,0:T(8,128)}) fusion(f32[1024,1024]{1,0:T(8,128)} %param.5, s32[]{:T(128)S(6)} %select_n.211, s32[]{:T(128)S(6)} %select_n.210), kind=kLoop, calls=%fused_computation.61 | loop fusion | bytes 8388616 | tf_op jit(solution)/shard_map/dynamic_slice | solution.py:118
  138.4 3.3 %shard_map.39.early = f32[768,512]{1,0:T(8,128)S(1)} custom-call(bf16[4,128,768]{2,1,0:T(8,128)(2,1)S(1)} %pad_maximum_fusion.a0, bf16[4,128,768]{2,1,0:T(8,128)(2,1)S(1)} %copy-done.2, bf16[4,128,768]{2,1,0:T(8,128)(2,1)} %collective-permute-done.17.a3, bf16[4,4,128,512]{3,2,1,0:T(8,128)(2,1)} %collective-permute-done.29.cols), custom_call_target="tpu_custom_call" | custom-call | flops 1207959552 | bytes 4456448 | tf_op jit(solution)/shard_map/pallas_call | solution.py:78
  141.7 3.6 %collective-permute-done.23.e2 = bf16[4,128,256]{2,1,0:T(8,128)(2,1)S(1)} collective-permute-done((bf16[4,128,256]{2,1,0:T(8,128)(2,1)S(1)}, bf16[4,128,256]{2,1,0:T(8,128)(2,1)S(1)}, u32[]{:S(2)}, u32[]{:S(2)}) %collective-permute-start.23) | collective-permute-done | bytes 262176 | tf_op jit(solution)/shard_map/ppermute | solution.py:15
  145.4 6.6 %shard_map.40 = f32[4,4,64,512]{3,2,1,0:T(8,128)} custom-call(bf16[4,128,768]{2,1,0:T(8,128)(2,1)S(1)} %pad_maximum_fusion.a0, bf16[4,128,768]{2,1,0:T(8,128)(2,1)S(1)} %copy-done.2, bf16[2,128,768]{2,1,0:T(8,128)(2,1)S(1)} %collective-permute-done.16.a2, bf16[2,128,768]{2,1,0:T(8,128)(2,1)S(1)} %collective-permute-done.18.a2b, ...), custom_call_target="tpu_custom_call" | custom-call | flops 2013265920 | bytes 9961472 | tf_op jit(solution)/shard_map/pallas_call | solution.py:78
  151.9 2.5 %shard_map.37.early = f32[768,512]{1,0:T(8,128)S(1)} custom-call(bf16[4,128,768]{2,1,0:T(8,128)(2,1)S(1)} %pad_maximum_fusion.a0, bf16[4,128,768]{2,1,0:T(8,128)(2,1)S(1)} %copy-done.2, bf16[4,128,768]{2,1,0:T(8,128)(2,1)} %collective-permute-done.17.a3, bf16[4,4,128,512]{3,2,1,0:T(8,128)(2,1)S(1)} %bitcast.151), custom_call_target="tpu_custom_call" | custom-call | flops 1207959552 | bytes 4456448 | tf_op jit(solution)/shard_map/pallas_call | solution.py:78
  154.5 6.5 %shard_map.38 = f32[4,4,64,512]{3,2,1,0:T(8,128)} custom-call(bf16[4,128,768]{2,1,0:T(8,128)(2,1)S(1)} %pad_maximum_fusion.a0, bf16[4,128,768]{2,1,0:T(8,128)(2,1)S(1)} %copy-done.2, bf16[2,128,768]{2,1,0:T(8,128)(2,1)S(1)} %collective-permute-done.16.a2, bf16[2,128,768]{2,1,0:T(8,128)(2,1)S(1)} %collective-permute-done.18.a2b, ...), custom_call_target="tpu_custom_call" | custom-call | flops 2013265920 | bytes 9961472 | tf_op jit(solution)/shard_map/pallas_call | solution.py:78
  161.0 2.1 add.249
  163.2 9.8 %collective-permute-start.33 = (bf16[16,2,8,512]{3,2,0,1:T(8,128)(2,1)S(1)}, bf16[16,2,8,512]{3,2,0,1:T(8,128)(2,1)S(1)}, u32[]{:S(2)}, u32[]{:S(2)}) collective-permute-start(bf16[16,2,8,512]{3,2,0,1:T(8,128)(2,1)S(1)} %get-tuple-element.8), channel_id=1, source_target_pairs={{0,96},{32,0},{64,32},{96,64},{1,97},{33,1},{65,33},{97,65},{2,98}... | collective-permute-start | bytes 786440 | tf_op jit(solution)/shard_map/ppermute | solution.py:15
  173.0 1.6 collective-permute-start.31
  174.5 5.1 %collective-permute-done.33 = bf16[16,2,8,512]{3,2,0,1:T(8,128)(2,1)S(1)} collective-permute-done((bf16[16,2,8,512]{3,2,0,1:T(8,128)(2,1)S(1)}, bf16[16,2,8,512]{3,2,0,1:T(8,128)(2,1)S(1)}, u32[]{:S(2)}, u32[]{:S(2)}) %collective-permute-start.33) | collective-permute-done | bytes 262176 | tf_op jit(solution)/shard_map/ppermute | solution.py:15
  179.7 5.2 %collective-permute-done.32 = bf16[16,2,8,512]{3,2,0,1:T(8,128)(2,1)S(1)} collective-permute-done((bf16[16,2,8,512]{3,2,0,1:T(8,128)(2,1)S(1)}, bf16[16,2,8,512]{3,2,0,1:T(8,128)(2,1)S(1)}, u32[]{:S(2)}, u32[]{:S(2)}) %collective-permute-start.32) | collective-permute-done | bytes 262176 | tf_op jit(solution)/shard_map/ppermute | solution.py:15
  184.8 0.9 collective-permute-done.31
  185.9 7.0 %collective-permute-start.34 = (bf16[16,8,512]{2,1,0:T(8,128)(2,1)S(1)}, bf16[16,8,512]{2,1,0:T(8,128)(2,1)S(1)}, u32[]{:S(2)}, u32[]{:S(2)}) collective-permute-start(bf16[16,8,512]{2,1,0:T(8,128)(2,1)S(1)} %fusion.7), channel_id=1, source_target_pairs={{0,128},{128,0},{1,129},{129,1},{2,130},{130,2},{3,131},{131,3},{4... | collective-permute-start | bytes 393224 | tf_op jit(solution)/shard_map/ppermute | solution.py:15
  192.9 3.7 %collective-permute-done.34 = bf16[16,8,512]{2,1,0:T(8,128)(2,1)S(1)} collective-permute-done((bf16[16,8,512]{2,1,0:T(8,128)(2,1)S(1)}, bf16[16,8,512]{2,1,0:T(8,128)(2,1)S(1)}, u32[]{:S(2)}, u32[]{:S(2)}) %collective-permute-start.34) | collective-permute-done | bytes 131104 | tf_op jit(solution)/shard_map/ppermute | solution.py:15
  196.8 0.7 copy.40
  197.5 10.6 %all-to-all-start = ((bf16[16,8,512]{2,1,0:T(8,128)(2,1)}), bf16[16,8,512]{2,1,0:T(8,128)(2,1)S(1)}, u32[]{:S(2)}, u32[]{:S(2)}) async-start(bf16[16,8,512]{2,1,0:T(8,128)(2,1)} %bitcast.79), calls=%async_computation | async-start | bytes 262144 | tf_op jit(solution)/shard_map/all_to_all | solution.py:135
  208.1 8.9 %all-to-all-done = bf16[16,8,512]{2,1,0:T(8,128)(2,1)S(1)} async-done(((bf16[16,8,512]{2,1,0:T(8,128)(2,1)}), bf16[16,8,512]{2,1,0:T(8,128)(2,1)S(1)}, u32[]{:S(2)}, u32[]{:S(2)}) %all-to-all-start) | async-done | bytes 131104 | tf_op jit(solution)/shard_map/all_to_all | solution.py:135
  217.3 1.2 collective-permute-done.35
  218.7 0.7 reshape.85
  (69 shorter events, 2.9 us)
Async XLA Ops:
  1.2 1.6 collective-permute-start
  4.5 7.2 %collective-permute-start.3 = (bf16[4,2,8,512]{3,2,0,1:T(8,128)(2,1)S(1)}, bf16[4,2,8,512]{3,2,0,1:T(8,128)(2,1)S(1)}, u32[]{:S(2)}, u32[]{:S(2)}) collective-permute-start(bf16[4,2,8,512]{3,2,0,1:T(8,128)(2,1)S(1)} %get-tuple-element.17), channel_id=1, source_target_pairs={{0,12},{4,0},{8,4},{12,8},{1,13},{5,1},{9,5},{13,9},{2,14},{6,2},{... | collective-permute-start | bytes 196616 | tf_op jit(solution)/shard_map/ppermute | solution.py:15
  9.2 6.6 %collective-permute-start.2 = (bf16[4,2,8,512]{3,2,0,1:T(8,128)(2,1)S(1)}, bf16[4,2,8,512]{3,2,0,1:T(8,128)(2,1)S(1)}, u32[]{:S(2)}, u32[]{:S(2)}) collective-permute-start(bf16[4,2,8,512]{3,2,0,1:T(8,128)(2,1)S(1)} %get-tuple-element.18), channel_id=1, source_target_pairs={{0,8},{4,12},{8,0},{12,4},{1,9},{5,13},{9,1},{13,5},{2,10},{6,14},... | collective-permute-start | bytes 196616 | tf_op jit(solution)/shard_map/ppermute | solution.py:15
  9.2 6.6 %collective-permute-start.1 = (bf16[4,2,8,512]{3,2,0,1:T(8,128)(2,1)S(1)}, bf16[4,2,8,512]{3,2,0,1:T(8,128)(2,1)S(1)}, u32[]{:S(2)}, u32[]{:S(2)}) collective-permute-start(bf16[4,2,8,512]{3,2,0,1:T(8,128)(2,1)S(1)} %get-tuple-element.19), channel_id=1, source_target_pairs={{0,4},{4,8},{8,12},{12,0},{1,5},{5,9},{9,13},{13,1},{2,6},{6,10},{... | collective-permute-start | bytes 196616 | tf_op jit(solution)/shard_map/ppermute | solution.py:15
  15.8 12.8 %collective-permute-start.4 = (bf16[4,4,2,8,512]{4,3,1,0,2:T(8,128)(2,1)S(1)}, bf16[4,4,2,8,512]{4,3,1,0,2:T(8,128)(2,1)S(1)}, u32[]{:S(2)}, u32[]{:S(2)}) collective-permute-start(bf16[4,4,2,8,512]{4,3,1,0,2:T(8,128)(2,1)S(1)} %get-tuple-element.24), channel_id=1, source_target_pairs={{0,128},{128,0},{1,129},{129,1},{2,130},{130,2},{3,131},{131,3},{4... | collective-permute-start | bytes 786440 | tf_op jit(solution)/shard_map/ppermute | solution.py:15
  28.7 25.5 %copy-start.3 = (bf16[4,16384]{1,0:T(4,128)(2,1)S(1)}, bf16[4,16384]{1,0:T(4,128)(2,1)}, u32[]{:S(2)}) copy-start(bf16[4,16384]{1,0:T(4,128)(2,1)} %param.4) | copy-start | bytes 393220
  28.7 25.5 %copy-start.4 = (bf16[4,16384]{1,0:T(4,128)(2,1)S(1)}, bf16[4,16384]{1,0:T(4,128)(2,1)}, u32[]{:S(2)}) copy-start(bf16[4,16384]{1,0:T(4,128)(2,1)} %param.3) | copy-start | bytes 393220
  28.7 5.8 %collective-permute-start.7 = (bf16[2,4,2,8,512]{4,3,2,1,0:T(8,128)(2,1)S(1)}, bf16[2,4,2,8,512]{4,3,2,1,0:T(8,128)(2,1)S(1)}, u32[]{:S(2)}, u32[]{:S(2)}) collective-permute-start(bf16[2,4,2,8,512]{4,3,2,1,0:T(8,128)(2,1)S(1)} %bitcast.177), channel_id=1, source_target_pairs={{0,3},{1,0},{2,1},{3,2},{4,7},{5,4},{6,5},{7,6},{8,11},{9,8},{10,9... | collective-permute-start | bytes 393224 | tf_op jit(solution)/shard_map/ppermute | solution.py:15
  31.8 6.7 %collective-permute-start.6 = (bf16[2,4,2,8,512]{4,3,2,1,0:T(8,128)(2,1)S(1)}, bf16[2,4,2,8,512]{4,3,2,1,0:T(8,128)(2,1)S(1)}, u32[]{:S(2)}, u32[]{:S(2)}) collective-permute-start(bf16[2,4,2,8,512]{4,3,2,1,0:T(8,128)(2,1)S(1)} %bitcast.178), channel_id=1, source_target_pairs={{0,2},{1,3},{2,0},{3,1},{4,6},{5,7},{6,4},{7,5},{8,10},{9,11},{10,... | collective-permute-start | bytes 393224 | tf_op jit(solution)/shard_map/ppermute | solution.py:15
  32.6 7.2 %collective-permute-start.5 = (bf16[2,4,2,8,512]{4,3,2,1,0:T(8,128)(2,1)S(1)}, bf16[2,4,2,8,512]{4,3,2,1,0:T(8,128)(2,1)S(1)}, u32[]{:S(2)}, u32[]{:S(2)}) collective-permute-start(bf16[2,4,2,8,512]{4,3,2,1,0:T(8,128)(2,1)S(1)} %bitcast.179), channel_id=1, source_target_pairs={{0,1},{1,2},{2,3},{3,0},{4,5},{5,6},{6,7},{7,4},{8,9},{9,10},{10,1... | collective-permute-start | bytes 393224 | tf_op jit(solution)/shard_map/ppermute | solution.py:15
  39.9 12.1 %collective-permute-start.27 = (bf16[4,2,4,2,8,512]{5,4,3,2,1,0:T(8,128)(2,1)S(1)}, bf16[4,2,4,2,8,512]{5,4,3,2,1,0:T(8,128)(2,1)S(1)}, u32[]{:S(2)}, u32[]{:S(2)}) collective-permute-start(bf16[4,2,4,2,8,512]{5,4,3,2,1,0:T(8,128)(2,1)S(1)} %get-tuple-element.11), channel_id=1, source_target_pairs={{0,96},{32,0},{64,32},{96,64},{1,97},{33,1},{65,33},{97,65},{2,98}... | collective-permute-start | bytes 1572872 | tf_op jit(solution)/shard_map/ppermute | solution.py:15
  40.5 11.8 %collective-permute-start.25 = (bf16[4,2,4,2,8,512]{5,4,3,2,1,0:T(8,128)(2,1)S(1)}, bf16[4,2,4,2,8,512]{5,4,3,2,1,0:T(8,128)(2,1)S(1)}, u32[]{:S(2)}, u32[]{:S(2)}) collective-permute-start(bf16[4,2,4,2,8,512]{5,4,3,2,1,0:T(8,128)(2,1)S(1)} %get-tuple-element.11), channel_id=1, source_target_pairs={{0,32},{32,64},{64,96},{96,0},{1,33},{33,65},{65,97},{97,1},{2,34}... | collective-permute-start | bytes 1572872 | tf_op jit(solution)/shard_map/ppermute | solution.py:15
  52.0 6.4 %collective-permute-start.28 = (bf16[2,2,4,2,8,512]{5,4,3,2,1,0:T(8,128)(2,1)S(1)}, bf16[2,2,4,2,8,512]{5,4,3,2,1,0:T(8,128)(2,1)S(1)}, u32[]{:S(2)}, u32[]{:S(2)}) collective-permute-start(bf16[2,2,4,2,8,512]{5,4,3,2,1,0:T(8,128)(2,1)S(1)} %slice.62), channel_id=1, source_target_pairs={{0,96},{32,0},{64,32},{96,64},{1,97},{33,1},{65,33},{97,65},{2,98}... | collective-permute-start | bytes 786440 | tf_op jit(solution)/shard_map/ppermute | solution.py:15
  52.3 7.6 %collective-permute-start.26 = (bf16[2,2,4,2,8,512]{5,4,3,2,1,0:T(8,128)(2,1)S(1)}, bf16[2,2,4,2,8,512]{5,4,3,2,1,0:T(8,128)(2,1)}, u32[]{:S(2)}, u32[]{:S(2)}) collective-permute-start(bf16[2,2,4,2,8,512]{5,4,3,2,1,0:T(8,128)(2,1)S(1)} %slice.61), channel_id=1, source_target_pairs={{0,32},{32,64},{64,96},{96,0},{1,33},{33,65},{65,97},{97,1},{2,34}... | collective-permute-start | bytes 786440 | tf_op jit(solution)/shard_map/ppermute | solution.py:15
  61.5 90.5 %copy-start = (bf16[4,4,2,2,4,8,512]{6,5,4,3,2,1,0:T(8,128)(2,1)}, bf16[4,4,2,2,4,8,512]{6,5,4,3,2,1,0:T(8,128)(2,1)S(1)}, u32[]{:S(2)}) copy-start(bf16[4,4,2,2,4,8,512]{6,5,4,3,2,1,0:T(8,128)(2,1)S(1)} %copy.37) | copy-start | bytes 6291460
  61.5 69.4 %collective-permute-start.29 = (bf16[4,4,128,512]{3,2,1,0:T(8,128)(2,1)S(1)}, bf16[4,4,128,512]{3,2,1,0:T(8,128)(2,1)}, u32[]{:S(2)}, u32[]{:S(2)}) collective-permute-start(bf16[4,4,128,512]{3,2,1,0:T(8,128)(2,1)S(1)} %bitcast.150), channel_id=1, source_target_pairs={{0,16},{16,0},{1,17},{17,1},{2,18},{18,2},{3,19},{19,3},{4,20},{20... | collective-permute-start | bytes 6291464 | tf_op jit(solution)/shard_map/ppermute | solution.py:15
  61.6 5.8 %collective-permute-start.10 = (bf16[2,2,8,1024]{3,2,0,1:T(8,128)(2,1)S(1)}, bf16[2,2,8,1024]{3,2,0,1:T(8,128)(2,1)S(1)}, u32[]{:S(2)}, u32[]{:S(2)}) collective-permute-start(bf16[2,2,8,1024]{3,2,0,1:T(8,128)(2,1)S(1)} %get-tuple-element.21), channel_id=1, source_target_pairs={{0,96},{32,0},{64,32},{96,64},{1,97},{33,1},{65,33},{97,65},{2,98}... | collective-permute-start | bytes 196616 | tf_op jit(solution)/shard_map/ppermute | solution.py:15
  64.9 5.8 %collective-permute-start.9 = (bf16[2,2,8,1024]{3,2,0,1:T(8,128)(2,1)S(1)}, bf16[2,2,8,1024]{3,2,0,1:T(8,128)(2,1)S(1)}, u32[]{:S(2)}, u32[]{:S(2)}) collective-permute-start(bf16[2,2,8,1024]{3,2,0,1:T(8,128)(2,1)S(1)} %get-tuple-element.22), channel_id=1, source_target_pairs={{0,64},{32,96},{64,0},{96,32},{1,65},{33,97},{65,1},{97,33},{2,66}... | collective-permute-start | bytes 196616 | tf_op jit(solution)/shard_map/ppermute | solution.py:15
  65.0 5.8 %collective-permute-start.8 = (bf16[2,2,8,1024]{3,2,0,1:T(8,128)(2,1)S(1)}, bf16[2,2,8,1024]{3,2,0,1:T(8,128)(2,1)S(1)}, u32[]{:S(2)}, u32[]{:S(2)}) collective-permute-start(bf16[2,2,8,1024]{3,2,0,1:T(8,128)(2,1)S(1)} %get-tuple-element.23), channel_id=1, source_target_pairs={{0,32},{32,64},{64,96},{96,0},{1,33},{33,65},{65,97},{97,1},{2,34}... | collective-permute-start | bytes 196616 | tf_op jit(solution)/shard_map/ppermute | solution.py:15
  70.8 11.4 %collective-permute-start.11 = (bf16[4,2,8,1024]{3,2,0,1:T(8,128)(2,1)S(1)}, bf16[4,2,8,1024]{3,2,0,1:T(8,128)(2,1)S(1)}, u32[]{:S(2)}, u32[]{:S(2)}) collective-permute-start(bf16[4,2,8,1024]{3,2,0,1:T(8,128)(2,1)S(1)} %get-tuple-element.31), channel_id=1, source_target_pairs={{0,128},{128,0},{1,129},{129,1},{2,130},{130,2},{3,131},{131,3},{4... | collective-permute-start | bytes 393224 | tf_op jit(solution)/shard_map/ppermute | solution.py:15
  82.2 11.8 %collective-permute-start.14 = (bf16[128,768]{1,0:T(8,128)(2,1)S(1)}, bf16[128,768]{1,0:T(8,128)(2,1)S(1)}, u32[]{:S(2)}, u32[]{:S(2)}) collective-permute-start(bf16[128,768]{1,0:T(8,128)(2,1)S(1)} %get-tuple-element.29), channel_id=1, source_target_pairs={{0,12},{4,0},{8,4},{12,8},{1,13},{5,1},{9,5},{13,9},{2,14},{6,2},{... | collective-permute-start | bytes 589832 | tf_op jit(solution)/shard_map/ppermute | solution.py:15
  82.4 23.2 %collective-permute-start.13 = (bf16[128,768]{1,0:T(8,128)(2,1)S(1)}, bf16[128,768]{1,0:T(8,128)(2,1)S(1)}, u32[]{:S(2)}, u32[]{:S(2)}) collective-permute-start(bf16[128,768]{1,0:T(8,128)(2,1)S(1)} %get-tuple-element.29), channel_id=1, source_target_pairs={{0,8},{4,12},{8,0},{12,4},{1,9},{5,13},{9,1},{13,5},{2,10},{6,14},... | collective-permute-start | bytes 589832 | tf_op jit(solution)/shard_map/ppermute | solution.py:15
  92.1 13.4 %collective-permute-start.12 = (bf16[128,768]{1,0:T(8,128)(2,1)S(1)}, bf16[128,768]{1,0:T(8,128)(2,1)S(1)}, u32[]{:S(2)}, u32[]{:S(2)}) collective-permute-start(bf16[128,768]{1,0:T(8,128)(2,1)S(1)} %get-tuple-element.29), channel_id=1, source_target_pairs={{0,4},{4,8},{8,12},{12,0},{1,5},{5,9},{9,13},{13,1},{2,6},{6,10},{... | collective-permute-start | bytes 589832 | tf_op jit(solution)/shard_map/ppermute | solution.py:15
  105.7 15.6 %collective-permute-start.15 = (bf16[4,128,768]{2,1,0:T(8,128)(2,1)S(1)}, bf16[4,128,768]{2,1,0:T(8,128)(2,1)S(1)}, u32[]{:S(2)}, u32[]{:S(2)}) collective-permute-start(bf16[4,128,768]{2,1,0:T(8,128)(2,1)S(1)} %pad_maximum_fusion.a0), channel_id=1, source_target_pairs={{0,1},{1,2},{2,3},{3,0},{4,5},{5,6},{6,7},{7,4},{8,9},{9,10},{10,1... | collective-permute-start | bytes 2359304 | tf_op jit(solution)/shard_map/ppermute | solution.py:15
  105.8 17.6 %collective-permute-start.17 = (bf16[4,128,768]{2,1,0:T(8,128)(2,1)S(1)}, bf16[4,128,768]{2,1,0:T(8,128)(2,1)}, u32[]{:S(2)}, u32[]{:S(2)}) collective-permute-start(bf16[4,128,768]{2,1,0:T(8,128)(2,1)S(1)} %pad_maximum_fusion.a0), channel_id=1, source_target_pairs={{0,3},{1,0},{2,1},{3,2},{4,7},{5,4},{6,5},{7,6},{8,11},{9,8},{10,9... | collective-permute-start | bytes 2359304 | tf_op jit(solution)/shard_map/ppermute | solution.py:15
  109.0 17.9 %collective-permute-start.21 = (bf16[128,256]{1,0:T(8,128)(2,1)S(1)}, bf16[128,256]{1,0:T(8,128)(2,1)}, u32[]{:S(2)}, u32[]{:S(2)}) collective-permute-start(bf16[128,256]{1,0:T(8,128)(2,1)S(1)} %get-tuple-element.27), channel_id=1, source_target_pairs={{0,3},{1,0},{2,1},{3,2},{4,7},{5,4},{6,5},{7,6},{8,11},{9,8},{10,9... | collective-permute-start | bytes 196616 | tf_op jit(solution)/shard_map/ppermute | solution.py:15
  109.1 18.7 %collective-permute-start.20 = (bf16[128,256]{1,0:T(8,128)(2,1)S(1)}, bf16[128,256]{1,0:T(8,128)(2,1)}, u32[]{:S(2)}, u32[]{:S(2)}) collective-permute-start(bf16[128,256]{1,0:T(8,128)(2,1)S(1)} %get-tuple-element.27), channel_id=1, source_target_pairs={{0,2},{1,3},{2,0},{3,1},{4,6},{5,7},{6,4},{7,5},{8,10},{9,11},{10,... | collective-permute-start | bytes 196616 | tf_op jit(solution)/shard_map/ppermute | solution.py:15
  121.3 0.9 copy-start.1
  122.2 5.8 %collective-permute-start.19 = (bf16[128,256]{1,0:T(8,128)(2,1)S(1)}, bf16[128,256]{1,0:T(8,128)(2,1)}, u32[]{:S(2)}, u32[]{:S(2)}) collective-permute-start(bf16[128,256]{1,0:T(8,128)(2,1)S(1)} %get-tuple-element.27), channel_id=1, source_target_pairs={{0,1},{1,2},{2,3},{3,0},{4,5},{5,6},{6,7},{7,4},{8,9},{9,10},{10,1... | collective-permute-start | bytes 196616 | tf_op jit(solution)/shard_map/ppermute | solution.py:15
  123.4 22.0 %collective-permute-start.16 = (bf16[2,128,768]{2,1,0:T(8,128)(2,1)S(1)}, bf16[2,128,768]{2,1,0:T(8,128)(2,1)S(1)}, u32[]{:S(2)}, u32[]{:S(2)}) collective-permute-start(bf16[2,128,768]{2,1,0:T(8,128)(2,1)S(1)} %slice.58), channel_id=1, source_target_pairs={{0,1},{1,2},{2,3},{3,0},{4,5},{5,6},{6,7},{7,4},{8,9},{9,10},{10,1... | collective-permute-start | bytes 1179656 | tf_op jit(solution)/shard_map/ppermute | solution.py:15
  126.9 18.5 %collective-permute-start.18 = (bf16[2,128,768]{2,1,0:T(8,128)(2,1)S(1)}, bf16[2,128,768]{2,1,0:T(8,128)(2,1)S(1)}, u32[]{:S(2)}, u32[]{:S(2)}) collective-permute-start(bf16[2,128,768]{2,1,0:T(8,128)(2,1)S(1)} %slice.59), channel_id=1, source_target_pairs={{0,3},{1,0},{2,1},{3,2},{4,7},{5,4},{6,5},{7,6},{8,11},{9,8},{10,9... | collective-permute-start | bytes 1179656 | tf_op jit(solution)/shard_map/ppermute | solution.py:15
  128.9 9.5 %copy-start.2 = (bf16[4,128,768]{2,1,0:T(8,128)(2,1)S(1)}, bf16[4,128,768]{2,1,0:T(8,128)(2,1)}, u32[]{:S(2)}) copy-start(bf16[4,128,768]{2,1,0:T(8,128)(2,1)} %copy-done.1) | copy-start | bytes 2359300
  129.0 12.7 %collective-permute-start.22 = (bf16[4,128,256]{2,1,0:T(8,128)(2,1)S(1)}, bf16[4,128,256]{2,1,0:T(8,128)(2,1)S(1)}, u32[]{:S(2)}, u32[]{:S(2)}) collective-permute-start(bf16[4,128,256]{2,1,0:T(8,128)(2,1)S(1)} %pad_maximum_fusion.6.e0), channel_id=1, source_target_pairs={{0,4},{4,8},{8,12},{12,0},{1,5},{5,9},{9,13},{13,1},{2,6},{6,10},{... | collective-permute-start | bytes 786440 | tf_op jit(solution)/shard_map/ppermute | solution.py:15
  129.6 15.7 %collective-permute-start.23 = (bf16[4,128,256]{2,1,0:T(8,128)(2,1)S(1)}, bf16[4,128,256]{2,1,0:T(8,128)(2,1)S(1)}, u32[]{:S(2)}, u32[]{:S(2)}) collective-permute-start(bf16[4,128,256]{2,1,0:T(8,128)(2,1)S(1)} %pad_maximum_fusion.6.e0), channel_id=1, source_target_pairs={{0,8},{4,12},{8,0},{12,4},{1,9},{5,13},{9,1},{13,5},{2,10},{6,14},... | collective-permute-start | bytes 786440 | tf_op jit(solution)/shard_map/ppermute | solution.py:15
  130.9 14.5 %collective-permute-start.24 = (bf16[4,128,256]{2,1,0:T(8,128)(2,1)S(1)}, bf16[4,128,256]{2,1,0:T(8,128)(2,1)S(1)}, u32[]{:S(2)}, u32[]{:S(2)}) collective-permute-start(bf16[4,128,256]{2,1,0:T(8,128)(2,1)S(1)} %pad_maximum_fusion.6.e0), channel_id=1, source_target_pairs={{0,12},{4,0},{8,4},{12,8},{1,13},{5,1},{9,5},{13,9},{2,14},{6,2},{... | collective-permute-start | bytes 786440 | tf_op jit(solution)/shard_map/ppermute | solution.py:15
  151.9 9.1 %collective-permute-start.30 = (f32[4,4,64,512]{3,2,1,0:T(8,128)}, f32[4,4,64,512]{3,2,1,0:T(8,128)S(1)}, u32[]{:S(2)}, u32[]{:S(2)}) collective-permute-start(f32[4,4,64,512]{3,2,1,0:T(8,128)} %shard_map.40), channel_id=1, source_target_pairs={{0,16},{16,0},{1,17},{17,1},{2,18},{18,2},{3,19},{19,3},{4,20},{20... | collective-permute-start | bytes 6291464 | tf_op jit(solution)/shard_map/ppermute | solution.py:15
  163.2 16.5 %collective-permute-start.33 = (bf16[16,2,8,512]{3,2,0,1:T(8,128)(2,1)S(1)}, bf16[16,2,8,512]{3,2,0,1:T(8,128)(2,1)S(1)}, u32[]{:S(2)}, u32[]{:S(2)}) collective-permute-start(bf16[16,2,8,512]{3,2,0,1:T(8,128)(2,1)S(1)} %get-tuple-element.8), channel_id=1, source_target_pairs={{0,96},{32,0},{64,32},{96,64},{1,97},{33,1},{65,33},{97,65},{2,98}... | collective-permute-start | bytes 786440 | tf_op jit(solution)/shard_map/ppermute | solution.py:15
  173.0 11.8 %collective-permute-start.32 = (bf16[16,2,8,512]{3,2,0,1:T(8,128)(2,1)S(1)}, bf16[16,2,8,512]{3,2,0,1:T(8,128)(2,1)S(1)}, u32[]{:S(2)}, u32[]{:S(2)}) collective-permute-start(bf16[16,2,8,512]{3,2,0,1:T(8,128)(2,1)S(1)} %get-tuple-element.9), channel_id=1, source_target_pairs={{0,64},{32,96},{64,0},{96,32},{1,65},{33,97},{65,1},{97,33},{2,66}... | collective-permute-start | bytes 786440 | tf_op jit(solution)/shard_map/ppermute | solution.py:15
  173.0 12.7 %collective-permute-start.31 = (bf16[16,2,8,512]{3,2,0,1:T(8,128)(2,1)S(1)}, bf16[16,2,8,512]{3,2,0,1:T(8,128)(2,1)S(1)}, u32[]{:S(2)}, u32[]{:S(2)}) collective-permute-start(bf16[16,2,8,512]{3,2,0,1:T(8,128)(2,1)S(1)} %get-tuple-element.7), channel_id=1, source_target_pairs={{0,32},{32,64},{64,96},{96,0},{1,33},{33,65},{65,97},{97,1},{2,34}... | collective-permute-start | bytes 786440 | tf_op jit(solution)/shard_map/ppermute | solution.py:15
  185.9 10.7 %collective-permute-start.34 = (bf16[16,8,512]{2,1,0:T(8,128)(2,1)S(1)}, bf16[16,8,512]{2,1,0:T(8,128)(2,1)S(1)}, u32[]{:S(2)}, u32[]{:S(2)}) collective-permute-start(bf16[16,8,512]{2,1,0:T(8,128)(2,1)S(1)} %fusion.7), channel_id=1, source_target_pairs={{0,128},{128,0},{1,129},{129,1},{2,130},{130,2},{3,131},{131,3},{4... | collective-permute-start | bytes 393224 | tf_op jit(solution)/shard_map/ppermute | solution.py:15
  197.5 19.6 %all-to-all-start = ((bf16[16,8,512]{2,1,0:T(8,128)(2,1)}), bf16[16,8,512]{2,1,0:T(8,128)(2,1)S(1)}, u32[]{:S(2)}, u32[]{:S(2)}) async-start(bf16[16,8,512]{2,1,0:T(8,128)(2,1)} %bitcast.79), calls=%async_computation | async-start | bytes 262144 | tf_op jit(solution)/shard_map/all_to_all | solution.py:135
  217.2 1.3 collective-permute-start.35
where the time goes:
time: 224 us; the launch traced here: 219 us
  waiting for transfers between devices  95.2 us (42%)
  starting transfers between devices  86.8 us (39%)
  Pallas kernels  18.9 us (8%)
  local copies, waits for them, and re-layouts  9.98 us (4%)
  other arithmetic  8.14 us (4%)
    ppermute x36, waiting for transfers between devices, shift(): return lax.ppermute(value, axis, [(i, (i + step) % n) for i in range(n)])  86.3 us
    ppermute x36, starting transfers between devices, shift(): return lax.ppermute(value, axis, [(i, (i + step) % n) for i in range(n)])  76.1 us
    pallas_call x4, Pallas kernels, call(): pl.pallas_call(kernel, out_shape=jax.ShapeDtypeStruct(shape, F32), in_spe...  18.9 us
    all_to_all x1, starting transfers between devices, body(): lax.all_to_all(back.transpose(1, 0, 2, 3).reshape(16, rows, hw), ('zl', '...  10.6 us
    all_to_all x1, waiting for transfers between devices, body(): lax.all_to_all(back.transpose(1, 0, 2, 3).reshape(16, rows, hw), ('zl', '...  8.93 us
    dynamic_slice x1, local copies, waits for them, and re-layouts, share(): kept = lax.dynamic_slice_in_dim(stored, which * hw, hw, 1)  4.71 us
  transfers between devices with their start and end apart: 37, of which 23 were waited for; matrix products, arithmetic and copies ran while one was open for 4% of the time, Pallas kernels for 6%

commit v1 on v0

--- a/solution.py
+++ b/solution.py
@@ -48,38 +48,46 @@
     out[...] = total
 
 
-def share_kernel(a0, a1, a2, a2b, a3, e0, e1, e2, e3, cols, early, kept, out):
-    wa = early.shape[0]
+def share_kernel(which, a0, a1, a2, a2b, a3, e0, e1, e2, e3, cols, early, stored, out, kept, tile, sem):
+    wa, hw = early.shape
     rows = a0.shape[1] // 2
+    edges = (e0, e1, e2, e3)
+    start = pl.multiple_of(which[0] * hw, hw)
+    load = pltpu.make_async_copy(stored.at[:, pl.ds(start, hw)], kept, sem)
+    load.start()
+    side = None
+    for d, e in enumerate(edges):
+        term = dot(flat(e[...]), flat(cols[:, d]), ((0,), (0,)))
+        side = term if side is None else side + term
     main = early[...]
     main += dot(flat(a2[...]), flat(cols[2, :2]), ((0,), (0,)))
     main += dot(flat(a2b[...]), flat(cols[2, 2:]), ((0,), (0,)))
-    main = (0.5 * main + kept[:wa]).astype(BF16)
-    side = None
-    for d, e in enumerate((e0, e1, e2, e3)):
-        term = dot(flat(e[...]), flat(cols[:, d]), ((0,), (0,)))
-        side = term if side is None else side + term
-    side = (0.5 * side + kept[wa:]).astype(BF16)
+    load.wait()
+    tile[:wa] = (0.5 * main + kept[:wa]).astype(BF16)
+    tile[wa:] = (0.5 * side + kept[wa:]).astype(BF16)
     for a, j, lo in ((a0, 0, 0), (a1, 1, 0), (a2, 2, 0), (a2b, 2, 2), (a3, 3, 0)):
         n = a.shape[0]
-        upper = dot(flat(a[:, :rows]), main, ((1,), (0,)))
-        for z in range(n):
-            e = (e0, e1, e2, e3)[lo + z]
-            out[j, lo + z] = upper[z * rows : (z + 1) * rows] + dot(e[j, :rows], side, ((1,), (0,)))
+        wide = flat(a[:, :rows])
+        thin = jnp.concatenate([edges[lo + z][j, :rows] for z in range(n)])
+        value = dot(jnp.concatenate([wide, thin], 1), tile[...], ((1,), (0,)))
+        out[j, lo : lo + n] = value.reshape(n, rows, hw)
 
 
 def flat(value):
     return value.reshape(-1, value.shape[-1])
 
 
-def call(kernel, shape, flops, *args):
-    spec = pl.BlockSpec(memory_space=pltpu.VMEM)
+VMEM_SPEC = pl.BlockSpec(memory_space=pltpu.VMEM)
+
+
+def call(kernel, shape, flops, args, specs, scratch=()):
     size = sum(a.size * a.dtype.itemsize for a in args)
     return pl.pallas_call(
         kernel,
         out_shape=jax.ShapeDtypeStruct(shape, F32),
-        in_specs=[spec] * len(args),
-        out_specs=spec,
+        in_specs=specs,
+        out_specs=VMEM_SPEC,
+        scratch_shapes=scratch,
         compiler_params=pltpu.CompilerParams(vmem_limit_bytes=48 << 20),
         cost_estimate=pl.CostEstimate(flops=flops, bytes_accessed=size, transcendentals=0),
     )(*args)
@@ -91,9 +99,8 @@
     wa = 3 * w // 4
     core, zl, y = (lax.axis_index(a) for a in ("core", "zl", "y"))
 
-    own = jnp.stack([orbitals, gradient])
-    sibling = shift(own, "core", 1)
-    both = jnp.where(core == 0, jnp.concatenate([own, sibling], 1), jnp.concatenate([sibling, own], 1))
+    near, far = (orbitals, gradient), [shift(v, "core", 1) for v in (orbitals, gradient)]
+    both = jnp.stack([jnp.where(core == 0, jnp.concatenate([p, q]), jnp.concatenate([q, p])) for p, q in zip(near, far)])
 
     to_r = pick(both.reshape(2, rows, 2, 4, 2, w), core, 4).transpose(3, 2, 0, 1, 4)
     to_c = pick(both[::-1].reshape(2, rows, 4, 4, 2, hw), core, 4).transpose(2, 3, 0, 1, 4)
@@ -101,8 +108,9 @@
     part_r = exchange(to_r, "x", 0)
     part_r = exchange(part_r, "zh", 1).transpose(2, 0, 1, 3, 4).reshape(16 * rows, w)
     part_c = exchange(to_c, "zl", 0)
-    part_c = jnp.stack(gather(part_c, "zh"))
-    part_c = exchange(part_c, "y", 2)
+    part_c = exchange(part_c, "y", 1)
+    mine = part_c[:, :, 0].reshape(16, rows, hw).astype(F32)
+    part_c = jnp.stack(gather(part_c, "zh"), 1)
 
     near = jnp.stack(gather(part_r[:, :wa], "zl"))
     edge = jnp.stack(gather(part_r[:, wa:], "y"))
@@ -115,19 +123,20 @@
     other = shift(panel, "core", 1)
 
     def share(cols, which):
-        kept = lax.dynamic_slice_in_dim(stored, which * hw, hw, 1)
-        early = call(early_kernel, (wa, hw), 2 * 192 * rows * wa * hw, a0, a1, a3, cols)
+        early = call(early_kernel, (wa, hw), 2 * 192 * rows * wa * hw, (a0, a1, a3, cols), [VMEM_SPEC] * 4)
         flops = 2 * 64 * rows * (wa + 4 * (w - wa)) * hw + 2 * 128 * rows * w * hw
-        return call(share_kernel, (4, 4, 8 * rows, hw), flops, a0, a1, a2, a2b, a3, *edges, cols, early, kept)
+        args = (which[None], a0, a1, a2, a2b, a3, *edges, cols, early, stored)
+        specs = [pl.BlockSpec(memory_space=pltpu.SMEM)] + [VMEM_SPEC] * 11 + [pl.BlockSpec(memory_space=pl.ANY)]
+        scratch = (pltpu.VMEM((w, hw), F32), pltpu.VMEM((w, hw), BF16), pltpu.SemaphoreType.DMA)
+        return call(share_kernel, (4, 4, 8 * rows, hw), flops, args, specs, scratch)
 
     away = shift(share(other, 1 - core), "core", 1)
     total = (share(panel, core) + away).reshape(16, 2, 4, rows, hw)
 
     got = [shift(total[:, :, 4 - d].astype(BF16), "x", d) for d in range(1, 4)]
     total = total[:, :, 0] + sum(g.astype(F32) for g in got)
-    total = total[:, 0] + shift(total[:, 1].astype(BF16), "zh", 1).astype(F32)
+    total = total[:, 0] + shift(total[:, 1], "zh", 1)
 
-    mine = part_c[:, 0, :, 0].reshape(16, rows, hw).astype(F32)
     result = (mine - total).astype(BF16).reshape(4, 4, rows, hw)
     back = result[::-1, ::-1]
     back = lax.dynamic_slice_in_dim(jnp.concatenate([back, back], 0), 3 - y, 4, 0)

time: 224 us -> 220 us (0.982); the launches traced: 219 us -> 218 us
  waiting for transfers between devices: 95.2 us -> 111 us
  starting transfers between devices: 86.8 us -> 77.1 us
  local copies, waits for them, and re-layouts: 9.98 us -> 6.35 us
    ppermute x36 -> x37, waiting for transfers between devices: 86.3 us -> 102 us  [shift(): return lax.ppermute(value, axis, [(i, (i + step) % n) for i in range(n)])]
    all_to_all x1, starting transfers between devices: 10.6 us -> 3.51 us  [body(): lax.all_to_all(back.transpose(1, 0, 2, 3).reshape(16, rows, hw), ('zl', '...]
    dynamic_slice x1 -> x0, local copies, waits for them, and re-layouts: 4.71 us -> none  [share(): kept = lax.dynamic_slice_in_dim(stored, which * hw, hw, 1)]
    ppermute x36 -> x37, starting transfers between devices: 76.1 us -> 73.6 us  [shift(): return lax.ppermute(value, axis, [(i, (i + step) % n) for i in range(n)])]
  transfers between devices with their start and end apart: 37 -> 38, of which waited for: 23 -> 20; matrix products, arithmetic and copies ran while one was open for 4% -> 2% of each run, Pallas kernels for 6% -> 5%
where the time goes in v1:
time: 220 us; the launch traced here: 218 us
  waiting for transfers between devices  111 us (50%)
  starting transfers between devices  77.1 us (35%)
  Pallas kernels  16.9 us (8%)
  local copies, waits for them, and re-layouts  6.35 us (3%)
  other arithmetic  6.09 us (3%)
    ppermute x37, waiting for transfers between devices, shift(): return lax.ppermute(value, axis, [(i, (i + step) % n) for i in range(n)])  102 us
    ppermute x37, starting transfers between devices, shift(): return lax.ppermute(value, axis, [(i, (i + step) % n) for i in range(n)])  73.6 us
    pallas_call x4, Pallas kernels, call(): pl.pallas_call(kernel, out_shape=jax.ShapeDtypeStruct(shape, F32), in_spe...  16.9 us
    all_to_all x1, waiting for transfers between devices, body(): lax.all_to_all(back.transpose(1, 0, 2, 3).reshape(16, rows, hw), ('zl', '...  8.99 us
  transfers between devices with their start and end apart: 38, of which 20 were waited for; matrix products, arithmetic and copies ran while one was open for 2% of the time, Pallas kernels for 5%

profile of v1, /device:TPU:2, one launch (start us, length us, event | category | flops | bytes accessed | tf_op | source)
XLA Modules:
  0.0 217.7 jit_solution(5168727737958125976)
XLA Ops:
  0.0 0.5 collective-permute-start
  0.5 1.0 collective-permute-done.1
  1.6 1.2 maximum_select_fusion.1
  2.8 1.2 maximum_select_fusion
  4.2 4.7 %collective-permute-start.4 = (bf16[4,2,8,512]{3,2,0,1:T(8,128)(2,1)S(1)}, bf16[4,2,8,512]{3,2,0,1:T(8,128)(2,1)S(1)}, u32[]{:S(2)}, u32[]{:S(2)}) collective-permute-start(bf16[4,2,8,512]{3,2,0,1:T(8,128)(2,1)S(1)} %get-tuple-element.11), channel_id=1, source_target_pairs={{0,12},{4,0},{8,4},{12,8},{1,13},{5,1},{9,5},{13,9},{2,14},{6,2},{... | collective-permute-start | bytes 196616 | tf_op jit(solution)/shard_map/ppermute | solution.py:15
  8.9 0.7 collective-permute-start.2
  9.6 1.9 collective-permute-done.4
  11.4 4.1 %collective-permute-done.3 = bf16[4,2,8,512]{3,2,0,1:T(8,128)(2,1)S(1)} collective-permute-done((bf16[4,2,8,512]{3,2,0,1:T(8,128)(2,1)S(1)}, bf16[4,2,8,512]{3,2,0,1:T(8,128)(2,1)S(1)}, u32[]{:S(2)}, u32[]{:S(2)}) %collective-permute-start.3) | collective-permute-done | bytes 65568 | tf_op jit(solution)/shard_map/ppermute | solution.py:15
  15.6 1.7 collective-permute-start.5
  17.3 2.9 %collective-permute-start.6 = (bf16[4,2,8,512]{3,2,1,0:T(8,128)(2,1)S(1)}, bf16[4,2,8,512]{3,2,1,0:T(8,128)(2,1)S(1)}, u32[]{:S(2)}, u32[]{:S(2)}) collective-permute-start(bf16[4,2,8,512]{3,2,1,0:T(8,128)(2,1)S(1)} %bitcast.185), channel_id=1, source_target_pairs={{0,2},{1,3},{2,0},{3,1},{4,6},{5,7},{6,4},{7,5},{8,10},{9,11},{10,... | collective-permute-start | bytes 196616 | tf_op jit(solution)/shard_map/ppermute | solution.py:15
  20.2 1.3 collective-permute-start.7
  21.6 1.7 collective-permute-done.6
  23.2 1.2 collective-permute-done.7
  24.5 5.3 %collective-permute-start.25 = (bf16[4,4,2,8,512]{4,3,2,1,0:T(8,128)(2,1)S(1)}, bf16[4,4,2,8,512]{4,3,2,1,0:T(8,128)(2,1)S(1)}, u32[]{:S(2)}, u32[]{:S(2)}) collective-permute-start(bf16[4,4,2,8,512]{4,3,2,1,0:T(8,128)(2,1)S(1)} %get-tuple-element.19), channel_id=1, source_target_pairs={{0,128},{128,0},{1,129},{129,1},{2,130},{130,2},{3,131},{131,3},{4... | collective-permute-start | bytes 786440 | tf_op jit(solution)/shard_map/ppermute | solution.py:15
  29.8 6.4 %collective-permute-done.25 = bf16[4,4,2,8,512]{4,3,2,1,0:T(8,128)(2,1)S(1)} collective-permute-done((bf16[4,4,2,8,512]{4,3,2,1,0:T(8,128)(2,1)S(1)}, bf16[4,4,2,8,512]{4,3,2,1,0:T(8,128)(2,1)S(1)}, u32[]{:S(2)}, u32[]{:S(2)}) %collective-permute-start.25) | collective-permute-done | bytes 262176 | tf_op jit(solution)/shard_map/ppermute | solution.py:15
  36.3 1.6 collective-permute-start.26
  37.9 0.5 collective-permute-start.28
  38.4 10.0 %collective-permute-done.26 = bf16[4,2,4,2,8,512]{5,4,3,2,0,1:T(8,128)(2,1)S(1)} collective-permute-done((bf16[4,2,4,2,8,512]{5,4,3,2,0,1:T(8,128)(2,1)S(1)}, bf16[4,2,4,2,8,512]{5,4,3,2,0,1:T(8,128)(2,1)S(1)}, u32[]{:S(2)}, u32[]{:S(2)}) %collective-permute-start.26) | collective-permute-done | bytes 524320 | tf_op jit(solution)/shard_map/ppermute | solution.py:15
  48.4 1.6 collective-permute-start.27
  50.0 0.6 collective-permute-start.29
  51.1 3.8 %collective-permute-done.27 = bf16[2,2,4,2,8,512]{5,4,3,2,0,1:T(8,128)(2,1)S(1)} collective-permute-done((bf16[2,2,4,2,8,512]{5,4,3,2,0,1:T(8,128)(2,1)S(1)}, bf16[2,2,4,2,8,512]{5,4,3,2,0,1:T(8,128)(2,1)S(1)}, u32[]{:S(2)}, u32[]{:S(2)}) %collective-permute-start.27) | collective-permute-done | bytes 262176 | tf_op jit(solution)/shard_map/ppermute | solution.py:15
  54.8 1.6 collective-permute-done.29
  57.2 0.8 collective-permute-start.10
  58.0 1.5 collective-permute-start.8
  59.5 3.5 %collective-permute-start.9 = (bf16[2,2,8,1024]{3,2,0,1:T(8,128)(2,1)S(1)}, bf16[2,2,8,1024]{3,2,0,1:T(8,128)(2,1)S(1)}, u32[]{:S(2)}, u32[]{:S(2)}) collective-permute-start(bf16[2,2,8,1024]{3,2,0,1:T(8,128)(2,1)S(1)} %get-tuple-element.17), channel_id=1, source_target_pairs={{0,64},{32,96},{64,0},{96,32},{1,65},{33,97},{65,1},{97,33},{2,66}... | collective-permute-start | bytes 196616 | tf_op jit(solution)/shard_map/ppermute | solution.py:15
  63.1 0.5 collective-permute-done.8
  63.6 1.7 collective-permute-done.9
  65.4 5.6 %collective-permute-start.11 = (bf16[4,2,8,1024]{3,2,0,1:T(8,128)(2,1)S(1)}, bf16[4,2,8,1024]{3,2,0,1:T(8,128)(2,1)S(1)}, u32[]{:S(2)}, u32[]{:S(2)}) collective-permute-start(bf16[4,2,8,1024]{3,2,0,1:T(8,128)(2,1)S(1)} %get-tuple-element.29), channel_id=1, source_target_pairs={{0,128},{128,0},{1,129},{129,1},{2,130},{130,2},{3,131},{131,3},{4... | collective-permute-start | bytes 393224 | tf_op jit(solution)/shard_map/ppermute | solution.py:15
  71.0 3.4 %collective-permute-done.11 = bf16[4,2,8,1024]{3,2,0,1:T(8,128)(2,1)S(1)} collective-permute-done((bf16[4,2,8,1024]{3,2,0,1:T(8,128)(2,1)S(1)}, bf16[4,2,8,1024]{3,2,0,1:T(8,128)(2,1)S(1)}, u32[]{:S(2)}, u32[]{:S(2)}) %collective-permute-start.11) | collective-permute-done | bytes 131104 | tf_op jit(solution)/shard_map/ppermute | solution.py:15
  74.4 9.4 %collective-permute-start.13 = (bf16[128,768]{1,0:T(8,128)(2,1)S(1)}, bf16[128,768]{1,0:T(8,128)(2,1)S(1)}, u32[]{:S(2)}, u32[]{:S(2)}) collective-permute-start(bf16[128,768]{1,0:T(8,128)(2,1)S(1)} %get-tuple-element.27), channel_id=1, source_target_pairs={{0,8},{4,12},{8,0},{12,4},{1,9},{5,13},{9,1},{13,5},{2,10},{6,14},... | collective-permute-start | bytes 589832 | tf_op jit(solution)/shard_map/ppermute | solution.py:15
  83.8 3.8 %collective-permute-start.14 = (bf16[128,768]{1,0:T(8,128)(2,1)S(1)}, bf16[128,768]{1,0:T(8,128)(2,1)S(1)}, u32[]{:S(2)}, u32[]{:S(2)}) collective-permute-start(bf16[128,768]{1,0:T(8,128)(2,1)S(1)} %get-tuple-element.27), channel_id=1, source_target_pairs={{0,12},{4,0},{8,4},{12,8},{1,13},{5,1},{9,5},{13,9},{2,14},{6,2},{... | collective-permute-start | bytes 589832 | tf_op jit(solution)/shard_map/ppermute | solution.py:15
  87.6 10.0 %collective-permute-done.13 = bf16[128,768]{1,0:T(8,128)(2,1)S(1)} collective-permute-done((bf16[128,768]{1,0:T(8,128)(2,1)S(1)}, bf16[128,768]{1,0:T(8,128)(2,1)S(1)}, u32[]{:S(2)}, u32[]{:S(2)}) %collective-permute-start.13) | collective-permute-done | bytes 196640 | tf_op jit(solution)/shard_map/ppermute | solution.py:15
  97.7 1.2 collective-permute-start.17
  98.9 0.9 collective-permute-start.15
  99.8 0.7 collective-permute-start.20
  100.5 2.5 %collective-permute-start.19 = (bf16[128,256]{1,0:T(8,128)(2,1)S(1)}, bf16[128,256]{1,0:T(8,128)(2,1)S(1)}, u32[]{:S(2)}, u32[]{:S(2)}) collective-permute-start(bf16[128,256]{1,0:T(8,128)(2,1)S(1)} %get-tuple-element.25), channel_id=1, source_target_pairs={{0,1},{1,2},{2,3},{3,0},{4,5},{5,6},{6,7},{7,4},{8,9},{9,10},{10,1... | collective-permute-start | bytes 196616 | tf_op jit(solution)/shard_map/ppermute | solution.py:15
  103.1 12.4 %collective-permute-done.17.a3 = bf16[4,128,768]{2,1,0:T(8,128)(2,1)S(1)} collective-permute-done((bf16[4,128,768]{2,1,0:T(8,128)(2,1)S(1)}, bf16[4,128,768]{2,1,0:T(8,128)(2,1)S(1)}, u32[]{:S(2)}, u32[]{:S(2)}) %collective-permute-start.17) | collective-permute-done | bytes 786464 | tf_op jit(solution)/shard_map/ppermute | solution.py:15
  115.5 3.7 %collective-permute-start.21 = (bf16[128,256]{1,0:T(8,128)(2,1)S(1)}, bf16[128,256]{1,0:T(8,128)(2,1)S(1)}, u32[]{:S(2)}, u32[]{:S(2)}) collective-permute-start(bf16[128,256]{1,0:T(8,128)(2,1)S(1)} %get-tuple-element.25), channel_id=1, source_target_pairs={{0,3},{1,0},{2,1},{3,2},{4,7},{5,4},{6,5},{7,6},{8,11},{9,8},{10,9... | collective-permute-start | bytes 196616 | tf_op jit(solution)/shard_map/ppermute | solution.py:15
  119.1 0.8 slice.58
  120.0 0.9 slice.57
  121.0 1.8 collective-permute-start.16
  122.8 1.6 collective-permute-start.24
  124.4 4.7 %collective-permute-start.23 = (bf16[4,128,256]{2,1,0:T(8,128)(2,1)S(1)}, bf16[4,128,256]{2,1,0:T(8,128)(2,1)}, u32[]{:S(2)}, u32[]{:S(2)}) collective-permute-start(bf16[4,128,256]{2,1,0:T(8,128)(2,1)S(1)} %pad_maximum_fusion.7.e0), channel_id=1, source_target_pairs={{0,8},{4,12},{8,0},{12,4},{1,9},{5,13},{9,1},{13,5},{2,10},{6,14},... | collective-permute-start | bytes 786440 | tf_op jit(solution)/shard_map/ppermute | solution.py:15
  129.1 0.4 collective-permute-start.22
  129.5 1.1 copy-done.2
  130.6 1.1 copy-done.4
  131.8 3.0 %shard_map.39.early = f32[768,512]{1,0:T(8,128)S(1)} custom-call(bf16[4,128,768]{2,1,0:T(8,128)(2,1)S(1)} %pad_maximum_fusion.a0, bf16[4,128,768]{2,1,0:T(8,128)(2,1)S(1)} %copy-done.4, bf16[4,128,768]{2,1,0:T(8,128)(2,1)S(1)} %copy-done.2, bf16[4,4,128,512]{3,2,1,0:T(8,128)(2,1)} %collective-permute-done.30.cols), custom_call_target="tpu_custom_call" | custom-call | flops 1207959552 | bytes 4456448 | tf_op jit(solution)/shard_map/pallas_call | solution.py:85
  134.8 15.1 %collective-permute-done.23.e2 = bf16[4,128,256]{2,1,0:T(8,128)(2,1)} collective-permute-done((bf16[4,128,256]{2,1,0:T(8,128)(2,1)S(1)}, bf16[4,128,256]{2,1,0:T(8,128)(2,1)}, u32[]{:S(2)}, u32[]{:S(2)}) %collective-permute-start.23) | collective-permute-done | bytes 262176 | tf_op jit(solution)/shard_map/ppermute | solution.py:15
  149.9 6.2 %shard_map.40 = f32[4,4,64,512]{3,2,1,0:T(8,128)} custom-call(s32[1]{0:T(128)} %bitcast.74.which, bf16[4,128,768]{2,1,0:T(8,128)(2,1)S(1)} %pad_maximum_fusion.a0, bf16[4,128,768]{2,1,0:T(8,128)(2,1)S(1)} %copy-done.4, bf16[2,128,768]{2,1,0:T(8,128)(2,1)} %collective-permute-done.16.a2, bf16[2,128,768]{2,1,0:T(8,128)(2,1)S(1)} %collective-permute-done.18.a2b, ...), custom_call_target="tpu_custom_call" | custom-call | flops 2013265920 | bytes 12058628 | tf_op jit(solution)/shard_map/pallas_call | solution.py:85
  156.2 1.4 shard_map.37.early
  157.6 6.2 %shard_map.38 = f32[4,4,64,512]{3,2,1,0:T(8,128)} custom-call(s32[1]{0:T(128)} %bitcast.30.which, bf16[4,128,768]{2,1,0:T(8,128)(2,1)S(1)} %pad_maximum_fusion.a0, bf16[4,128,768]{2,1,0:T(8,128)(2,1)S(1)} %copy-done.4, bf16[2,128,768]{2,1,0:T(8,128)(2,1)} %collective-permute-done.16.a2, bf16[2,128,768]{2,1,0:T(8,128)(2,1)S(1)} %collective-permute-done.18.a2b, ...), custom_call_target="tpu_custom_call" | custom-call | flops 2013265920 | bytes 12058628 | tf_op jit(solution)/shard_map/pallas_call | solution.py:85
  163.9 2.1 add.241
  166.1 2.3 %collective-permute-start.32 = (bf16[16,2,8,512]{3,2,0,1:T(8,128)(2,1)S(1)}, bf16[16,2,8,512]{3,2,0,1:T(8,128)(2,1)S(1)}, u32[]{:S(2)}, u32[]{:S(2)}) collective-permute-start(bf16[16,2,8,512]{3,2,0,1:T(8,128)(2,1)S(1)} %get-tuple-element.5), channel_id=1, source_target_pairs={{0,32},{32,64},{64,96},{96,0},{1,33},{33,65},{65,97},{97,1},{2,34}... | collective-permute-start | bytes 786440 | tf_op jit(solution)/shard_map/ppermute | solution.py:15
  168.4 2.4 %collective-permute-start.34 = (bf16[16,2,8,512]{3,2,0,1:T(8,128)(2,1)S(1)}, bf16[16,2,8,512]{3,2,0,1:T(8,128)(2,1)S(1)}, u32[]{:S(2)}, u32[]{:S(2)}) collective-permute-start(bf16[16,2,8,512]{3,2,0,1:T(8,128)(2,1)S(1)} %get-tuple-element.6), channel_id=1, source_target_pairs={{0,96},{32,0},{64,32},{96,64},{1,97},{33,1},{65,33},{97,65},{2,98}... | collective-permute-start | bytes 786440 | tf_op jit(solution)/shard_map/ppermute | solution.py:15
  170.8 2.0 collective-permute-start.33
  172.8 5.1 %collective-permute-done.32 = bf16[16,2,8,512]{3,2,0,1:T(8,128)(2,1)S(1)} collective-permute-done((bf16[16,2,8,512]{3,2,0,1:T(8,128)(2,1)S(1)}, bf16[16,2,8,512]{3,2,0,1:T(8,128)(2,1)S(1)}, u32[]{:S(2)}, u32[]{:S(2)}) %collective-permute-start.32) | collective-permute-done | bytes 262176 | tf_op jit(solution)/shard_map/ppermute | solution.py:15
  177.9 7.2 %collective-permute-done.33 = bf16[16,2,8,512]{3,2,0,1:T(8,128)(2,1)S(1)} collective-permute-done((bf16[16,2,8,512]{3,2,0,1:T(8,128)(2,1)S(1)}, bf16[16,2,8,512]{3,2,0,1:T(8,128)(2,1)S(1)}, u32[]{:S(2)}, u32[]{:S(2)}) %collective-permute-start.33) | collective-permute-done | bytes 262176 | tf_op jit(solution)/shard_map/ppermute | solution.py:15
  185.3 3.0 %collective-permute-start.35 = (f32[16,8,512]{2,1,0:T(8,128)S(1)}, f32[16,8,512]{2,1,0:T(8,128)S(1)}, u32[]{:S(2)}, u32[]{:S(2)}) collective-permute-start(f32[16,8,512]{2,1,0:T(8,128)S(1)} %slice_bitcast_fusion.1), channel_id=1, source_target_pairs={{0,128},{128,0},{1,129},{129,1},{2,130},{130,2},{3,131},{131,3},{4... | collective-permute-start | bytes 786440 | tf_op jit(solution)/shard_map/ppermute | solution.py:15
  188.3 13.6 %collective-permute-done.35 = f32[16,8,512]{2,1,0:T(8,128)S(1)} collective-permute-done((f32[16,8,512]{2,1,0:T(8,128)S(1)}, f32[16,8,512]{2,1,0:T(8,128)S(1)}, u32[]{:S(2)}, u32[]{:S(2)}) %collective-permute-start.35) | collective-permute-done | bytes 262176 | tf_op jit(solution)/shard_map/ppermute | solution.py:15
  202.1 0.7 copy.41
  202.8 3.5 %all-to-all-start = ((bf16[16,8,512]{2,1,0:T(8,128)(2,1)}), bf16[16,8,512]{2,1,0:T(8,128)(2,1)S(1)}, u32[]{:S(2)}, u32[]{:S(2)}) async-start(bf16[16,8,512]{2,1,0:T(8,128)(2,1)} %bitcast.84), calls=%async_computation | async-start | bytes 262144 | tf_op jit(solution)/shard_map/all_to_all | solution.py:144
  206.3 9.0 %all-to-all-done = bf16[16,8,512]{2,1,0:T(8,128)(2,1)S(1)} async-done(((bf16[16,8,512]{2,1,0:T(8,128)(2,1)}), bf16[16,8,512]{2,1,0:T(8,128)(2,1)S(1)}, u32[]{:S(2)}, u32[]{:S(2)}) %all-to-all-start) | async-done | bytes 131104 | tf_op jit(solution)/shard_map/all_to_all | solution.py:144
  215.6 1.2 collective-permute-done.36
  216.9 0.7 reshape.302
  (81 shorter events, 2.9 us)
Async XLA Ops:
  0.0 1.6 collective-permute-start.1
  0.0 2.8 %collective-permute-start = (bf16[4,16384]{1,0:T(4,128)(2,1)}, bf16[4,16384]{1,0:T(4,128)(2,1)S(1)}, u32[]{:S(2)}, u32[]{:S(2)}) collective-permute-start(bf16[4,16384]{1,0:T(4,128)(2,1)} %param.3), channel_id=1, source_target_pairs={{0,16},{16,0},{1,17},{17,1},{2,18},{18,2},{3,19},{19,3},{4,20},{20... | collective-permute-start | bytes 393224 | tf_op jit(solution)/shard_map/ppermute | solution.py:15
  4.2 7.2 %collective-permute-start.4 = (bf16[4,2,8,512]{3,2,0,1:T(8,128)(2,1)S(1)}, bf16[4,2,8,512]{3,2,0,1:T(8,128)(2,1)S(1)}, u32[]{:S(2)}, u32[]{:S(2)}) collective-permute-start(bf16[4,2,8,512]{3,2,0,1:T(8,128)(2,1)S(1)} %get-tuple-element.11), channel_id=1, source_target_pairs={{0,12},{4,0},{8,4},{12,8},{1,13},{5,1},{9,5},{13,9},{2,14},{6,2},{... | collective-permute-start | bytes 196616 | tf_op jit(solution)/shard_map/ppermute | solution.py:15
  8.9 6.6 %collective-permute-start.3 = (bf16[4,2,8,512]{3,2,0,1:T(8,128)(2,1)S(1)}, bf16[4,2,8,512]{3,2,0,1:T(8,128)(2,1)S(1)}, u32[]{:S(2)}, u32[]{:S(2)}) collective-permute-start(bf16[4,2,8,512]{3,2,0,1:T(8,128)(2,1)S(1)} %get-tuple-element.12), channel_id=1, source_target_pairs={{0,8},{4,12},{8,0},{12,4},{1,9},{5,13},{9,1},{13,5},{2,10},{6,14},... | collective-permute-start | bytes 196616 | tf_op jit(solution)/shard_map/ppermute | solution.py:15
  8.9 6.6 %collective-permute-start.2 = (bf16[4,2,8,512]{3,2,0,1:T(8,128)(2,1)S(1)}, bf16[4,2,8,512]{3,2,0,1:T(8,128)(2,1)S(1)}, u32[]{:S(2)}, u32[]{:S(2)}) collective-permute-start(bf16[4,2,8,512]{3,2,0,1:T(8,128)(2,1)S(1)} %get-tuple-element.13), channel_id=1, source_target_pairs={{0,4},{4,8},{8,12},{12,0},{1,5},{5,9},{9,13},{13,1},{2,6},{6,10},{... | collective-permute-start | bytes 196616 | tf_op jit(solution)/shard_map/ppermute | solution.py:15
  15.6 35.0 %copy-start.7 = (bf16[4,16384]{1,0:T(4,128)(2,1)S(1)}, bf16[4,16384]{1,0:T(4,128)(2,1)}, u32[]{:S(2)}) copy-start(bf16[4,16384]{1,0:T(4,128)(2,1)} %param.4) | copy-start | bytes 393220
  15.6 5.9 %collective-permute-start.5 = (bf16[4,2,8,512]{3,2,1,0:T(8,128)(2,1)S(1)}, bf16[4,2,8,512]{3,2,1,0:T(8,128)(2,1)S(1)}, u32[]{:S(2)}, u32[]{:S(2)}) collective-permute-start(bf16[4,2,8,512]{3,2,1,0:T(8,128)(2,1)S(1)} %bitcast.186), channel_id=1, source_target_pairs={{0,1},{1,2},{2,3},{3,0},{4,5},{5,6},{6,7},{7,4},{8,9},{9,10},{10,1... | collective-permute-start | bytes 196616 | tf_op jit(solution)/shard_map/ppermute | solution.py:15
  17.3 5.9 %collective-permute-start.6 = (bf16[4,2,8,512]{3,2,1,0:T(8,128)(2,1)S(1)}, bf16[4,2,8,512]{3,2,1,0:T(8,128)(2,1)S(1)}, u32[]{:S(2)}, u32[]{:S(2)}) collective-permute-start(bf16[4,2,8,512]{3,2,1,0:T(8,128)(2,1)S(1)} %bitcast.185), channel_id=1, source_target_pairs={{0,2},{1,3},{2,0},{3,1},{4,6},{5,7},{6,4},{7,5},{8,10},{9,11},{10,... | collective-permute-start | bytes 196616 | tf_op jit(solution)/shard_map/ppermute | solution.py:15
  20.2 4.3 %collective-permute-start.7 = (bf16[4,2,8,512]{3,2,1,0:T(8,128)(2,1)S(1)}, bf16[4,2,8,512]{3,2,1,0:T(8,128)(2,1)S(1)}, u32[]{:S(2)}, u32[]{:S(2)}) collective-permute-start(bf16[4,2,8,512]{3,2,1,0:T(8,128)(2,1)S(1)} %bitcast.184), channel_id=1, source_target_pairs={{0,3},{1,0},{2,1},{3,2},{4,7},{5,4},{6,5},{7,6},{8,11},{9,8},{10,9... | collective-permute-start | bytes 196616 | tf_op jit(solution)/shard_map/ppermute | solution.py:15
  21.5 29.3 %copy-start.8 = (bf16[4,16384]{1,0:T(4,128)(2,1)S(1)}, bf16[4,16384]{1,0:T(4,128)(2,1)}, u32[]{:S(2)}) copy-start(bf16[4,16384]{1,0:T(4,128)(2,1)} %param.3) | copy-start | bytes 393220
  24.5 11.7 %copy-start.5 = (bf16[4,4,2,8,512]{4,3,2,1,0:T(8,128)(2,1)}, bf16[4,4,2,8,512]{4,3,2,1,0:T(8,128)(2,1)S(1)}, u32[]{:S(2)}) copy-start(bf16[4,4,2,8,512]{4,3,2,1,0:T(8,128)(2,1)S(1)} %get-tuple-element.19) | copy-start | bytes 786436
  24.5 11.7 %collective-permute-start.25 = (bf16[4,4,2,8,512]{4,3,2,1,0:T(8,128)(2,1)S(1)}, bf16[4,4,2,8,512]{4,3,2,1,0:T(8,128)(2,1)S(1)}, u32[]{:S(2)}, u32[]{:S(2)}) collective-permute-start(bf16[4,4,2,8,512]{4,3,2,1,0:T(8,128)(2,1)S(1)} %get-tuple-element.19), channel_id=1, source_target_pairs={{0,128},{128,0},{1,129},{129,1},{2,130},{130,2},{3,131},{131,3},{4... | collective-permute-start | bytes 786440 | tf_op jit(solution)/shard_map/ppermute | solution.py:15
  36.3 12.1 %collective-permute-start.26 = (bf16[4,2,4,2,8,512]{5,4,3,2,0,1:T(8,128)(2,1)S(1)}, bf16[4,2,4,2,8,512]{5,4,3,2,0,1:T(8,128)(2,1)S(1)}, u32[]{:S(2)}, u32[]{:S(2)}) collective-permute-start(bf16[4,2,4,2,8,512]{5,4,3,2,0,1:T(8,128)(2,1)S(1)} %get-tuple-element.9), channel_id=1, source_target_pairs={{0,32},{32,64},{64,96},{96,0},{1,33},{33,65},{65,97},{97,1},{2,34}... | collective-permute-start | bytes 1572872 | tf_op jit(solution)/shard_map/ppermute | solution.py:15
  37.9 12.1 %collective-permute-start.28 = (bf16[4,2,4,2,8,512]{5,4,3,2,0,1:T(8,128)(2,1)S(1)}, bf16[4,2,4,2,8,512]{5,4,3,2,0,1:T(8,128)(2,1)S(1)}, u32[]{:S(2)}, u32[]{:S(2)}) collective-permute-start(bf16[4,2,4,2,8,512]{5,4,3,2,0,1:T(8,128)(2,1)S(1)} %get-tuple-element.9), channel_id=1, source_target_pairs={{0,96},{32,0},{64,32},{96,64},{1,97},{33,1},{65,33},{97,65},{2,98}... | collective-permute-start | bytes 1572872 | tf_op jit(solution)/shard_map/ppermute | solution.py:15
  48.4 6.4 %collective-permute-start.27 = (bf16[2,2,4,2,8,512]{5,4,3,2,0,1:T(8,128)(2,1)S(1)}, bf16[2,2,4,2,8,512]{5,4,3,2,0,1:T(8,128)(2,1)S(1)}, u32[]{:S(2)}, u32[]{:S(2)}) collective-permute-start(bf16[2,2,4,2,8,512]{5,4,3,2,0,1:T(8,128)(2,1)S(1)} %slice.60), channel_id=1, source_target_pairs={{0,32},{32,64},{64,96},{96,0},{1,33},{33,65},{65,97},{97,1},{2,34}... | collective-permute-start | bytes 786440 | tf_op jit(solution)/shard_map/ppermute | solution.py:15
  50.0 6.4 %collective-permute-start.29 = (bf16[2,2,4,2,8,512]{5,4,3,2,0,1:T(8,128)(2,1)S(1)}, bf16[2,2,4,2,8,512]{5,4,3,2,0,1:T(8,128)(2,1)S(1)}, u32[]{:S(2)}, u32[]{:S(2)}) collective-permute-start(bf16[2,2,4,2,8,512]{5,4,3,2,0,1:T(8,128)(2,1)S(1)} %slice.61), channel_id=1, source_target_pairs={{0,96},{32,0},{64,32},{96,64},{1,97},{33,1},{65,33},{97,65},{2,98}... | collective-permute-start | bytes 786440 | tf_op jit(solution)/shard_map/ppermute | solution.py:15
  57.1 99.1 %copy-start = (bf16[4,4,2,2,4,8,512]{6,5,4,3,2,1,0:T(8,128)(2,1)}, bf16[4,4,2,2,4,8,512]{6,5,4,3,2,1,0:T(8,128)(2,1)S(1)}, u32[]{:S(2)}) copy-start(bf16[4,4,2,2,4,8,512]{6,5,4,3,2,1,0:T(8,128)(2,1)S(1)} %copy.38) | copy-start | bytes 6291460
  57.1 72.0 %collective-permute-start.30 = (bf16[4,4,128,512]{3,2,1,0:T(8,128)(2,1)S(1)}, bf16[4,4,128,512]{3,2,1,0:T(8,128)(2,1)}, u32[]{:S(2)}, u32[]{:S(2)}) collective-permute-start(bf16[4,4,128,512]{3,2,1,0:T(8,128)(2,1)S(1)} %bitcast.155), channel_id=1, source_target_pairs={{0,16},{16,0},{1,17},{17,1},{2,18},{18,2},{3,19},{19,3},{4,20},{20... | collective-permute-start | bytes 6291464 | tf_op jit(solution)/shard_map/ppermute | solution.py:15
  57.2 5.8 %collective-permute-start.10 = (bf16[2,2,8,1024]{3,2,0,1:T(8,128)(2,1)S(1)}, bf16[2,2,8,1024]{3,2,0,1:T(8,128)(2,1)S(1)}, u32[]{:S(2)}, u32[]{:S(2)}) collective-permute-start(bf16[2,2,8,1024]{3,2,0,1:T(8,128)(2,1)S(1)} %get-tuple-element.15), channel_id=1, source_target_pairs={{0,96},{32,0},{64,32},{96,64},{1,97},{33,1},{65,33},{97,65},{2,98}... | collective-permute-start | bytes 196616 | tf_op jit(solution)/shard_map/ppermute | solution.py:15
  58.0 5.5 %collective-permute-start.8 = (bf16[2,2,8,1024]{3,2,0,1:T(8,128)(2,1)S(1)}, bf16[2,2,8,1024]{3,2,0,1:T(8,128)(2,1)S(1)}, u32[]{:S(2)}, u32[]{:S(2)}) collective-permute-start(bf16[2,2,8,1024]{3,2,0,1:T(8,128)(2,1)S(1)} %get-tuple-element.16), channel_id=1, source_target_pairs={{0,32},{32,64},{64,96},{96,0},{1,33},{33,65},{65,97},{97,1},{2,34}... | collective-permute-start | bytes 196616 | tf_op jit(solution)/shard_map/ppermute | solution.py:15
  59.5 5.8 %collective-permute-start.9 = (bf16[2,2,8,1024]{3,2,0,1:T(8,128)(2,1)S(1)}, bf16[2,2,8,1024]{3,2,0,1:T(8,128)(2,1)S(1)}, u32[]{:S(2)}, u32[]{:S(2)}) collective-permute-start(bf16[2,2,8,1024]{3,2,0,1:T(8,128)(2,1)S(1)} %get-tuple-element.17), channel_id=1, source_target_pairs={{0,64},{32,96},{64,0},{96,32},{1,65},{33,97},{65,1},{97,33},{2,66}... | collective-permute-start | bytes 196616 | tf_op jit(solution)/shard_map/ppermute | solution.py:15
  65.4 9.0 %collective-permute-start.11 = (bf16[4,2,8,1024]{3,2,0,1:T(8,128)(2,1)S(1)}, bf16[4,2,8,1024]{3,2,0,1:T(8,128)(2,1)S(1)}, u32[]{:S(2)}, u32[]{:S(2)}) collective-permute-start(bf16[4,2,8,1024]{3,2,0,1:T(8,128)(2,1)S(1)} %get-tuple-element.29), channel_id=1, source_target_pairs={{0,128},{128,0},{1,129},{129,1},{2,130},{130,2},{3,131},{131,3},{4... | collective-permute-start | bytes 393224 | tf_op jit(solution)/shard_map/ppermute | solution.py:15
  74.4 23.2 %collective-permute-start.13 = (bf16[128,768]{1,0:T(8,128)(2,1)S(1)}, bf16[128,768]{1,0:T(8,128)(2,1)S(1)}, u32[]{:S(2)}, u32[]{:S(2)}) collective-permute-start(bf16[128,768]{1,0:T(8,128)(2,1)S(1)} %get-tuple-element.27), channel_id=1, source_target_pairs={{0,8},{4,12},{8,0},{12,4},{1,9},{5,13},{9,1},{13,5},{2,10},{6,14},... | collective-permute-start | bytes 589832 | tf_op jit(solution)/shard_map/ppermute | solution.py:15
  83.8 13.8 %collective-permute-start.12 = (bf16[128,768]{1,0:T(8,128)(2,1)S(1)}, bf16[128,768]{1,0:T(8,128)(2,1)S(1)}, u32[]{:S(2)}, u32[]{:S(2)}) collective-permute-start(bf16[128,768]{1,0:T(8,128)(2,1)S(1)} %get-tuple-element.27), channel_id=1, source_target_pairs={{0,4},{4,8},{8,12},{12,0},{1,5},{5,9},{9,13},{13,1},{2,6},{6,10},{... | collective-permute-start | bytes 589832 | tf_op jit(solution)/shard_map/ppermute | solution.py:15
  83.8 13.8 %collective-permute-start.14 = (bf16[128,768]{1,0:T(8,128)(2,1)S(1)}, bf16[128,768]{1,0:T(8,128)(2,1)S(1)}, u32[]{:S(2)}, u32[]{:S(2)}) collective-permute-start(bf16[128,768]{1,0:T(8,128)(2,1)S(1)} %get-tuple-element.27), channel_id=1, source_target_pairs={{0,12},{4,0},{8,4},{12,8},{1,13},{5,1},{9,5},{13,9},{2,14},{6,2},{... | collective-permute-start | bytes 589832 | tf_op jit(solution)/shard_map/ppermute | solution.py:15
  97.7 17.8 %collective-permute-start.17 = (bf16[4,128,768]{2,1,0:T(8,128)(2,1)S(1)}, bf16[4,128,768]{2,1,0:T(8,128)(2,1)S(1)}, u32[]{:S(2)}, u32[]{:S(2)}) collective-permute-start(bf16[4,128,768]{2,1,0:T(8,128)(2,1)S(1)} %pad_maximum_fusion.a0), channel_id=1, source_target_pairs={{0,3},{1,0},{2,1},{3,2},{4,7},{5,4},{6,5},{7,6},{8,11},{9,8},{10,9... | collective-permute-start | bytes 2359304 | tf_op jit(solution)/shard_map/ppermute | solution.py:15
  98.9 21.1 %collective-permute-start.15 = (bf16[4,128,768]{2,1,0:T(8,128)(2,1)S(1)}, bf16[4,128,768]{2,1,0:T(8,128)(2,1)S(1)}, u32[]{:S(2)}, u32[]{:S(2)}) collective-permute-start(bf16[4,128,768]{2,1,0:T(8,128)(2,1)S(1)} %pad_maximum_fusion.a0), channel_id=1, source_target_pairs={{0,1},{1,2},{2,3},{3,0},{4,5},{5,6},{6,7},{7,4},{8,9},{9,10},{10,1... | collective-permute-start | bytes 2359304 | tf_op jit(solution)/shard_map/ppermute | solution.py:15
  99.8 21.1 %collective-permute-start.20 = (bf16[128,256]{1,0:T(8,128)(2,1)S(1)}, bf16[128,256]{1,0:T(8,128)(2,1)S(1)}, u32[]{:S(2)}, u32[]{:S(2)}) collective-permute-start(bf16[128,256]{1,0:T(8,128)(2,1)S(1)} %get-tuple-element.25), channel_id=1, source_target_pairs={{0,2},{1,3},{2,0},{3,1},{4,6},{5,7},{6,4},{7,5},{8,10},{9,11},{10,... | collective-permute-start | bytes 196616 | tf_op jit(solution)/shard_map/ppermute | solution.py:15
  100.5 22.2 %collective-permute-start.19 = (bf16[128,256]{1,0:T(8,128)(2,1)S(1)}, bf16[128,256]{1,0:T(8,128)(2,1)S(1)}, u32[]{:S(2)}, u32[]{:S(2)}) collective-permute-start(bf16[128,256]{1,0:T(8,128)(2,1)S(1)} %get-tuple-element.25), channel_id=1, source_target_pairs={{0,1},{1,2},{2,3},{3,0},{4,5},{5,6},{6,7},{7,4},{8,9},{9,10},{10,1... | collective-permute-start | bytes 196616 | tf_op jit(solution)/shard_map/ppermute | solution.py:15
  115.4 13.6 %copy-start.1 = (bf16[4,128,768]{2,1,0:T(8,128)(2,1)}, bf16[4,128,768]{2,1,0:T(8,128)(2,1)S(1)}, u32[]{:S(2)}) copy-start(bf16[4,128,768]{2,1,0:T(8,128)(2,1)S(1)} %collective-permute-done.17.a3) | copy-start | bytes 2359300
  115.5 7.3 %collective-permute-start.21 = (bf16[128,256]{1,0:T(8,128)(2,1)S(1)}, bf16[128,256]{1,0:T(8,128)(2,1)S(1)}, u32[]{:S(2)}, u32[]{:S(2)}) collective-permute-start(bf16[128,256]{1,0:T(8,128)(2,1)S(1)} %get-tuple-element.25), channel_id=1, source_target_pairs={{0,3},{1,0},{2,1},{3,2},{4,7},{5,4},{6,5},{7,6},{8,11},{9,8},{10,9... | collective-permute-start | bytes 196616 | tf_op jit(solution)/shard_map/ppermute | solution.py:15
  119.9 9.2 %copy-start.3 = (bf16[4,128,768]{2,1,0:T(8,128)(2,1)}, bf16[4,128,768]{2,1,0:T(8,128)(2,1)S(1)}, u32[]{:S(2)}) copy-start(bf16[4,128,768]{2,1,0:T(8,128)(2,1)S(1)} %collective-permute-done.15.a1) | copy-start | bytes 2359300
  119.9 29.9 %collective-permute-start.18 = (bf16[2,128,768]{2,1,0:T(8,128)(2,1)}, bf16[2,128,768]{2,1,0:T(8,128)(2,1)S(1)}, u32[]{:S(2)}, u32[]{:S(2)}) collective-permute-start(bf16[2,128,768]{2,1,0:T(8,128)(2,1)} %slice.58), channel_id=1, source_target_pairs={{0,3},{1,0},{2,1},{3,2},{4,7},{5,4},{6,5},{7,6},{8,11},{9,8},{10,9... | collective-permute-start | bytes 1179656 | tf_op jit(solution)/shard_map/ppermute | solution.py:15
  121.0 28.9 %collective-permute-start.16 = (bf16[2,128,768]{2,1,0:T(8,128)(2,1)}, bf16[2,128,768]{2,1,0:T(8,128)(2,1)}, u32[]{:S(2)}, u32[]{:S(2)}) collective-permute-start(bf16[2,128,768]{2,1,0:T(8,128)(2,1)} %slice.57), channel_id=1, source_target_pairs={{0,1},{1,2},{2,3},{3,0},{4,5},{5,6},{6,7},{7,4},{8,9},{9,10},{10,1... | collective-permute-start | bytes 1179656 | tf_op jit(solution)/shard_map/ppermute | solution.py:15
  122.8 12.0 %collective-permute-start.24 = (bf16[4,128,256]{2,1,0:T(8,128)(2,1)S(1)}, bf16[4,128,256]{2,1,0:T(8,128)(2,1)}, u32[]{:S(2)}, u32[]{:S(2)}) collective-permute-start(bf16[4,128,256]{2,1,0:T(8,128)(2,1)S(1)} %pad_maximum_fusion.7.e0), channel_id=1, source_target_pairs={{0,12},{4,0},{8,4},{12,8},{1,13},{5,1},{9,5},{13,9},{2,14},{6,2},{... | collective-permute-start | bytes 786440 | tf_op jit(solution)/shard_map/ppermute | solution.py:15
  124.4 25.5 %collective-permute-start.23 = (bf16[4,128,256]{2,1,0:T(8,128)(2,1)S(1)}, bf16[4,128,256]{2,1,0:T(8,128)(2,1)}, u32[]{:S(2)}, u32[]{:S(2)}) collective-permute-start(bf16[4,128,256]{2,1,0:T(8,128)(2,1)S(1)} %pad_maximum_fusion.7.e0), channel_id=1, source_target_pairs={{0,8},{4,12},{8,0},{12,4},{1,9},{5,13},{9,1},{13,5},{2,10},{6,14},... | collective-permute-start | bytes 786440 | tf_op jit(solution)/shard_map/ppermute | solution.py:15
  129.1 20.8 %collective-permute-start.22 = (bf16[4,128,256]{2,1,0:T(8,128)(2,1)S(1)}, bf16[4,128,256]{2,1,0:T(8,128)(2,1)}, u32[]{:S(2)}, u32[]{:S(2)}) collective-permute-start(bf16[4,128,256]{2,1,0:T(8,128)(2,1)S(1)} %pad_maximum_fusion.7.e0), channel_id=1, source_target_pairs={{0,4},{4,8},{8,12},{12,0},{1,5},{5,9},{9,13},{13,1},{2,6},{6,10},{... | collective-permute-start | bytes 786440 | tf_op jit(solution)/shard_map/ppermute | solution.py:15
  129.5 1.1 copy-start.2
  130.6 1.1 copy-start.4
  156.1 7.8 %collective-permute-start.31 = (f32[4,4,64,512]{3,2,1,0:T(8,128)}, f32[4,4,64,512]{3,2,1,0:T(8,128)S(1)}, u32[]{:S(2)}, u32[]{:S(2)}) collective-permute-start(f32[4,4,64,512]{3,2,1,0:T(8,128)} %shard_map.40), channel_id=1, source_target_pairs={{0,16},{16,0},{1,17},{17,1},{2,18},{18,2},{3,19},{19,3},{4,20},{20... | collective-permute-start | bytes 6291464 | tf_op jit(solution)/shard_map/ppermute | solution.py:15
  166.0 22.3 %copy-start.6 = (bf16[4,4,2,8,512]{4,3,2,1,0:T(8,128)(2,1)S(1)}, bf16[4,4,2,8,512]{4,3,2,1,0:T(8,128)(2,1)}, u32[]{:S(2)}) copy-start(bf16[4,4,2,8,512]{4,3,2,1,0:T(8,128)(2,1)} %copy-done.5) | copy-start | bytes 786436
  166.1 11.8 %collective-permute-start.32 = (bf16[16,2,8,512]{3,2,0,1:T(8,128)(2,1)S(1)}, bf16[16,2,8,512]{3,2,0,1:T(8,128)(2,1)S(1)}, u32[]{:S(2)}, u32[]{:S(2)}) collective-permute-start(bf16[16,2,8,512]{3,2,0,1:T(8,128)(2,1)S(1)} %get-tuple-element.5), channel_id=1, source_target_pairs={{0,32},{32,64},{64,96},{96,0},{1,33},{33,65},{65,97},{97,1},{2,34}... | collective-permute-start | bytes 786440 | tf_op jit(solution)/shard_map/ppermute | solution.py:15
  168.4 9.5 %collective-permute-start.34 = (bf16[16,2,8,512]{3,2,0,1:T(8,128)(2,1)S(1)}, bf16[16,2,8,512]{3,2,0,1:T(8,128)(2,1)S(1)}, u32[]{:S(2)}, u32[]{:S(2)}) collective-permute-start(bf16[16,2,8,512]{3,2,0,1:T(8,128)(2,1)S(1)} %get-tuple-element.6), channel_id=1, source_target_pairs={{0,96},{32,0},{64,32},{96,64},{1,97},{33,1},{65,33},{97,65},{2,98}... | collective-permute-start | bytes 786440 | tf_op jit(solution)/shard_map/ppermute | solution.py:15
  170.8 14.3 %collective-permute-start.33 = (bf16[16,2,8,512]{3,2,0,1:T(8,128)(2,1)S(1)}, bf16[16,2,8,512]{3,2,0,1:T(8,128)(2,1)S(1)}, u32[]{:S(2)}, u32[]{:S(2)}) collective-permute-start(bf16[16,2,8,512]{3,2,0,1:T(8,128)(2,1)S(1)} %get-tuple-element.7), channel_id=1, source_target_pairs={{0,64},{32,96},{64,0},{96,32},{1,65},{33,97},{65,1},{97,33},{2,66}... | collective-permute-start | bytes 786440 | tf_op jit(solution)/shard_map/ppermute | solution.py:15
  185.3 16.6 %collective-permute-start.35 = (f32[16,8,512]{2,1,0:T(8,128)S(1)}, f32[16,8,512]{2,1,0:T(8,128)S(1)}, u32[]{:S(2)}, u32[]{:S(2)}) collective-permute-start(f32[16,8,512]{2,1,0:T(8,128)S(1)} %slice_bitcast_fusion.1), channel_id=1, source_target_pairs={{0,128},{128,0},{1,129},{129,1},{2,130},{130,2},{3,131},{131,3},{4... | collective-permute-start | bytes 786440 | tf_op jit(solution)/shard_map/ppermute | solution.py:15
  202.8 12.5 %all-to-all-start = ((bf16[16,8,512]{2,1,0:T(8,128)(2,1)}), bf16[16,8,512]{2,1,0:T(8,128)(2,1)S(1)}, u32[]{:S(2)}, u32[]{:S(2)}) async-start(bf16[16,8,512]{2,1,0:T(8,128)(2,1)} %bitcast.84), calls=%async_computation | async-start | bytes 262144 | tf_op jit(solution)/shard_map/all_to_all | solution.py:144
  215.4 1.3 collective-permute-start.36

commit v2 on v1

v2 whole, which is shorter than its diff:
```python
import jax
import jax.numpy as jnp
from jax import lax
from jax.experimental import pallas as pl
from jax.experimental.pallas import tpu as pltpu
from jax.sharding import Mesh, PartitionSpec as P

AXES = ("zh", "x", "core", "zl", "y")
SIZES = {"zh": 2, "x": 4, "core": 2, "zl": 4, "y": 4}
F32, BF16 = jnp.float32, jnp.bfloat16


def shift(value, axis, step):
    n = SIZES[axis]
    return lax.ppermute(value, axis, [(i, (i + step) % n) for i in range(n)])


def pick(value, index, dim=0):
    return lax.dynamic_index_in_dim(value, index, dim, keepdims=False)


def exchange(pieces, axis, dim):
    n = SIZES[axis]
    me = lax.axis_index(axis)
    sent = [pick(pieces, (me + d) % n, dim) for d in range(n)]
    return jnp.stack([sent[0]] + [shift(sent[d], axis, d) for d in range(1, n)])


def gather(block, axis):
    return [block] + [shift(block, axis, d) for d in range(1, SIZES[axis])]


def gather_ring(block, axis):
    half = block.shape[0] // 2
    left, right = shift(block, axis, 1), shift(block, axis, -1)
    return block, left, shift(left[:half], axis, 1), shift(right[half:], axis, -1), right


def absolute(pieces, me, n, dim):
    turned = jnp.flip(pieces, dim)
    twice = jnp.concatenate([turned, turned], dim)
    return lax.dynamic_slice_in_dim(twice, n - 1 - me, n, dim)


def dot(left, right, dims):
    return lax.dot_general(left, right, (dims, ((), ())), preferred_element_type=F32)


def pair_kernel(a0, a1, a2, a2b, a3, part, out):
    for a, j, lo in ((a0, 0, 0), (a1, 1, 0), (a2, 2, 0), (a2b, 2, 2), (a3, 3, 0)):
        n = a.shape[0]
        value = dot(flat(a[...]), part[...], ((1,), (1,)))
        out[j, lo : lo + n] = value.reshape(n, a.shape[1], -1)


def tile_kernel(which, x_ref, kept, out, tile):
    @pl.when(pl.program_id(0) == 0)
    def _():
        tile[...] = kept[...].astype(BF16)

    out[...] = dot(x_ref[...], tile[...], ((1,), (0,)))


def mix_kernel(pairs, panel, tiles, mine, out, total):
    n = panel.shape[0]
    total[...] = jnp.zeros_like(total)

    @pl.loop(0, n * n)
    def _(step):
        dy, dz = step // n, step % n
        rows = []
        for i in range(n):
            src = (i + n - dy) % n
            rows += [pairs[src // 2, dy, dz, src % 2, (j + n - dz) % n] for j in range(n)]
        value = jnp.concatenate(rows)
        high = value.astype(BF16)
        low = (value - high.astype(F32)).astype(BF16)
        right = panel[dy, dz]
        total[...] += dot(jnp.concatenate([high, low], 1), jnp.concatenate([right, right]), ((1,), (0,)))

    out[...] = (mine[...].astype(F32) - (0.5 * total[...] + tiles[...])).astype(BF16)


def flat(value):
    return value.reshape(-1, value.shape[-1])


VMEM_SPEC = pl.BlockSpec(memory_space=pltpu.VMEM)


def call(kernel, shape, flops, args, specs, scratch=(), kind=F32):
    size = sum(a.size * a.dtype.itemsize for a in args)
    return pl.pallas_call(
        kernel,
        out_shape=jax.ShapeDtypeStruct(shape, kind),
        in_specs=specs,
        out_specs=VMEM_SPEC,
        scratch_shapes=scratch,
        compiler_params=pltpu.CompilerParams(vmem_limit_bytes=48 << 20),
        cost_estimate=pl.CostEstimate(flops=flops, bytes_accessed=size, transcendentals=0),
    )(*args)


def body(orbitals, gradient, stored):
    k, n = orbitals.shape
    rows, w, hw = 2 * k, n // 16, n // 32
    zh, x, core, zl, y = (lax.axis_index(a) for a in AXES)

    near, far = (orbitals, gradient), [shift(v, "core", 1) for v in (orbitals, gradient)]
    both = jnp.stack([jnp.where(core == 0, jnp.concatenate([p, q]), jnp.concatenate([q, p])) for p, q in zip(near, far)])

    to_r = pick(both.reshape(2, rows, 2, 4, 2, w), core, 4).transpose(3, 2, 0, 1, 4)
    to_c = pick(both[::-1].reshape(2, rows, 4, 4, 2, hw), core, 4).transpose(2, 3, 0, 1, 4)

    part_r = exchange(to_r, "x", 0)
    part_r = exchange(part_r, "zh", 1)
    near = jnp.stack(gather(part_r[:, :, 0].reshape(8 * rows, w), "zl"))
    pieces = gather_ring(near, "y")
    ordered = absolute(absolute(part_r, zh, 2, 0), x, 4, 1)
    ordered = ordered.transpose(2, 0, 1, 3, 4).reshape(16 * rows, w)

    part_c = exchange(to_c, "zl", 0)
    part_c = lax.optimization_barrier(exchange(part_c, "y", 1))
    mine = part_c[:, :, 0].reshape(16 * rows, hw)
    parts = gather(part_c, "zh")
    part_c = absolute(jnp.stack(parts), zh, 2, 0).transpose(1, 0, 2, 3, 4, 5)
    c0, c1, c2, c2b, c3 = gather_ring(part_c, "x")
    panel = absolute(jnp.stack([c0, c1, jnp.concatenate([c2, c2b]), c3]), x, 4, 0)
    panel = panel.transpose(1, 3, 4, 2, 0, 5, 6).reshape(4, 4, 16 * rows, hw)

    pairs = call(
        pair_kernel, (4, 4, 8 * rows, 16 * rows), 2 * 128 * rows * 16 * rows * w, (*pieces, ordered), [VMEM_SPEC] * 6
    ).reshape(2, 2, 4, 2, 4, rows, 16 * rows)
    pairs = pick(pairs, core) + shift(pick(pairs, 1 - core), "core", 1)
    pairs = pairs[:, :, :, 0] + sum(shift(pairs[:, :, :, 4 - d], "x", d) for d in range(1, 4))
    pairs = pairs[:, :, 0] + shift(pairs[:, :, 1], "zh", 1)
    pairs = jnp.stack(gather(pairs, "zl"))
    pairs = jnp.stack(gather(pairs, "y"))
    twin = shift(pairs, "core", 1)
    pairs = jnp.where(core == 0, jnp.stack([pairs, twin]), jnp.stack([twin, pairs]))

    x_r = jnp.concatenate([flat(p) for p in pieces])

    def product(which):
        step = 32 * rows
        grid = pltpu.PrefetchScalarGridSpec(
            num_scalar_prefetch=1,
            grid=(4,),
            in_specs=[pl.BlockSpec((step, w), lambda i, s: (i, 0)), pl.BlockSpec((w, hw), lambda i, s: (0, s[0]))],
            out_specs=pl.BlockSpec((step, hw), lambda i, s: (i, 0)),
            scratch_shapes=[pltpu.VMEM((w, hw), BF16)],
        )
        return pl.pallas_call(
            tile_kernel,
            out_shape=jax.ShapeDtypeStruct((4 * step, hw), F32),
            grid_spec=grid,
            compiler_params=pltpu.CompilerParams(vmem_limit_bytes=32 << 20),
            cost_estimate=pl.CostEstimate(flops=8 * step * w * hw, bytes_accessed=6 * w * hw, transcendentals=0),
        )(which[None], x_r, stored)

    away = product(1 - core)
    away = shift(away, "core", 1)
    own = product(core)
    total = (own + away).reshape(16, 2, 4, rows, hw)
    sent = [total[:, :, 4 - d].astype(BF16) for d in range(1, 4)]
    got = [shift(v, "x", d) for d, v in enumerate(sent, 1)]
    total = total[:, :, 0] + sum(g.astype(F32) for g in got)
    total = total[:, 0] + shift(total[:, 1].astype(BF16), "zh", 1).astype(F32)

    args = (pairs, panel, total.reshape(16 * rows, hw), mine)
    result = call(mix_kernel, mine.shape, 8 * 16 * rows * 128 * rows * hw, args, [VMEM_SPEC] * 4, [pltpu.VMEM(mine.shape, F32)], BF16)
    result = result.reshape(4, 4, rows, hw)
    back = absolute(absolute(result, y, 4, 0), zl, 4, 1)
    result = lax.all_to_all(
        back.transpose(1, 0, 2, 3).reshape(16, rows, hw), ("zl", "y"), split_axis=0, concat_axis=0, tiled=True
    )
    result = result.reshape(16, 2, k, hw)
    kept, got = pick(result, core, 1), shift(pick(result, 1 - core, 1), "core", 1)
    halves = jnp.where(core == 0, jnp.stack([kept, got]), jnp.stack([got, kept]))
    return halves.transpose(2, 1, 0, 3).reshape(k, n)


def solution(mesh):
    fine = Mesh(mesh.devices.reshape(tuple(SIZES.values())), AXES)
    return jax.shard_map(
        body,
        mesh=fine,
        in_specs=(P(AXES, None), P(AXES, None), P(("zh", "x", "core"), ("zl", "y"))),
        out_specs=P(AXES, None),
        check_vma=False,
    )
```

time: 220 us -> 166 us (0.75)
  waiting for transfers between devices: 111 us -> 35.5 us
  blocking collectives: 0 us -> 13.6 us
  local copies, waits for them, and re-layouts: 6.35 us -> 17.2 us
  other arithmetic: 6.09 us -> 15 us
  Pallas kernels: 16.9 us -> 10.3 us
  starting transfers between devices: 77.1 us -> 72.4 us
    ppermute x37 -> x42, waiting for transfers between devices: 102 us -> 35.5 us  [shift(): return lax.ppermute(value, axis, [(i, (i + step) % n) for i in range(n)])]
    all_to_all x0 -> x1, blocking collectives: none -> 13.6 us  [body(): lax.all_to_all(back.transpose(1, 0, 2, 3).reshape(16, rows, hw), ('zl', '...]
    all_to_all x1 -> x0, waiting for transfers between devices: 8.99 us -> none  [body(): lax.all_to_all(back.transpose(1, 0, 2, 3).reshape(16, rows, hw), ('zl', '...]
    another operation x5 -> x7, other arithmetic: 0.3 us -> 7.54 us  [the longest x3 5.42 us: body(): jnp.stack([c0, c1, jnp.concatenate([c2, c2b]), c3])]
    pallas_call x4, Pallas kernels: 16.9 us -> 10.3 us  [the longest x2 5.29 us: product(): pl.pallas_call(tile_kernel, out_shape=jax.ShapeDtypeStruct((4 * step, hw)...]
    rev x1 -> x6, local copies, waits for them, and re-layouts: 0.01 us -> 5.31 us  [absolute(): turned = jnp.flip(pieces, dim)]
    all_to_all x1 -> x0, starting transfers between devices: 3.51 us -> none  [body(): lax.all_to_all(back.transpose(1, 0, 2, 3).reshape(16, rows, hw), ('zl', '...]
    unnamed x19 -> x22, local copies, waits for them, and re-layouts: 2.31 us -> 4.66 us
  transfers between devices with their start and end apart: 38 -> 42, of which waited for: 20 -> 17; matrix products, arithmetic and copies ran while one was open for 2% -> 16% of each run, Pallas kernels for 5% -> 4%
where the time goes in v2:
time: 166 us; the launch traced here: 164 us
  starting transfers between devices  72.4 us (44%)
  waiting for transfers between devices  35.5 us (21%)
  local copies, waits for them, and re-layouts  17.2 us (10%)
  other arithmetic  15 us (9%)
  blocking collectives  13.6 us (8%)
  Pallas kernels  10.3 us (6%)
    ppermute x42, starting transfers between devices, shift(): return lax.ppermute(value, axis, [(i, (i + step) % n) for i in range(n)])  72.4 us
    ppermute x42, waiting for transfers between devices, shift(): return lax.ppermute(value, axis, [(i, (i + step) % n) for i in range(n)])  35.5 us
    all_to_all x1, blocking collectives, body(): lax.all_to_all(back.transpose(1, 0, 2, 3).reshape(16, rows, hw), ('zl', '...  13.6 us
    another operation x3, other arithmetic, body(): jnp.stack([c0, c1, jnp.concatenate([c2, c2b]), c3])  5.42 us
    rev x6, local copies, waits for them, and re-layouts, absolute(): turned = jnp.flip(pieces, dim)  5.31 us
    pallas_call x2, Pallas kernels, product(): pl.pallas_call(tile_kernel, out_shape=jax.ShapeDtypeStruct((4 * step, hw)...  5.29 us
    pallas_call x2, Pallas kernels, call(): pl.pallas_call(kernel, out_shape=jax.ShapeDtypeStruct(shape, kind), in_sp...  5.04 us
    unnamed x22, local copies, waits for them, and re-layouts  4.66 us
  transfers between devices with their start and end apart: 42, of which 17 were waited for; matrix products, arithmetic and copies ran while one was open for 16% of the time, Pallas kernels for 4%

profile of v2, /device:TPU:2, one launch (start us, length us, event | category | flops | bytes accessed | tf_op | source)
XLA Modules:
  0.0 164.5 jit_solution(17502866573817561483)
XLA Ops:
  0.5 1.0 collective-permute-done
  1.6 1.2 maximum_select_fusion.1
  2.8 1.2 maximum_select_fusion.2
  4.1 1.6 collective-permute-start.2
  5.7 2.8 %collective-permute-start.3 = (bf16[2,2,8,1024]{3,2,0,1:T(8,128)(2,1)S(1)}, bf16[2,2,8,1024]{3,2,0,1:T(8,128)(2,1)S(1)}, u32[]{:S(2)}, u32[]{:S(2)}) collective-permute-start(bf16[2,2,8,1024]{3,2,0,1:T(8,128)(2,1)S(1)} %get-tuple-element.21), channel_id=1, source_target_pairs={{0,64},{32,96},{64,0},{96,32},{1,65},{33,97},{65,1},{97,33},{2,66}... | collective-permute-start | bytes 196616 | tf_op jit(solution)/shard_map/ppermute | solution.py:15
  9.4 2.4 %collective-permute-done.3 = bf16[2,2,8,1024]{3,2,0,1:T(8,128)(2,1)S(1)} collective-permute-done((bf16[2,2,8,1024]{3,2,0,1:T(8,128)(2,1)S(1)}, bf16[2,2,8,1024]{3,2,0,1:T(8,128)(2,1)S(1)}, u32[]{:S(2)}, u32[]{:S(2)}) %collective-permute-start.3) | collective-permute-done | bytes 65568 | tf_op jit(solution)/shard_map/ppermute | solution.py:15
  11.8 0.9 collective-permute-done.4
  12.8 6.3 %collective-permute-start.5 = (bf16[4,2,8,1024]{3,2,0,1:T(8,128)(2,1)S(1)}, bf16[4,2,8,1024]{3,2,0,1:T(8,128)(2,1)S(1)}, u32[]{:S(2)}, u32[]{:S(2)}) collective-permute-start(bf16[4,2,8,1024]{3,2,0,1:T(8,128)(2,1)S(1)} %get-tuple-element.29), channel_id=1, source_target_pairs={{0,128},{128,0},{1,129},{129,1},{2,130},{130,2},{3,131},{131,3},{4... | collective-permute-start | bytes 393224 | tf_op jit(solution)/shard_map/ppermute | solution.py:15
  19.2 1.1 collective-permute-start.25
  20.3 1.5 collective-permute-start.26
  21.8 1.9 %collective-permute-start.27 = (bf16[4,2,8,512]{3,2,0,1:T(8,128)(2,1)S(1)}, bf16[4,2,8,512]{3,2,0,1:T(8,128)(2,1)S(1)}, u32[]{:S(2)}, u32[]{:S(2)}) collective-permute-start(bf16[4,2,8,512]{3,2,0,1:T(8,128)(2,1)S(1)} %get-tuple-element.11), channel_id=1, source_target_pairs={{0,12},{4,0},{8,4},{12,8},{1,13},{5,1},{9,5},{13,9},{2,14},{6,2},{... | collective-permute-start | bytes 196616 | tf_op jit(solution)/shard_map/ppermute | solution.py:15
  24.4 3.8 %collective-permute-start.6 = (bf16[64,1024]{1,0:T(8,128)(2,1)S(1)}, bf16[64,1024]{1,0:T(8,128)(2,1)S(1)}, u32[]{:S(2)}, u32[]{:S(2)}) collective-permute-start(bf16[64,1024]{1,0:T(8,128)(2,1)S(1)} %bitcast.210), channel_id=1, source_target_pairs={{0,4},{4,8},{8,12},{12,0},{1,5},{5,9},{9,13},{13,1},{2,6},{6,10},{... | collective-permute-start | bytes 393224 | tf_op jit(solution)/shard_map/ppermute | solution.py:15
  28.4 2.4 %collective-permute-start.8 = (bf16[64,1024]{1,0:T(8,128)(2,1)S(1)}, bf16[64,1024]{1,0:T(8,128)(2,1)S(1)}, u32[]{:S(2)}, u32[]{:S(2)}) collective-permute-start(bf16[64,1024]{1,0:T(8,128)(2,1)S(1)} %bitcast.212), channel_id=1, source_target_pairs={{0,12},{4,0},{8,4},{12,8},{1,13},{5,1},{9,5},{13,9},{2,14},{6,2},{... | collective-permute-start | bytes 393224 | tf_op jit(solution)/shard_map/ppermute | solution.py:15
  30.8 1.7 %collective-permute-done.26 = bf16[4,2,8,512]{3,2,0,1:T(8,128)(2,1)S(1)} collective-permute-done((bf16[4,2,8,512]{3,2,0,1:T(8,128)(2,1)S(1)}, bf16[4,2,8,512]{3,2,0,1:T(8,128)(2,1)S(1)}, u32[]{:S(2)}, u32[]{:S(2)}) %collective-permute-start.26) | collective-permute-done | bytes 65568 | tf_op jit(solution)/shard_map/ppermute | solution.py:15
  32.6 1.7 %collective-permute-start.28 = (bf16[4,2,8,512]{3,2,0,1:T(8,128)(2,1)S(1)}, bf16[4,2,8,512]{3,2,0,1:T(8,128)(2,1)S(1)}, u32[]{:S(2)}, u32[]{:S(2)}) collective-permute-start(bf16[4,2,8,512]{3,2,0,1:T(8,128)(2,1)S(1)} %get-tuple-element.25), channel_id=1, source_target_pairs={{0,1},{1,2},{2,3},{3,0},{4,5},{5,6},{6,7},{7,4},{8,9},{9,10},{10,1... | collective-permute-start | bytes 196616 | tf_op jit(solution)/shard_map/ppermute | solution.py:15
  34.3 2.9 %collective-permute-start.29 = (bf16[4,2,8,512]{3,2,0,1:T(8,128)(2,1)S(1)}, bf16[4,2,8,512]{3,2,0,1:T(8,128)(2,1)S(1)}, u32[]{:S(2)}, u32[]{:S(2)}) collective-permute-start(bf16[4,2,8,512]{3,2,0,1:T(8,128)(2,1)S(1)} %get-tuple-element.24), channel_id=1, source_target_pairs={{0,2},{1,3},{2,0},{3,1},{4,6},{5,7},{6,4},{7,5},{8,10},{9,11},{10,... | collective-permute-start | bytes 196616 | tf_op jit(solution)/shard_map/ppermute | solution.py:15
  37.2 1.3 collective-permute-start.30
  38.8 1.8 %collective-permute-start.9 = (bf16[4,64,1024]{2,1,0:T(8,128)(2,1)S(1)}, bf16[4,64,1024]{2,1,0:T(8,128)(2,1)S(1)}, u32[]{:S(2)}, u32[]{:S(2)}) collective-permute-start(bf16[4,64,1024]{2,1,0:T(8,128)(2,1)S(1)} %pad_maximum_fusion.1.a0), channel_id=1, source_target_pairs={{0,1},{1,2},{2,3},{3,0},{4,5},{5,6},{6,7},{7,4},{8,9},{9,10},{10,1... | collective-permute-start | bytes 1572872 | tf_op jit(solution)/shard_map/ppermute | solution.py:15
  40.7 0.8 collective-permute-done.30
  42.2 4.8 %collective-permute-start.31 = (bf16[4,4,2,8,512]{4,3,1,0,2:T(8,128)(2,1)}, bf16[4,4,2,8,512]{4,3,1,0,2:T(8,128)(2,1)}, u32[]{:S(2)}, u32[]{:S(2)}) collective-permute-start(bf16[4,4,2,8,512]{4,3,1,0,2:T(8,128)(2,1)} %pad_maximum_fusion.8), channel_id=1, source_target_pairs={{0,128},{128,0},{1,129},{129,1},{2,130},{130,2},{3,131},{131,3},{4... | collective-permute-start | bytes 786440 | tf_op jit(solution)/shard_map/ppermute | solution.py:15
  47.0 2.6 %collective-permute-start.11 = (bf16[4,64,1024]{2,1,0:T(8,128)(2,1)S(1)}, bf16[4,64,1024]{2,1,0:T(8,128)(2,1)}, u32[]{:S(2)}, u32[]{:S(2)}) collective-permute-start(bf16[4,64,1024]{2,1,0:T(8,128)(2,1)S(1)} %pad_maximum_fusion.1.a0), channel_id=1, source_target_pairs={{0,3},{1,0},{2,1},{3,2},{4,7},{5,4},{6,5},{7,6},{8,11},{9,8},{10,9... | collective-permute-start | bytes 1572872 | tf_op jit(solution)/shard_map/ppermute | solution.py:15
  49.9 4.1 %collective-permute-done.9.a1 = bf16[4,64,1024]{2,1,0:T(8,128)(2,1)S(1)} collective-permute-done((bf16[4,64,1024]{2,1,0:T(8,128)(2,1)S(1)}, bf16[4,64,1024]{2,1,0:T(8,128)(2,1)S(1)}, u32[]{:S(2)}, u32[]{:S(2)}) %collective-permute-start.9) | collective-permute-done | bytes 524320 | tf_op jit(solution)/shard_map/ppermute | solution.py:15
  55.0 4.0 %collective-permute-done.31 = bf16[4,4,2,8,512]{4,3,1,0,2:T(8,128)(2,1)} collective-permute-done((bf16[4,4,2,8,512]{4,3,1,0,2:T(8,128)(2,1)}, bf16[4,4,2,8,512]{4,3,1,0,2:T(8,128)(2,1)}, u32[]{:S(2)}, u32[]{:S(2)}) %collective-permute-start.31) | collective-permute-done | bytes 262176 | tf_op jit(solution)/shard_map/ppermute | solution.py:15
  59.0 1.9 %pad_maximum_fusion.4 = bf16[2,4,4,2,8,512]{5,4,2,1,3,0:T(8,128)(2,1)} fusion(bf16[1,4,4,2,8,512]{5,4,2,1,3,0:T(8,128)(2,1)} %bitcast.80, bf16[1,4,4,2,8,512]{5,4,2,1,3,0:T(8,128)(2,1)} %bitcast.79), kind=kLoop, calls=%fused_computation.26 | loop fusion | flops 262144 | bytes 1048576 | tf_op jit(solution)/shard_map/stack | solution.py:126
  60.9 1.9 %rev.30 = bf16[2,4,4,2,8,512]{5,4,2,1,3,0:T(8,128)(2,1)} reverse(bf16[2,4,4,2,8,512]{5,4,2,1,3,0:T(8,128)(2,1)} %pad_maximum_fusion.4), dimensions={0} | reverse | bytes 1048576 | tf_op jit(solution)/shard_map/jit(_flip)/rev | solution.py:40
  62.8 1.0 slice.79
  63.8 1.9 %collective-permute-start.12 = (bf16[2,64,1024]{2,1,0:T(8,128)(2,1)S(1)}, bf16[2,64,1024]{2,1,0:T(8,128)(2,1)S(1)}, u32[]{:S(2)}, u32[]{:S(2)}) collective-permute-start(bf16[2,64,1024]{2,1,0:T(8,128)(2,1)S(1)} %slice.79), channel_id=1, source_target_pairs={{0,3},{1,0},{2,1},{3,2},{4,7},{5,4},{6,5},{7,6},{8,11},{9,8},{10,9... | collective-permute-start | bytes 786440 | tf_op jit(solution)/shard_map/ppermute | solution.py:15
  65.7 2.6 %fusion.26 = (bf16[1,4,2,4,2,8,512]{6,5,3,1,4,2,0:T(8,128)(2,1)}, bf16[4,2,4,2,8,512]{5,4,2,0,3,1:T(8,128)(2,1)}) fusion(s32[]{:T(128)S(6)} %select_n.236, bf16[2,4,4,2,8,512]{5,4,2,1,3,0:T(8,128)(2,1)} %rev.30), kind=kLoop, calls=%fused_computation.101 | loop fusion | flops 524288 | bytes 1572868 | tf_op jit(solution)/shard_map/stack | solution.py:128
  68.3 1.5 collective-permute-start.32
  70.3 1.0 constant_dynamic-update-slice_fusion.2
  71.4 1.1 constant_dynamic-update-slice_fusion.x_ref
  72.4 3.2 %shard_map.39 = f32[1024,512]{1,0:T(8,128)} custom-call(s32[1]{0:T(128)} %bitcast.94.which, bf16[1024,1024]{1,0:T(8,128)(2,1)S(1)} %constant_dynamic-update-slice_fusion.x_ref, f32[1024,1024]{1,0:T(8,128)S(1)} %copy-done), custom_call_target="tpu_custom_call" | custom-call | flops 1073741824 | bytes 3145728 | tf_op jit(solution)/shard_map/pallas_call | solution.py:153
  75.7 1.8 %shard_map.37 = f32[4,4,64,128]{3,2,1,0:T(8,128)S(1)} custom-call(bf16[4,64,1024]{2,1,0:T(8,128)(2,1)S(1)} %pad_maximum_fusion.1.a0, bf16[4,64,1024]{2,1,0:T(8,128)(2,1)S(1)} %collective-permute-done.9.a1, bf16[2,64,1024]{2,1,0:T(8,128)(2,1)} %collective-permute-done.10.a2, bf16[2,64,1024]{2,1,0:T(8,128)(2,1)S(1)} %collective-permute-done.12.a2b, ...), custom_call_target="tpu_custom_call" | custom-call | flops 268435456 | bytes 2359296 | tf_op jit(solution)/shard_map/pallas_call | solution.py:93
  78.2 0.9 slice.94
  79.5 1.0 slice.86
  80.5 1.6 collective-permute-start.33
  82.1 1.0 slice.87
  83.1 2.0 %collective-permute-start.14 = (f32[2,4,2,8,128]{4,3,1,0,2:T(8,128)S(1)}, f32[2,4,2,8,128]{4,3,1,0,2:T(8,128)S(1)}, u32[]{:S(2)}, u32[]{:S(2)}) collective-permute-start(f32[2,4,2,8,128]{4,3,1,0,2:T(8,128)S(1)} %get-tuple-element.28), channel_id=1, source_target_pairs={{0,32},{32,64},{64,96},{96,0},{1,33},{33,65},{65,97},{97,1},{2,34}... | collective-permute-start | bytes 196616 | tf_op jit(solution)/shard_map/ppermute | solution.py:15
  85.2 1.6 collective-permute-start.15
  86.8 2.5 %collective-permute-start.16 = (f32[2,4,2,8,128]{4,3,1,0,2:T(8,128)S(1)}, f32[2,4,2,8,128]{4,3,1,0,2:T(8,128)S(1)}, u32[]{:S(2)}, u32[]{:S(2)}) collective-permute-start(f32[2,4,2,8,128]{4,3,1,0,2:T(8,128)S(1)} %get-tuple-element.27), channel_id=1, source_target_pairs={{0,96},{32,0},{64,32},{96,64},{1,97},{33,1},{65,33},{97,65},{2,98}... | collective-permute-start | bytes 196616 | tf_op jit(solution)/shard_map/ppermute | solution.py:15
  89.3 2.2 %copy-done.1 = f32[1024,1024]{1,0:T(8,128)S(1)} copy-done((f32[1024,1024]{1,0:T(8,128)S(1)}, f32[1024,1024]{1,0:T(8,128)}, u32[]{:S(2)}) %copy-start.1) | copy-done | bytes 4194328
  91.5 2.0 %shard_map.38 = f32[1024,512]{1,0:T(8,128)S(1)} custom-call(s32[1]{0:T(128)} %bitcast.88.which, bf16[1024,1024]{1,0:T(8,128)(2,1)S(1)} %constant_dynamic-update-slice_fusion.x_ref, f32[1024,1024]{1,0:T(8,128)S(1)} %copy-done.1), custom_call_target="tpu_custom_call" | custom-call | flops 1073741824 | bytes 3145728 | tf_op jit(solution)/shard_map/pallas_call | solution.py:153
  93.6 1.4 copy-done.2
  95.5 5.0 %collective-permute-start.17 = (f32[2,4,8,128]{3,2,1,0:T(8,128)S(1)}, f32[2,4,8,128]{3,2,1,0:T(8,128)S(1)}, u32[]{:S(2)}, u32[]{:S(2)}) collective-permute-start(f32[2,4,8,128]{3,2,1,0:T(8,128)S(1)} %slice_bitcast_fusion.9), channel_id=1, source_target_pairs={{0,128},{128,0},{1,129},{129,1},{2,130},{130,2},{3,131},{131,3},{4... | collective-permute-start | bytes 98312 | tf_op jit(solution)/shard_map/ppermute | solution.py:15
  100.5 1.2 collective-permute-done.35
  101.7 2.1 %collective-permute-done.17 = f32[2,4,8,128]{3,2,1,0:T(8,128)S(1)} collective-permute-done((f32[2,4,8,128]{3,2,1,0:T(8,128)S(1)}, f32[2,4,8,128]{3,2,1,0:T(8,128)S(1)}, u32[]{:S(2)}, u32[]{:S(2)}) %collective-permute-start.17) | collective-permute-done | bytes 32800 | tf_op jit(solution)/shard_map/ppermute | solution.py:15
  103.8 5.4 %collective-permute-start.18 = (f32[2,4,8,128]{3,2,1,0:T(8,128)S(1)}, f32[2,4,8,128]{3,2,1,0:T(8,128)S(1)}, u32[]{:S(2)}, u32[]{:S(2)}) collective-permute-start(f32[2,4,8,128]{3,2,1,0:T(8,128)S(1)} %fusion.23), channel_id=1, source_target_pairs={{0,4},{4,8},{8,12},{12,0},{1,5},{5,9},{9,13},{13,1},{2,6},{6,10},{... | collective-permute-start | bytes 98312 | tf_op jit(solution)/shard_map/ppermute | solution.py:15
  109.2 2.5 %collective-permute-start.20 = (f32[2,4,8,128]{3,2,1,0:T(8,128)S(1)}, f32[2,4,8,128]{3,2,1,0:T(8,128)S(1)}, u32[]{:S(2)}, u32[]{:S(2)}) collective-permute-start(f32[2,4,8,128]{3,2,1,0:T(8,128)S(1)} %fusion.23), channel_id=1, source_target_pairs={{0,12},{4,0},{8,4},{12,8},{1,13},{5,1},{9,5},{13,9},{2,14},{6,2},{... | collective-permute-start | bytes 98312 | tf_op jit(solution)/shard_map/ppermute | solution.py:15
  111.7 2.8 %pad_maximum_fusion = bf16[4,4,2,4,2,8,512]{6,5,3,1,4,2,0:T(8,128)(2,1)} fusion(bf16[1,4,2,4,2,8,512]{6,5,3,1,4,2,0:T(8,128)(2,1)} %bitcast.85, bf16[1,4,2,4,2,8,512]{6,5,3,1,4,2,0:T(8,128)(2,1)S(1)} %maximum_bitcast_fusion, bf16[1,4,2,4,2,8,512]{6,5,3,1,4,2,0:T(8,128)(2,1)} %bitcast.83, bf16[1,4,2,4,2,8,512]{6,5,3,1,4,2,0:T(8,128)(2,1)S(1)} %copy-done.5), kind=kLoop, calls=%fused_computation.4 | loop fusion | flops 3145728 | bytes 4194304 | tf_op jit(solution)/shard_map/stack | solution.py:128
  114.4 3.4 %rev.31 = bf16[4,4,2,4,2,8,512]{6,5,3,1,4,2,0:T(8,128)(2,1)} reverse(bf16[4,4,2,4,2,8,512]{6,5,3,1,4,2,0:T(8,128)(2,1)} %pad_maximum_fusion), dimensions={0} | reverse | bytes 4194304 | tf_op jit(solution)/shard_map/jit(_flip)/rev | solution.py:40
  117.9 2.5 %collective-permute-start.22 = (f32[4,2,4,8,128]{4,3,2,1,0:T(8,128)S(1)}, f32[4,2,4,8,128]{4,3,2,1,0:T(8,128)S(1)}, u32[]{:S(2)}, u32[]{:S(2)}) collective-permute-start(f32[4,2,4,8,128]{4,3,2,1,0:T(8,128)S(1)} %get-tuple-element.34), channel_id=1, source_target_pairs={{0,2},{1,3},{2,0},{3,1},{4,6},{5,7},{6,4},{7,5},{8,10},{9,11},{10,... | collective-permute-start | bytes 393224 | tf_op jit(solution)/shard_map/ppermute | solution.py:15
  120.4 2.0 %collective-permute-start.23 = (f32[4,2,4,8,128]{4,3,2,1,0:T(8,128)S(1)}, f32[4,2,4,8,128]{4,3,2,1,0:T(8,128)S(1)}, u32[]{:S(2)}, u32[]{:S(2)}) collective-permute-start(f32[4,2,4,8,128]{4,3,2,1,0:T(8,128)S(1)} %get-tuple-element.34), channel_id=1, source_target_pairs={{0,3},{1,0},{2,1},{3,2},{4,7},{5,4},{6,5},{7,6},{8,11},{9,8},{10,9... | collective-permute-start | bytes 393224 | tf_op jit(solution)/shard_map/ppermute | solution.py:15
  122.4 2.1 %add.277 = f32[1024,512]{1,0:T(8,128)S(1)} add(f32[1024,512]{1,0:T(8,128)S(1)} %copy-done.3, f32[1024,512]{1,0:T(8,128)} %collective-permute-done.36) | non-fusion elementwise | flops 524288 | bytes 6291456 | tf_op jit(solution)/shard_map/add | solution.py:164
  124.6 0.9 collective-permute-start.37
  125.5 1.1 collective-permute-start.38
  126.5 1.1 collective-permute-start.39
  129.0 2.1 %collective-permute-done.37 = bf16[16,2,8,512]{3,2,0,1:T(8,128)(2,1)S(1)} collective-permute-done((bf16[16,2,8,512]{3,2,0,1:T(8,128)(2,1)S(1)}, bf16[16,2,8,512]{3,2,0,1:T(8,128)(2,1)S(1)}, u32[]{:S(2)}, u32[]{:S(2)}) %collective-permute-start.37) | collective-permute-done | bytes 262176 | tf_op jit(solution)/shard_map/ppermute | solution.py:15
  131.0 2.4 %collective-permute-done.38 = bf16[16,2,8,512]{3,2,0,1:T(8,128)(2,1)S(1)} collective-permute-done((bf16[16,2,8,512]{3,2,0,1:T(8,128)(2,1)S(1)}, bf16[16,2,8,512]{3,2,0,1:T(8,128)(2,1)S(1)}, u32[]{:S(2)}, u32[]{:S(2)}) %collective-permute-start.38) | collective-permute-done | bytes 262176 | tf_op jit(solution)/shard_map/ppermute | solution.py:15
  133.4 2.3 %collective-permute-done.39 = bf16[16,2,8,512]{3,2,0,1:T(8,128)(2,1)S(1)} collective-permute-done((bf16[16,2,8,512]{3,2,0,1:T(8,128)(2,1)S(1)}, bf16[16,2,8,512]{3,2,0,1:T(8,128)(2,1)S(1)}, u32[]{:S(2)}, u32[]{:S(2)}) %collective-permute-start.39) | collective-permute-done | bytes 262176 | tf_op jit(solution)/shard_map/ppermute | solution.py:15
  135.9 1.0 collective-permute-start.40
  137.0 8.0 %collective-permute-done.40 = bf16[16,8,512]{2,1,0:T(8,128)(2,1)S(1)} collective-permute-done((bf16[16,8,512]{2,1,0:T(8,128)(2,1)S(1)}, bf16[16,8,512]{2,1,0:T(8,128)(2,1)S(1)}, u32[]{:S(2)}, u32[]{:S(2)}) %collective-permute-start.40) | collective-permute-done | bytes 131104 | tf_op jit(solution)/shard_map/ppermute | solution.py:15
  145.1 3.2 %shard_map.40 = bf16[128,512]{1,0:T(8,128)(2,1)S(1)} custom-call(f32[2,4,4,2,4,8,128]{6,5,4,3,2,1,0:T(8,128)S(1)} %maximum_select_fusion.pairs, bf16[4,4,128,512]{3,2,1,0:T(8,128)(2,1)S(1)} %bitcast.187, f32[128,512]{1,0:T(8,128)S(1)} %fusion.7.tiles, bf16[128,512]{1,0:T(8,128)(2,1)S(1)} %bitcast.193), custom_call_target="tpu_custom_call" | custom-call | flops 536870912 | bytes 3538944 | tf_op jit(solution)/shard_map/pallas_call | solution.py:93
  148.5 13.6 %all_to_all.5 = bf16[16,8,512]{2,1,0:T(8,128)(2,1)S(1)} all-to-all(bf16[16,8,512]{2,1,0:T(8,128)(2,1)S(1)} %bitcast.209), channel_id=1, replica_groups=mesh['zh'=2,'x'=4,'core'=2,'zl'=4,'y'=4] {'zl','y'}, dimensions={0} | all-to-all | bytes 262144 | tf_op jit(solution)/shard_map/all_to_all | solution.py:174
  162.4 1.2 collective-permute-done.41
  (106 shorter events, 10.4 us)
Async XLA Ops:
  0.0 8.9 %copy-start.6 = (bf16[4,16384]{1,0:T(4,128)(2,1)S(1)}, bf16[4,16384]{1,0:T(4,128)(2,1)}, u32[]{:S(2)}) copy-start(bf16[4,16384]{1,0:T(4,128)(2,1)} %param.3) | copy-start | bytes 393220
  0.0 9.2 %copy-start.7 = (bf16[4,16384]{1,0:T(4,128)(2,1)S(1)}, bf16[4,16384]{1,0:T(4,128)(2,1)}, u32[]{:S(2)}) copy-start(bf16[4,16384]{1,0:T(4,128)(2,1)} %param.4) | copy-start | bytes 393220
  0.0 1.6 collective-permute-start
  0.0 2.8 %collective-permute-start.1 = (bf16[4,16384]{1,0:T(4,128)(2,1)}, bf16[4,16384]{1,0:T(4,128)(2,1)S(1)}, u32[]{:S(2)}, u32[]{:S(2)}) collective-permute-start(bf16[4,16384]{1,0:T(4,128)(2,1)} %param.4), channel_id=1, source_target_pairs={{0,16},{16,0},{1,17},{17,1},{2,18},{18,2},{3,19},{19,3},{4,20},{20... | collective-permute-start | bytes 393224 | tf_op jit(solution)/shard_map/ppermute | solution.py:15
  4.1 5.3 %collective-permute-start.2 = (bf16[2,2,8,1024]{3,2,0,1:T(8,128)(2,1)S(1)}, bf16[2,2,8,1024]{3,2,0,1:T(8,128)(2,1)S(1)}, u32[]{:S(2)}, u32[]{:S(2)}) collective-permute-start(bf16[2,2,8,1024]{3,2,0,1:T(8,128)(2,1)S(1)} %get-tuple-element.20), channel_id=1, source_target_pairs={{0,32},{32,64},{64,96},{96,0},{1,33},{33,65},{65,97},{97,1},{2,34}... | collective-permute-start | bytes 196616 | tf_op jit(solution)/shard_map/ppermute | solution.py:15
  5.7 6.2 %collective-permute-start.3 = (bf16[2,2,8,1024]{3,2,0,1:T(8,128)(2,1)S(1)}, bf16[2,2,8,1024]{3,2,0,1:T(8,128)(2,1)S(1)}, u32[]{:S(2)}, u32[]{:S(2)}) collective-permute-start(bf16[2,2,8,1024]{3,2,0,1:T(8,128)(2,1)S(1)} %get-tuple-element.21), channel_id=1, source_target_pairs={{0,64},{32,96},{64,0},{96,32},{1,65},{33,97},{65,1},{97,33},{2,66}... | collective-permute-start | bytes 196616 | tf_op jit(solution)/shard_map/ppermute | solution.py:15
  8.5 4.3 %collective-permute-start.4 = (bf16[2,2,8,1024]{3,2,0,1:T(8,128)(2,1)S(1)}, bf16[2,2,8,1024]{3,2,0,1:T(8,128)(2,1)S(1)}, u32[]{:S(2)}, u32[]{:S(2)}) collective-permute-start(bf16[2,2,8,1024]{3,2,0,1:T(8,128)(2,1)S(1)} %get-tuple-element.19), channel_id=1, source_target_pairs={{0,96},{32,0},{64,32},{96,64},{1,97},{33,1},{65,33},{97,65},{2,98}... | collective-permute-start | bytes 196616 | tf_op jit(solution)/shard_map/ppermute | solution.py:15
  12.8 11.5 %collective-permute-start.5 = (bf16[4,2,8,1024]{3,2,0,1:T(8,128)(2,1)S(1)}, bf16[4,2,8,1024]{3,2,0,1:T(8,128)(2,1)S(1)}, u32[]{:S(2)}, u32[]{:S(2)}) collective-permute-start(bf16[4,2,8,1024]{3,2,0,1:T(8,128)(2,1)S(1)} %get-tuple-element.29), channel_id=1, source_target_pairs={{0,128},{128,0},{1,129},{129,1},{2,130},{130,2},{3,131},{131,3},{4... | collective-permute-start | bytes 393224 | tf_op jit(solution)/shard_map/ppermute | solution.py:15
  19.2 9.2 %collective-permute-start.25 = (bf16[4,2,8,512]{3,2,0,1:T(8,128)(2,1)S(1)}, bf16[4,2,8,512]{3,2,0,1:T(8,128)(2,1)S(1)}, u32[]{:S(2)}, u32[]{:S(2)}) collective-permute-start(bf16[4,2,8,512]{3,2,0,1:T(8,128)(2,1)S(1)} %get-tuple-element.13), channel_id=1, source_target_pairs={{0,4},{4,8},{8,12},{12,0},{1,5},{5,9},{9,13},{13,1},{2,6},{6,10},{... | collective-permute-start | bytes 196616 | tf_op jit(solution)/shard_map/ppermute | solution.py:15
  20.3 12.2 %collective-permute-start.26 = (bf16[4,2,8,512]{3,2,0,1:T(8,128)(2,1)S(1)}, bf16[4,2,8,512]{3,2,0,1:T(8,128)(2,1)S(1)}, u32[]{:S(2)}, u32[]{:S(2)}) collective-permute-start(bf16[4,2,8,512]{3,2,0,1:T(8,128)(2,1)S(1)} %get-tuple-element.12), channel_id=1, source_target_pairs={{0,8},{4,12},{8,0},{12,4},{1,9},{5,13},{9,1},{13,5},{2,10},{6,14},... | collective-permute-start | bytes 196616 | tf_op jit(solution)/shard_map/ppermute | solution.py:15
  21.8 10.7 %collective-permute-start.27 = (bf16[4,2,8,512]{3,2,0,1:T(8,128)(2,1)S(1)}, bf16[4,2,8,512]{3,2,0,1:T(8,128)(2,1)S(1)}, u32[]{:S(2)}, u32[]{:S(2)}) collective-permute-start(bf16[4,2,8,512]{3,2,0,1:T(8,128)(2,1)S(1)} %get-tuple-element.11), channel_id=1, source_target_pairs={{0,12},{4,0},{8,4},{12,8},{1,13},{5,1},{9,5},{13,9},{2,14},{6,2},{... | collective-permute-start | bytes 196616 | tf_op jit(solution)/shard_map/ppermute | solution.py:15
  24.4 12.8 %collective-permute-start.6 = (bf16[64,1024]{1,0:T(8,128)(2,1)S(1)}, bf16[64,1024]{1,0:T(8,128)(2,1)S(1)}, u32[]{:S(2)}, u32[]{:S(2)}) collective-permute-start(bf16[64,1024]{1,0:T(8,128)(2,1)S(1)} %bitcast.210), channel_id=1, source_target_pairs={{0,4},{4,8},{8,12},{12,0},{1,5},{5,9},{9,13},{13,1},{2,6},{6,10},{... | collective-permute-start | bytes 393224 | tf_op jit(solution)/shard_map/ppermute | solution.py:15
  28.2 10.6 %collective-permute-start.7 = (bf16[64,1024]{1,0:T(8,128)(2,1)S(1)}, bf16[64,1024]{1,0:T(8,128)(2,1)S(1)}, u32[]{:S(2)}, u32[]{:S(2)}) collective-permute-start(bf16[64,1024]{1,0:T(8,128)(2,1)S(1)} %bitcast.211), channel_id=1, source_target_pairs={{0,8},{4,12},{8,0},{12,4},{1,9},{5,13},{9,1},{13,5},{2,10},{6,14},... | collective-permute-start | bytes 393224 | tf_op jit(solution)/shard_map/ppermute | solution.py:15
  28.4 10.3 %collective-permute-start.8 = (bf16[64,1024]{1,0:T(8,128)(2,1)S(1)}, bf16[64,1024]{1,0:T(8,128)(2,1)S(1)}, u32[]{:S(2)}, u32[]{:S(2)}) collective-permute-start(bf16[64,1024]{1,0:T(8,128)(2,1)S(1)} %bitcast.212), channel_id=1, source_target_pairs={{0,12},{4,0},{8,4},{12,8},{1,13},{5,1},{9,5},{13,9},{2,14},{6,2},{... | collective-permute-start | bytes 393224 | tf_op jit(solution)/shard_map/ppermute | solution.py:15
  32.6 8.0 %collective-permute-start.28 = (bf16[4,2,8,512]{3,2,0,1:T(8,128)(2,1)S(1)}, bf16[4,2,8,512]{3,2,0,1:T(8,128)(2,1)S(1)}, u32[]{:S(2)}, u32[]{:S(2)}) collective-permute-start(bf16[4,2,8,512]{3,2,0,1:T(8,128)(2,1)S(1)} %get-tuple-element.25), channel_id=1, source_target_pairs={{0,1},{1,2},{2,3},{3,0},{4,5},{5,6},{6,7},{7,4},{8,9},{9,10},{10,1... | collective-permute-start | bytes 196616 | tf_op jit(solution)/shard_map/ppermute | solution.py:15
  34.3 6.4 %collective-permute-start.29 = (bf16[4,2,8,512]{3,2,0,1:T(8,128)(2,1)S(1)}, bf16[4,2,8,512]{3,2,0,1:T(8,128)(2,1)S(1)}, u32[]{:S(2)}, u32[]{:S(2)}) collective-permute-start(bf16[4,2,8,512]{3,2,0,1:T(8,128)(2,1)S(1)} %get-tuple-element.24), channel_id=1, source_target_pairs={{0,2},{1,3},{2,0},{3,1},{4,6},{5,7},{6,4},{7,5},{8,10},{9,11},{10,... | collective-permute-start | bytes 196616 | tf_op jit(solution)/shard_map/ppermute | solution.py:15
  37.2 4.3 %collective-permute-start.30 = (bf16[4,2,8,512]{3,2,0,1:T(8,128)(2,1)S(1)}, bf16[4,2,8,512]{3,2,0,1:T(8,128)(2,1)S(1)}, u32[]{:S(2)}, u32[]{:S(2)}) collective-permute-start(bf16[4,2,8,512]{3,2,0,1:T(8,128)(2,1)S(1)} %get-tuple-element.23), channel_id=1, source_target_pairs={{0,3},{1,0},{2,1},{3,2},{4,7},{5,4},{6,5},{7,6},{8,11},{9,8},{10,9... | collective-permute-start | bytes 196616 | tf_op jit(solution)/shard_map/ppermute | solution.py:15
  38.8 15.1 %collective-permute-start.9 = (bf16[4,64,1024]{2,1,0:T(8,128)(2,1)S(1)}, bf16[4,64,1024]{2,1,0:T(8,128)(2,1)S(1)}, u32[]{:S(2)}, u32[]{:S(2)}) collective-permute-start(bf16[4,64,1024]{2,1,0:T(8,128)(2,1)S(1)} %pad_maximum_fusion.1.a0), channel_id=1, source_target_pairs={{0,1},{1,2},{2,3},{3,0},{4,5},{5,6},{6,7},{7,4},{8,9},{9,10},{10,1... | collective-permute-start | bytes 1572872 | tf_op jit(solution)/shard_map/ppermute | solution.py:15
  42.2 16.8 %collective-permute-start.31 = (bf16[4,4,2,8,512]{4,3,1,0,2:T(8,128)(2,1)}, bf16[4,4,2,8,512]{4,3,1,0,2:T(8,128)(2,1)}, u32[]{:S(2)}, u32[]{:S(2)}) collective-permute-start(bf16[4,4,2,8,512]{4,3,1,0,2:T(8,128)(2,1)} %pad_maximum_fusion.8), channel_id=1, source_target_pairs={{0,128},{128,0},{1,129},{129,1},{2,130},{130,2},{3,131},{131,3},{4... | collective-permute-start | bytes 786440 | tf_op jit(solution)/shard_map/ppermute | solution.py:15
  47.0 15.9 %collective-permute-start.11 = (bf16[4,64,1024]{2,1,0:T(8,128)(2,1)S(1)}, bf16[4,64,1024]{2,1,0:T(8,128)(2,1)}, u32[]{:S(2)}, u32[]{:S(2)}) collective-permute-start(bf16[4,64,1024]{2,1,0:T(8,128)(2,1)S(1)} %pad_maximum_fusion.1.a0), channel_id=1, source_target_pairs={{0,3},{1,0},{2,1},{3,2},{4,7},{5,4},{6,5},{7,6},{8,11},{9,8},{10,9... | collective-permute-start | bytes 1572872 | tf_op jit(solution)/shard_map/ppermute | solution.py:15
  54.7 15.6 %collective-permute-start.10 = (bf16[2,64,1024]{2,1,0:T(8,128)(2,1)}, bf16[2,64,1024]{2,1,0:T(8,128)(2,1)}, u32[]{:S(2)}, u32[]{:S(2)}) collective-permute-start(bf16[2,64,1024]{2,1,0:T(8,128)(2,1)} %slice.78), channel_id=1, source_target_pairs={{0,1},{1,2},{2,3},{3,0},{4,5},{5,6},{6,7},{7,4},{8,9},{9,10},{10,1... | collective-permute-start | bytes 786440 | tf_op jit(solution)/shard_map/ppermute | solution.py:15
  63.8 8.6 %copy-start = (f32[1024,1024]{1,0:T(8,128)S(1)}, f32[1024,1024]{1,0:T(8,128)}, u32[]{:S(2)}) copy-start(f32[1024,1024]{1,0:T(8,128)} %kept.3) | copy-start | bytes 12582916
  63.8 7.5 %collective-permute-start.12 = (bf16[2,64,1024]{2,1,0:T(8,128)(2,1)S(1)}, bf16[2,64,1024]{2,1,0:T(8,128)(2,1)S(1)}, u32[]{:S(2)}, u32[]{:S(2)}) collective-permute-start(bf16[2,64,1024]{2,1,0:T(8,128)(2,1)S(1)} %slice.79), channel_id=1, source_target_pairs={{0,3},{1,0},{2,1},{3,2},{4,7},{5,4},{6,5},{7,6},{8,11},{9,8},{10,9... | collective-permute-start | bytes 786440 | tf_op jit(solution)/shard_map/ppermute | solution.py:15
  68.3 11.2 %collective-permute-start.32 = (bf16[4,2,4,2,8,512]{5,4,2,0,3,1:T(8,128)(2,1)}, bf16[4,2,4,2,8,512]{5,4,2,0,3,1:T(8,128)(2,1)}, u32[]{:S(2)}, u32[]{:S(2)}) collective-permute-start(bf16[4,2,4,2,8,512]{5,4,2,0,3,1:T(8,128)(2,1)} %get-tuple-element.9), channel_id=1, source_target_pairs={{0,32},{32,64},{64,96},{96,0},{1,33},{33,65},{65,97},{97,1},{2,34}... | collective-permute-start | bytes 1572872 | tf_op jit(solution)/shard_map/ppermute | solution.py:15
  69.8 12.3 %collective-permute-start.34 = (bf16[4,2,4,2,8,512]{5,4,2,0,3,1:T(8,128)(2,1)}, bf16[4,2,4,2,8,512]{5,4,2,0,3,1:T(8,128)(2,1)}, u32[]{:S(2)}, u32[]{:S(2)}) collective-permute-start(bf16[4,2,4,2,8,512]{5,4,2,0,3,1:T(8,128)(2,1)} %get-tuple-element.9), channel_id=1, source_target_pairs={{0,96},{32,0},{64,32},{96,64},{1,97},{33,1},{65,33},{97,65},{2,98}... | collective-permute-start | bytes 1572872 | tf_op jit(solution)/shard_map/ppermute | solution.py:15
  75.7 46.7 %collective-permute-start.36 = (f32[1024,512]{1,0:T(8,128)}, f32[1024,512]{1,0:T(8,128)}, u32[]{:S(2)}, u32[]{:S(2)}) collective-permute-start(f32[1024,512]{1,0:T(8,128)} %shard_map.39), channel_id=1, source_target_pairs={{0,16},{16,0},{1,17},{17,1},{2,18},{18,2},{3,19},{19,3},{4,20},{20... | collective-permute-start | bytes 6291464 | tf_op jit(solution)/shard_map/ppermute | solution.py:15
  77.6 5.5 %collective-permute-start.13 = (f32[2,4,2,4,8,128]{5,4,1,0,2,3:T(8,128)S(1)}, f32[2,4,2,4,8,128]{5,4,1,0,2,3:T(8,128)S(1)}, u32[]{:S(2)}, u32[]{:S(2)}) collective-permute-start(f32[2,4,2,4,8,128]{5,4,1,0,2,3:T(8,128)S(1)} %bitcast.214), channel_id=1, source_target_pairs={{0,16},{16,0},{1,17},{17,1},{2,18},{18,2},{3,19},{19,3},{4,20},{20... | collective-permute-start | bytes 786440 | tf_op jit(solution)/shard_map/ppermute | solution.py:15
  80.5 20.0 %collective-permute-start.33 = (bf16[2,2,4,2,8,512]{5,4,2,0,3,1:T(8,128)(2,1)S(1)}, bf16[2,2,4,2,8,512]{5,4,2,0,3,1:T(8,128)(2,1)S(1)}, u32[]{:S(2)}, u32[]{:S(2)}) collective-permute-start(bf16[2,2,4,2,8,512]{5,4,2,0,3,1:T(8,128)(2,1)S(1)} %slice.86), channel_id=1, source_target_pairs={{0,32},{32,64},{64,96},{96,0},{1,33},{33,65},{65,97},{97,1},{2,34}... | collective-permute-start | bytes 786440 | tf_op jit(solution)/shard_map/ppermute | solution.py:15
  83.1 11.8 %collective-permute-start.14 = (f32[2,4,2,8,128]{4,3,1,0,2:T(8,128)S(1)}, f32[2,4,2,8,128]{4,3,1,0,2:T(8,128)S(1)}, u32[]{:S(2)}, u32[]{:S(2)}) collective-permute-start(f32[2,4,2,8,128]{4,3,1,0,2:T(8,128)S(1)} %get-tuple-element.28), channel_id=1, source_target_pairs={{0,32},{32,64},{64,96},{96,0},{1,33},{33,65},{65,97},{97,1},{2,34}... | collective-permute-start | bytes 196616 | tf_op jit(solution)/shard_map/ppermute | solution.py:15
  85.2 10.3 %collective-permute-start.15 = (f32[2,4,2,8,128]{4,3,1,0,2:T(8,128)S(1)}, f32[2,4,2,8,128]{4,3,1,0,2:T(8,128)S(1)}, u32[]{:S(2)}, u32[]{:S(2)}) collective-permute-start(f32[2,4,2,8,128]{4,3,1,0,2:T(8,128)S(1)} %get-tuple-element.26), channel_id=1, source_target_pairs={{0,64},{32,96},{64,0},{96,32},{1,65},{33,97},{65,1},{97,33},{2,66}... | collective-permute-start | bytes 196616 | tf_op jit(solution)/shard_map/ppermute | solution.py:15
  86.8 8.7 %collective-permute-start.16 = (f32[2,4,2,8,128]{4,3,1,0,2:T(8,128)S(1)}, f32[2,4,2,8,128]{4,3,1,0,2:T(8,128)S(1)}, u32[]{:S(2)}, u32[]{:S(2)}) collective-permute-start(f32[2,4,2,8,128]{4,3,1,0,2:T(8,128)S(1)} %get-tuple-element.27), channel_id=1, source_target_pairs={{0,96},{32,0},{64,32},{96,64},{1,97},{33,1},{65,33},{97,65},{2,98}... | collective-permute-start | bytes 196616 | tf_op jit(solution)/shard_map/ppermute | solution.py:15
  89.3 2.2 %copy-start.1 = (f32[1024,1024]{1,0:T(8,128)S(1)}, f32[1024,1024]{1,0:T(8,128)}, u32[]{:S(2)}) copy-start(f32[1024,1024]{1,0:T(8,128)} %kept.3) | copy-start | bytes 12582916
  91.5 20.1 %copy-start.5 = (bf16[1,4,2,4,2,8,512]{6,5,3,1,4,2,0:T(8,128)(2,1)S(1)}, bf16[1,4,2,4,2,8,512]{6,5,3,1,4,2,0:T(8,128)(2,1)}, u32[]{:S(2)}) copy-start(bf16[1,4,2,4,2,8,512]{6,5,3,1,4,2,0:T(8,128)(2,1)} %get-tuple-element.8) | copy-start | bytes 1572868
  93.6 1.4 copy-start.2
  95.0 6.7 %collective-permute-start.35 = (bf16[2,2,4,2,8,512]{5,4,2,0,3,1:T(8,128)(2,1)S(1)}, bf16[2,2,4,2,8,512]{5,4,2,0,3,1:T(8,128)(2,1)S(1)}, u32[]{:S(2)}, u32[]{:S(2)}) collective-permute-start(bf16[2,2,4,2,8,512]{5,4,2,0,3,1:T(8,128)(2,1)S(1)} %slice.87), channel_id=1, source_target_pairs={{0,96},{32,0},{64,32},{96,64},{1,97},{33,1},{65,33},{97,65},{2,98}... | collective-permute-start | bytes 786440 | tf_op jit(solution)/shard_map/ppermute | solution.py:15
  95.5 8.2 %collective-permute-start.17 = (f32[2,4,8,128]{3,2,1,0:T(8,128)S(1)}, f32[2,4,8,128]{3,2,1,0:T(8,128)S(1)}, u32[]{:S(2)}, u32[]{:S(2)}) collective-permute-start(f32[2,4,8,128]{3,2,1,0:T(8,128)S(1)} %slice_bitcast_fusion.9), channel_id=1, source_target_pairs={{0,128},{128,0},{1,129},{129,1},{2,130},{130,2},{3,131},{131,3},{4... | collective-permute-start | bytes 98312 | tf_op jit(solution)/shard_map/ppermute | solution.py:15
  103.8 14.0 %collective-permute-start.18 = (f32[2,4,8,128]{3,2,1,0:T(8,128)S(1)}, f32[2,4,8,128]{3,2,1,0:T(8,128)S(1)}, u32[]{:S(2)}, u32[]{:S(2)}) collective-permute-start(f32[2,4,8,128]{3,2,1,0:T(8,128)S(1)} %fusion.23), channel_id=1, source_target_pairs={{0,4},{4,8},{8,12},{12,0},{1,5},{5,9},{9,13},{13,1},{2,6},{6,10},{... | collective-permute-start | bytes 98312 | tf_op jit(solution)/shard_map/ppermute | solution.py:15
  109.2 8.6 %collective-permute-start.19 = (f32[2,4,8,128]{3,2,1,0:T(8,128)S(1)}, f32[2,4,8,128]{3,2,1,0:T(8,128)S(1)}, u32[]{:S(2)}, u32[]{:S(2)}) collective-permute-start(f32[2,4,8,128]{3,2,1,0:T(8,128)S(1)} %fusion.23), channel_id=1, source_target_pairs={{0,8},{4,12},{8,0},{12,4},{1,9},{5,13},{9,1},{13,5},{2,10},{6,14},... | collective-permute-start | bytes 98312 | tf_op jit(solution)/shard_map/ppermute | solution.py:15
  109.2 8.6 %collective-permute-start.20 = (f32[2,4,8,128]{3,2,1,0:T(8,128)S(1)}, f32[2,4,8,128]{3,2,1,0:T(8,128)S(1)}, u32[]{:S(2)}, u32[]{:S(2)}) collective-permute-start(f32[2,4,8,128]{3,2,1,0:T(8,128)S(1)} %fusion.23), channel_id=1, source_target_pairs={{0,12},{4,0},{8,4},{12,8},{1,13},{5,1},{9,5},{13,9},{2,14},{6,2},{... | collective-permute-start | bytes 98312 | tf_op jit(solution)/shard_map/ppermute | solution.py:15
  114.4 8.0 %copy-start.3 = (f32[1024,512]{1,0:T(8,128)S(1)}, f32[1024,512]{1,0:T(8,128)}, u32[]{:S(2)}) copy-start(f32[1024,512]{1,0:T(8,128)} %copy-done.2) | copy-start | bytes 6291460
  117.8 8.7 %collective-permute-start.21 = (f32[4,2,4,8,128]{4,3,2,1,0:T(8,128)S(1)}, f32[4,2,4,8,128]{4,3,2,1,0:T(8,128)S(1)}, u32[]{:S(2)}, u32[]{:S(2)}) collective-permute-start(f32[4,2,4,8,128]{4,3,2,1,0:T(8,128)S(1)} %get-tuple-element.34), channel_id=1, source_target_pairs={{0,1},{1,2},{2,3},{3,0},{4,5},{5,6},{6,7},{7,4},{8,9},{9,10},{10,1... | collective-permute-start | bytes 393224 | tf_op jit(solution)/shard_map/ppermute | solution.py:15
  117.9 9.7 %collective-permute-start.22 = (f32[4,2,4,8,128]{4,3,2,1,0:T(8,128)S(1)}, f32[4,2,4,8,128]{4,3,2,1,0:T(8,128)S(1)}, u32[]{:S(2)}, u32[]{:S(2)}) collective-permute-start(f32[4,2,4,8,128]{4,3,2,1,0:T(8,128)S(1)} %get-tuple-element.34), channel_id=1, source_target_pairs={{0,2},{1,3},{2,0},{3,1},{4,6},{5,7},{6,4},{7,5},{8,10},{9,11},{10,... | collective-permute-start | bytes 393224 | tf_op jit(solution)/shard_map/ppermute | solution.py:15
  120.4 7.3 %collective-permute-start.23 = (f32[4,2,4,8,128]{4,3,2,1,0:T(8,128)S(1)}, f32[4,2,4,8,128]{4,3,2,1,0:T(8,128)S(1)}, u32[]{:S(2)}, u32[]{:S(2)}) collective-permute-start(f32[4,2,4,8,128]{4,3,2,1,0:T(8,128)S(1)} %get-tuple-element.34), channel_id=1, source_target_pairs={{0,3},{1,0},{2,1},{3,2},{4,7},{5,4},{6,5},{7,6},{8,11},{9,8},{10,9... | collective-permute-start | bytes 393224 | tf_op jit(solution)/shard_map/ppermute | solution.py:15
  124.5 3.4 %copy-start.4 = (bf16[4,4,2,4,2,8,512]{6,5,3,1,4,2,0:T(8,128)(2,1)S(1)}, bf16[4,4,2,4,2,8,512]{6,5,3,1,4,2,0:T(8,128)(2,1)}, u32[]{:S(2)}) copy-start(bf16[4,4,2,4,2,8,512]{6,5,3,1,4,2,0:T(8,128)(2,1)} %rev.31) | copy-start | bytes 6291460
  124.6 6.4 %collective-permute-start.37 = (bf16[16,2,8,512]{3,2,0,1:T(8,128)(2,1)S(1)}, bf16[16,2,8,512]{3,2,0,1:T(8,128)(2,1)S(1)}, u32[]{:S(2)}, u32[]{:S(2)}) collective-permute-start(bf16[16,2,8,512]{3,2,0,1:T(8,128)(2,1)S(1)} %get-tuple-element.5), channel_id=1, source_target_pairs={{0,32},{32,64},{64,96},{96,0},{1,33},{33,65},{65,97},{97,1},{2,34}... | collective-permute-start | bytes 786440 | tf_op jit(solution)/shard_map/ppermute | solution.py:15
  125.5 8.0 %collective-permute-start.38 = (bf16[16,2,8,512]{3,2,0,1:T(8,128)(2,1)S(1)}, bf16[16,2,8,512]{3,2,0,1:T(8,128)(2,1)S(1)}, u32[]{:S(2)}, u32[]{:S(2)}) collective-permute-start(bf16[16,2,8,512]{3,2,0,1:T(8,128)(2,1)S(1)} %get-tuple-element.7), channel_id=1, source_target_pairs={{0,64},{32,96},{64,0},{96,32},{1,65},{33,97},{65,1},{97,33},{2,66}... | collective-permute-start | bytes 786440 | tf_op jit(solution)/shard_map/ppermute | solution.py:15
  126.5 9.2 %collective-permute-start.39 = (bf16[16,2,8,512]{3,2,0,1:T(8,128)(2,1)S(1)}, bf16[16,2,8,512]{3,2,0,1:T(8,128)(2,1)S(1)}, u32[]{:S(2)}, u32[]{:S(2)}) collective-permute-start(bf16[16,2,8,512]{3,2,0,1:T(8,128)(2,1)S(1)} %get-tuple-element.6), channel_id=1, source_target_pairs={{0,96},{32,0},{64,32},{96,64},{1,97},{33,1},{65,33},{97,65},{2,98}... | collective-permute-start | bytes 786440 | tf_op jit(solution)/shard_map/ppermute | solution.py:15
  127.8 9.1 %collective-permute-start.24 = (f32[4,4,2,4,8,128]{5,4,3,2,1,0:T(8,128)S(1)}, f32[4,4,2,4,8,128]{5,4,3,2,1,0:T(8,128)S(1)}, u32[]{:S(2)}, u32[]{:S(2)}) collective-permute-start(f32[4,4,2,4,8,128]{5,4,3,2,1,0:T(8,128)S(1)} %get-tuple-element.15), channel_id=1, source_target_pairs={{0,16},{16,0},{1,17},{17,1},{2,18},{18,2},{3,19},{19,3},{4,20},{20... | collective-permute-start | bytes 1572872 | tf_op jit(solution)/shard_map/ppermute | solution.py:15
  135.9 9.1 %collective-permute-start.40 = (bf16[16,8,512]{2,1,0:T(8,128)(2,1)S(1)}, bf16[16,8,512]{2,1,0:T(8,128)(2,1)S(1)}, u32[]{:S(2)}, u32[]{:S(2)}) collective-permute-start(bf16[16,8,512]{2,1,0:T(8,128)(2,1)S(1)} %fusion.11), channel_id=1, source_target_pairs={{0,128},{128,0},{1,129},{129,1},{2,130},{130,2},{3,131},{131,3},{4... | collective-permute-start | bytes 393224 | tf_op jit(solution)/shard_map/ppermute | solution.py:15
  162.2 1.3 collective-permute-start.41

commit v3 on v2

--- a/solution.py
+++ b/solution.py
@@ -61,7 +61,7 @@
     out[...] = dot(x_ref[...], tile[...], ((1,), (0,)))
 
 
-def mix_kernel(pairs, panel, tiles, mine, out, total):
+def mix_kernel(core, mine_pairs, twin_pairs, panel, near, far, mine, out, total):
     n = panel.shape[0]
     total[...] = jnp.zeros_like(total)
 
@@ -71,14 +71,17 @@
         rows = []
         for i in range(n):
             src = (i + n - dy) % n
-            rows += [pairs[src // 2, dy, dz, src % 2, (j + n - dz) % n] for j in range(n)]
+            held = src // 2 == core[0]
+            for j in range(n):
+                at = (dy, dz, src % 2, (j + n - dz) % n)
+                rows.append(jnp.where(held, mine_pairs[at], twin_pairs[at]))
         value = jnp.concatenate(rows)
         high = value.astype(BF16)
         low = (value - high.astype(F32)).astype(BF16)
         right = panel[dy, dz]
         total[...] += dot(jnp.concatenate([high, low], 1), jnp.concatenate([right, right]), ((1,), (0,)))
 
-    out[...] = (mine[...].astype(F32) - (0.5 * total[...] + tiles[...])).astype(BF16)
+    out[...] = (mine[...].astype(F32) - (0.5 * total[...] + (near[...] + far[...].astype(F32)))).astype(BF16)
 
 
 def flat(value):
@@ -124,6 +127,7 @@
     mine = part_c[:, :, 0].reshape(16 * rows, hw)
     parts = gather(part_c, "zh")
     part_c = absolute(jnp.stack(parts), zh, 2, 0).transpose(1, 0, 2, 3, 4, 5)
+    part_c = lax.optimization_barrier(part_c)
     c0, c1, c2, c2b, c3 = gather_ring(part_c, "x")
     panel = absolute(jnp.stack([c0, c1, jnp.concatenate([c2, c2b]), c3]), x, 4, 0)
     panel = panel.transpose(1, 3, 4, 2, 0, 5, 6).reshape(4, 4, 16 * rows, hw)
@@ -137,7 +141,6 @@
     pairs = jnp.stack(gather(pairs, "zl"))
     pairs = jnp.stack(gather(pairs, "y"))
     twin = shift(pairs, "core", 1)
-    pairs = jnp.where(core == 0, jnp.stack([pairs, twin]), jnp.stack([twin, pairs]))
 
     x_r = jnp.concatenate([flat(p) for p in pieces])
 
@@ -165,10 +168,13 @@
     sent = [total[:, :, 4 - d].astype(BF16) for d in range(1, 4)]
     got = [shift(v, "x", d) for d, v in enumerate(sent, 1)]
     total = total[:, :, 0] + sum(g.astype(F32) for g in got)
-    total = total[:, 0] + shift(total[:, 1].astype(BF16), "zh", 1).astype(F32)
+    sent = total[:, 1].astype(BF16)
+    got = shift(sent, "zh", 1)
 
-    args = (pairs, panel, total.reshape(16 * rows, hw), mine)
-    result = call(mix_kernel, mine.shape, 8 * 16 * rows * 128 * rows * hw, args, [VMEM_SPEC] * 4, [pltpu.VMEM(mine.shape, F32)], BF16)
+    args = (core[None], pairs, twin, panel, flat(total[:, 0]), flat(got), mine)
+    specs = [pl.BlockSpec(memory_space=pltpu.SMEM)] + [VMEM_SPEC] * 6
+    flops = 8 * 16 * rows * 128 * rows * hw
+    result = call(mix_kernel, mine.shape, flops, args, specs, [pltpu.VMEM(mine.shape, F32)], BF16)
     result = result.reshape(4, 4, rows, hw)
     back = absolute(absolute(result, y, 4, 0), zl, 4, 1)
     result = lax.all_to_all(

time: 166 us -> 165 us (level)
    another operation x3 -> x2, other arithmetic: 5.42 us -> 3.04 us  [body(): jnp.stack([c0, c1, jnp.concatenate([c2, c2b]), c3])]
    transpose x0 -> x1, other arithmetic: none -> 2.02 us  [body(): part_c = absolute(jnp.stack(parts), zh, 2, 0).transpose(1, 0, 2, 3, 4, 5)]
    unnamed x22 -> x20, local copies, waits for them, and re-layouts: 4.66 us -> 4.65 us
where the time goes in v3:
time: 165 us; the launch traced here: 164 us
  starting transfers between devices  72.9 us (44%)
  waiting for transfers between devices  35.4 us (21%)
  local copies, waits for them, and re-layouts  17.2 us (10%)
  other arithmetic  14.5 us (9%)
  blocking collectives  13.5 us (8%)
  Pallas kernels  10.4 us (6%)
    ppermute x42, starting transfers between devices, shift(): return lax.ppermute(value, axis, [(i, (i + step) % n) for i in range(n)])  72.9 us
    ppermute x42, waiting for transfers between devices, shift(): return lax.ppermute(value, axis, [(i, (i + step) % n) for i in range(n)])  35.4 us
    all_to_all x1, blocking collectives, body(): lax.all_to_all(back.transpose(1, 0, 2, 3).reshape(16, rows, hw), ('zl', '...  13.5 us
    pallas_call x2, Pallas kernels, product(): pl.pallas_call(tile_kernel, out_shape=jax.ShapeDtypeStruct((4 * step, hw)...  5.26 us
    rev x6, local copies, waits for them, and re-layouts, absolute(): turned = jnp.flip(pieces, dim)  5.26 us
    pallas_call x2, Pallas kernels, call(): pl.pallas_call(kernel, out_shape=jax.ShapeDtypeStruct(shape, kind), in_sp...  5.12 us
    unnamed x20, local copies, waits for them, and re-layouts  4.65 us
  transfers between devices with their start and end apart: 42, of which 17 were waited for; matrix products, arithmetic and copies ran while one was open for 16% of the time, Pallas kernels for 4%

profile of v3, /device:TPU:2, one launch (start us, length us, event | category | flops | bytes accessed | tf_op | source)
XLA Modules:
  0.0 164.2 jit_solution(11662857205240254333)
XLA Ops:
  0.5 1.0 collective-permute-done
  1.6 1.2 maximum_select_fusion
  2.8 1.2 maximum_select_fusion.1
  4.1 1.6 collective-permute-start.2
  5.7 2.8 %collective-permute-start.3 = (bf16[2,2,8,1024]{3,2,0,1:T(8,128)(2,1)S(1)}, bf16[2,2,8,1024]{3,2,0,1:T(8,128)(2,1)S(1)}, u32[]{:S(2)}, u32[]{:S(2)}) collective-permute-start(bf16[2,2,8,1024]{3,2,0,1:T(8,128)(2,1)S(1)} %get-tuple-element.17), channel_id=1, source_target_pairs={{0,64},{32,96},{64,0},{96,32},{1,65},{33,97},{65,1},{97,33},{2,66}... | collective-permute-start | bytes 196616 | tf_op jit(solution)/shard_map/ppermute | solution.py:15
  9.4 2.4 %collective-permute-done.3 = bf16[2,2,8,1024]{3,2,0,1:T(8,128)(2,1)S(1)} collective-permute-done((bf16[2,2,8,1024]{3,2,0,1:T(8,128)(2,1)S(1)}, bf16[2,2,8,1024]{3,2,0,1:T(8,128)(2,1)S(1)}, u32[]{:S(2)}, u32[]{:S(2)}) %collective-permute-start.3) | collective-permute-done | bytes 65568 | tf_op jit(solution)/shard_map/ppermute | solution.py:15
  11.8 0.9 collective-permute-done.4
  12.8 6.3 %collective-permute-start.5 = (bf16[4,2,8,1024]{3,2,0,1:T(8,128)(2,1)S(1)}, bf16[4,2,8,1024]{3,2,0,1:T(8,128)(2,1)S(1)}, u32[]{:S(2)}, u32[]{:S(2)}) collective-permute-start(bf16[4,2,8,1024]{3,2,0,1:T(8,128)(2,1)S(1)} %get-tuple-element.25), channel_id=1, source_target_pairs={{0,128},{128,0},{1,129},{129,1},{2,130},{130,2},{3,131},{131,3},{4... | collective-permute-start | bytes 393224 | tf_op jit(solution)/shard_map/ppermute | solution.py:15
  19.2 1.1 collective-permute-start.25
  20.3 1.5 collective-permute-start.26
  21.8 1.9 %collective-permute-start.27 = (bf16[4,2,8,512]{3,2,0,1:T(8,128)(2,1)S(1)}, bf16[4,2,8,512]{3,2,0,1:T(8,128)(2,1)S(1)}, u32[]{:S(2)}, u32[]{:S(2)}) collective-permute-start(bf16[4,2,8,512]{3,2,0,1:T(8,128)(2,1)S(1)} %get-tuple-element.9), channel_id=1, source_target_pairs={{0,12},{4,0},{8,4},{12,8},{1,13},{5,1},{9,5},{13,9},{2,14},{6,2},{... | collective-permute-start | bytes 196616 | tf_op jit(solution)/shard_map/ppermute | solution.py:15
  24.4 3.8 %collective-permute-start.6 = (bf16[64,1024]{1,0:T(8,128)(2,1)S(1)}, bf16[64,1024]{1,0:T(8,128)(2,1)S(1)}, u32[]{:S(2)}, u32[]{:S(2)}) collective-permute-start(bf16[64,1024]{1,0:T(8,128)(2,1)S(1)} %bitcast.200), channel_id=1, source_target_pairs={{0,4},{4,8},{8,12},{12,0},{1,5},{5,9},{9,13},{13,1},{2,6},{6,10},{... | collective-permute-start | bytes 393224 | tf_op jit(solution)/shard_map/ppermute | solution.py:15
  28.4 2.4 %collective-permute-start.8 = (bf16[64,1024]{1,0:T(8,128)(2,1)S(1)}, bf16[64,1024]{1,0:T(8,128)(2,1)S(1)}, u32[]{:S(2)}, u32[]{:S(2)}) collective-permute-start(bf16[64,1024]{1,0:T(8,128)(2,1)S(1)} %bitcast.202), channel_id=1, source_target_pairs={{0,12},{4,0},{8,4},{12,8},{1,13},{5,1},{9,5},{13,9},{2,14},{6,2},{... | collective-permute-start | bytes 393224 | tf_op jit(solution)/shard_map/ppermute | solution.py:15
  30.8 1.7 %collective-permute-done.26 = bf16[4,2,8,512]{3,2,0,1:T(8,128)(2,1)S(1)} collective-permute-done((bf16[4,2,8,512]{3,2,0,1:T(8,128)(2,1)S(1)}, bf16[4,2,8,512]{3,2,0,1:T(8,128)(2,1)S(1)}, u32[]{:S(2)}, u32[]{:S(2)}) %collective-permute-start.26) | collective-permute-done | bytes 65568 | tf_op jit(solution)/shard_map/ppermute | solution.py:15
  32.6 1.7 %collective-permute-start.28 = (bf16[4,2,8,512]{3,2,0,1:T(8,128)(2,1)S(1)}, bf16[4,2,8,512]{3,2,0,1:T(8,128)(2,1)S(1)}, u32[]{:S(2)}, u32[]{:S(2)}) collective-permute-start(bf16[4,2,8,512]{3,2,0,1:T(8,128)(2,1)S(1)} %get-tuple-element.21), channel_id=1, source_target_pairs={{0,1},{1,2},{2,3},{3,0},{4,5},{5,6},{6,7},{7,4},{8,9},{9,10},{10,1... | collective-permute-start | bytes 196616 | tf_op jit(solution)/shard_map/ppermute | solution.py:15
  34.3 2.9 %collective-permute-start.29 = (bf16[4,2,8,512]{3,2,0,1:T(8,128)(2,1)S(1)}, bf16[4,2,8,512]{3,2,0,1:T(8,128)(2,1)S(1)}, u32[]{:S(2)}, u32[]{:S(2)}) collective-permute-start(bf16[4,2,8,512]{3,2,0,1:T(8,128)(2,1)S(1)} %get-tuple-element.20), channel_id=1, source_target_pairs={{0,2},{1,3},{2,0},{3,1},{4,6},{5,7},{6,4},{7,5},{8,10},{9,11},{10,... | collective-permute-start | bytes 196616 | tf_op jit(solution)/shard_map/ppermute | solution.py:15
  37.2 1.3 collective-permute-start.30
  38.8 1.8 %collective-permute-start.9 = (bf16[4,64,1024]{2,1,0:T(8,128)(2,1)S(1)}, bf16[4,64,1024]{2,1,0:T(8,128)(2,1)S(1)}, u32[]{:S(2)}, u32[]{:S(2)}) collective-permute-start(bf16[4,64,1024]{2,1,0:T(8,128)(2,1)S(1)} %pad_maximum_fusion.1.a0), channel_id=1, source_target_pairs={{0,1},{1,2},{2,3},{3,0},{4,5},{5,6},{6,7},{7,4},{8,9},{9,10},{10,1... | collective-permute-start | bytes 1572872 | tf_op jit(solution)/shard_map/ppermute | solution.py:15
  40.7 0.8 collective-permute-done.30
  42.2 4.8 %collective-permute-start.31 = (bf16[4,4,2,8,512]{4,3,1,0,2:T(8,128)(2,1)}, bf16[4,4,2,8,512]{4,3,1,0,2:T(8,128)(2,1)}, u32[]{:S(2)}, u32[]{:S(2)}) collective-permute-start(bf16[4,4,2,8,512]{4,3,1,0,2:T(8,128)(2,1)} %pad_maximum_fusion.8), channel_id=1, source_target_pairs={{0,128},{128,0},{1,129},{129,1},{2,130},{130,2},{3,131},{131,3},{4... | collective-permute-start | bytes 786440 | tf_op jit(solution)/shard_map/ppermute | solution.py:15
  47.0 2.6 %collective-permute-start.11 = (bf16[4,64,1024]{2,1,0:T(8,128)(2,1)S(1)}, bf16[4,64,1024]{2,1,0:T(8,128)(2,1)}, u32[]{:S(2)}, u32[]{:S(2)}) collective-permute-start(bf16[4,64,1024]{2,1,0:T(8,128)(2,1)S(1)} %pad_maximum_fusion.1.a0), channel_id=1, source_target_pairs={{0,3},{1,0},{2,1},{3,2},{4,7},{5,4},{6,5},{7,6},{8,11},{9,8},{10,9... | collective-permute-start | bytes 1572872 | tf_op jit(solution)/shard_map/ppermute | solution.py:15
  49.9 4.0 %collective-permute-done.9.a1 = bf16[4,64,1024]{2,1,0:T(8,128)(2,1)S(1)} collective-permute-done((bf16[4,64,1024]{2,1,0:T(8,128)(2,1)S(1)}, bf16[4,64,1024]{2,1,0:T(8,128)(2,1)S(1)}, u32[]{:S(2)}, u32[]{:S(2)}) %collective-permute-start.9) | collective-permute-done | bytes 524320 | tf_op jit(solution)/shard_map/ppermute | solution.py:15
  55.0 4.0 %collective-permute-done.31 = bf16[4,4,2,8,512]{4,3,1,0,2:T(8,128)(2,1)} collective-permute-done((bf16[4,4,2,8,512]{4,3,1,0,2:T(8,128)(2,1)}, bf16[4,4,2,8,512]{4,3,1,0,2:T(8,128)(2,1)}, u32[]{:S(2)}, u32[]{:S(2)}) %collective-permute-start.31) | collective-permute-done | bytes 262176 | tf_op jit(solution)/shard_map/ppermute | solution.py:15
  59.0 1.9 %pad_maximum_fusion.4 = bf16[2,4,4,2,8,512]{5,4,2,1,3,0:T(8,128)(2,1)} fusion(bf16[1,4,4,2,8,512]{5,4,2,1,3,0:T(8,128)(2,1)} %bitcast.79, bf16[1,4,4,2,8,512]{5,4,2,1,3,0:T(8,128)(2,1)} %bitcast.78), kind=kLoop, calls=%fused_computation.26 | loop fusion | flops 262144 | bytes 1048576 | tf_op jit(solution)/shard_map/stack | solution.py:129
  60.9 1.9 %rev.30 = bf16[2,4,4,2,8,512]{5,4,2,1,3,0:T(8,128)(2,1)} reverse(bf16[2,4,4,2,8,512]{5,4,2,1,3,0:T(8,128)(2,1)} %pad_maximum_fusion.4), dimensions={0} | reverse | bytes 1048576 | tf_op jit(solution)/shard_map/jit(_flip)/rev | solution.py:40
  62.8 1.0 slice.79
  63.8 1.9 %collective-permute-start.12 = (bf16[2,64,1024]{2,1,0:T(8,128)(2,1)S(1)}, bf16[2,64,1024]{2,1,0:T(8,128)(2,1)S(1)}, u32[]{:S(2)}, u32[]{:S(2)}) collective-permute-start(bf16[2,64,1024]{2,1,0:T(8,128)(2,1)S(1)} %slice.79), channel_id=1, source_target_pairs={{0,3},{1,0},{2,1},{3,2},{4,7},{5,4},{6,5},{7,6},{8,11},{9,8},{10,9... | collective-permute-start | bytes 786440 | tf_op jit(solution)/shard_map/ppermute | solution.py:15
  65.6 2.0 %fusion.3 = bf16[4,2,4,2,8,512]{5,4,2,0,3,1:T(8,128)(2,1)} fusion(s32[]{:T(128)S(6)} %select_n.227, bf16[2,4,4,2,8,512]{5,4,2,1,3,0:T(8,128)(2,1)} %rev.30), kind=kLoop, calls=%fused_computation.16 | loop fusion | flops 262144 | bytes 1048580 | tf_op jit(solution)/shard_map/transpose | solution.py:129
  67.7 1.5 collective-permute-start.32
  69.7 1.0 constant_dynamic-update-slice_fusion.2
  70.8 1.1 constant_dynamic-update-slice_fusion.x_ref
  71.8 3.2 %shard_map.39 = f32[1024,512]{1,0:T(8,128)} custom-call(s32[1]{0:T(128)} %bitcast.92.which, bf16[1024,1024]{1,0:T(8,128)(2,1)S(1)} %constant_dynamic-update-slice_fusion.x_ref, f32[1024,1024]{1,0:T(8,128)S(1)} %copy-done), custom_call_target="tpu_custom_call" | custom-call | flops 1073741824 | bytes 3145728 | tf_op jit(solution)/shard_map/pallas_call | solution.py:156
  75.1 1.8 %shard_map.37 = f32[4,4,64,128]{3,2,1,0:T(8,128)S(1)} custom-call(bf16[4,64,1024]{2,1,0:T(8,128)(2,1)S(1)} %pad_maximum_fusion.1.a0, bf16[4,64,1024]{2,1,0:T(8,128)(2,1)S(1)} %collective-permute-done.9.a1, bf16[2,64,1024]{2,1,0:T(8,128)(2,1)} %collective-permute-done.10.a2, bf16[2,64,1024]{2,1,0:T(8,128)(2,1)S(1)} %collective-permute-done.12.a2b, ...), custom_call_target="tpu_custom_call" | custom-call | flops 268435456 | bytes 2359296 | tf_op jit(solution)/shard_map/pallas_call | solution.py:96
  77.6 0.9 slice.94
  78.9 1.0 slice.86
  79.9 1.6 collective-permute-start.33
  81.5 1.0 slice.87
  82.5 2.0 %collective-permute-start.14 = (f32[2,4,2,8,128]{4,3,1,0,2:T(8,128)S(1)}, f32[2,4,2,8,128]{4,3,1,0,2:T(8,128)S(1)}, u32[]{:S(2)}, u32[]{:S(2)}) collective-permute-start(f32[2,4,2,8,128]{4,3,1,0,2:T(8,128)S(1)} %get-tuple-element.24), channel_id=1, source_target_pairs={{0,32},{32,64},{64,96},{96,0},{1,33},{33,65},{65,97},{97,1},{2,34}... | collective-permute-start | bytes 196616 | tf_op jit(solution)/shard_map/ppermute | solution.py:15
  84.6 1.6 collective-permute-start.15
  86.2 2.5 %collective-permute-start.16 = (f32[2,4,2,8,128]{4,3,1,0,2:T(8,128)S(1)}, f32[2,4,2,8,128]{4,3,1,0,2:T(8,128)S(1)}, u32[]{:S(2)}, u32[]{:S(2)}) collective-permute-start(f32[2,4,2,8,128]{4,3,1,0,2:T(8,128)S(1)} %get-tuple-element.23), channel_id=1, source_target_pairs={{0,96},{32,0},{64,32},{96,64},{1,97},{33,1},{65,33},{97,65},{2,98}... | collective-permute-start | bytes 196616 | tf_op jit(solution)/shard_map/ppermute | solution.py:15
  88.7 2.2 %copy-done.1 = f32[1024,1024]{1,0:T(8,128)S(1)} copy-done((f32[1024,1024]{1,0:T(8,128)S(1)}, f32[1024,1024]{1,0:T(8,128)}, u32[]{:S(2)}) %copy-start.1) | copy-done | bytes 4194328
  90.9 2.0 %shard_map.38 = f32[1024,512]{1,0:T(8,128)S(1)} custom-call(s32[1]{0:T(128)} %bitcast.which.core, bf16[1024,1024]{1,0:T(8,128)(2,1)S(1)} %constant_dynamic-update-slice_fusion.x_ref, f32[1024,1024]{1,0:T(8,128)S(1)} %copy-done.1), custom_call_target="tpu_custom_call" | custom-call | flops 1073741824 | bytes 3145728 | tf_op jit(solution)/shard_map/pallas_call | solution.py:156
  93.0 1.3 copy-done.2
  94.9 4.9 %collective-permute-start.17 = (f32[2,4,8,128]{3,2,1,0:T(8,128)S(1)}, f32[2,4,8,128]{3,2,1,0:T(8,128)S(1)}, u32[]{:S(2)}, u32[]{:S(2)}) collective-permute-start(f32[2,4,8,128]{3,2,1,0:T(8,128)S(1)} %slice_bitcast_fusion.9), channel_id=1, source_target_pairs={{0,128},{128,0},{1,129},{129,1},{2,130},{130,2},{3,131},{131,3},{4... | collective-permute-start | bytes 98312 | tf_op jit(solution)/shard_map/ppermute | solution.py:15
  99.9 1.1 collective-permute-done.35
  101.1 2.1 %collective-permute-done.17 = f32[2,4,8,128]{3,2,1,0:T(8,128)S(1)} collective-permute-done((f32[2,4,8,128]{3,2,1,0:T(8,128)S(1)}, f32[2,4,8,128]{3,2,1,0:T(8,128)S(1)}, u32[]{:S(2)}, u32[]{:S(2)}) %collective-permute-start.17) | collective-permute-done | bytes 32800 | tf_op jit(solution)/shard_map/ppermute | solution.py:15
  103.2 5.4 %collective-permute-start.18 = (f32[2,4,8,128]{3,2,1,0:T(8,128)S(1)}, f32[2,4,8,128]{3,2,1,0:T(8,128)S(1)}, u32[]{:S(2)}, u32[]{:S(2)}) collective-permute-start(f32[2,4,8,128]{3,2,1,0:T(8,128)S(1)} %fusion.22), channel_id=1, source_target_pairs={{0,4},{4,8},{8,12},{12,0},{1,5},{5,9},{9,13},{13,1},{2,6},{6,10},{... | collective-permute-start | bytes 98312 | tf_op jit(solution)/shard_map/ppermute | solution.py:15
  108.6 2.5 %collective-permute-start.20 = (f32[2,4,8,128]{3,2,1,0:T(8,128)S(1)}, f32[2,4,8,128]{3,2,1,0:T(8,128)S(1)}, u32[]{:S(2)}, u32[]{:S(2)}) collective-permute-start(f32[2,4,8,128]{3,2,1,0:T(8,128)S(1)} %fusion.22), channel_id=1, source_target_pairs={{0,12},{4,0},{8,4},{12,8},{1,13},{5,1},{9,5},{13,9},{2,14},{6,2},{... | collective-permute-start | bytes 98312 | tf_op jit(solution)/shard_map/ppermute | solution.py:15
  111.1 3.0 %pad_maximum_fusion = bf16[4,4,2,4,2,8,512]{6,5,3,1,4,2,0:T(8,128)(2,1)} fusion(bf16[1,4,2,4,2,8,512]{6,5,3,1,4,2,0:T(8,128)(2,1)} %bitcast.84, bf16[1,4,2,4,2,8,512]{6,5,3,1,4,2,0:T(8,128)(2,1)S(1)} %maximum_bitcast_fusion, bf16[1,4,2,4,2,8,512]{6,5,3,1,4,2,0:T(8,128)(2,1)} %bitcast.82, bf16[1,4,2,4,2,8,512]{6,5,3,1,4,2,0:T(8,128)(2,1)} %bitcast.81), kind=kLoop, calls=%fused_computation.4 | loop fusion | flops 3145728 | bytes 4194304 | tf_op jit(solution)/shard_map/stack | solution.py:132
  114.0 3.3 %rev.31 = bf16[4,4,2,4,2,8,512]{6,5,3,1,4,2,0:T(8,128)(2,1)} reverse(bf16[4,4,2,4,2,8,512]{6,5,3,1,4,2,0:T(8,128)(2,1)} %pad_maximum_fusion), dimensions={0} | reverse | bytes 4194304 | tf_op jit(solution)/shard_map/jit(_flip)/rev | solution.py:40
  117.5 2.8 %collective-permute-start.22 = (f32[4,2,4,8,128]{4,3,2,1,0:T(8,128)S(1)}, f32[4,2,4,8,128]{4,3,2,1,0:T(8,128)S(1)}, u32[]{:S(2)}, u32[]{:S(2)}) collective-permute-start(f32[4,2,4,8,128]{4,3,2,1,0:T(8,128)S(1)} %get-tuple-element.30), channel_id=1, source_target_pairs={{0,2},{1,3},{2,0},{3,1},{4,6},{5,7},{6,4},{7,5},{8,10},{9,11},{10,... | collective-permute-start | bytes 393224 | tf_op jit(solution)/shard_map/ppermute | solution.py:15
  120.3 1.1 collective-permute-start.23
  121.4 2.2 %add.274 = f32[1024,512]{1,0:T(8,128)S(1)} add(f32[1024,512]{1,0:T(8,128)S(1)} %copy-done.3, f32[1024,512]{1,0:T(8,128)} %collective-permute-done.36) | non-fusion elementwise | flops 524288 | bytes 6291456 | tf_op jit(solution)/shard_map/add | solution.py:167
  123.7 1.7 %collective-permute-start.37 = (bf16[16,2,8,512]{3,2,0,1:T(8,128)(2,1)S(1)}, bf16[16,2,8,512]{3,2,0,1:T(8,128)(2,1)S(1)}, u32[]{:S(2)}, u32[]{:S(2)}) collective-permute-start(bf16[16,2,8,512]{3,2,0,1:T(8,128)(2,1)S(1)} %get-tuple-element.5), channel_id=1, source_target_pairs={{0,32},{32,64},{64,96},{96,0},{1,33},{33,65},{65,97},{97,1},{2,34}... | collective-permute-start | bytes 786440 | tf_op jit(solution)/shard_map/ppermute | solution.py:15
  125.8 1.7 %collective-permute-start.39 = (bf16[16,2,8,512]{3,2,0,1:T(8,128)(2,1)S(1)}, bf16[16,2,8,512]{3,2,0,1:T(8,128)(2,1)S(1)}, u32[]{:S(2)}, u32[]{:S(2)}) collective-permute-start(bf16[16,2,8,512]{3,2,0,1:T(8,128)(2,1)S(1)} %get-tuple-element.6), channel_id=1, source_target_pairs={{0,96},{32,0},{64,32},{96,64},{1,97},{33,1},{65,33},{97,65},{2,98}... | collective-permute-start | bytes 786440 | tf_op jit(solution)/shard_map/ppermute | solution.py:15
  127.6 0.7 fusion.1
  128.8 1.4 collective-permute-done.37
  130.2 3.1 %collective-permute-done.38 = bf16[16,2,8,512]{3,2,0,1:T(8,128)(2,1)S(1)} collective-permute-done((bf16[16,2,8,512]{3,2,0,1:T(8,128)(2,1)S(1)}, bf16[16,2,8,512]{3,2,0,1:T(8,128)(2,1)S(1)}, u32[]{:S(2)}, u32[]{:S(2)}) %collective-permute-start.38) | collective-permute-done | bytes 262176 | tf_op jit(solution)/shard_map/ppermute | solution.py:15
  133.4 1.7 %collective-permute-done.39 = bf16[16,2,8,512]{3,2,0,1:T(8,128)(2,1)S(1)} collective-permute-done((bf16[16,2,8,512]{3,2,0,1:T(8,128)(2,1)S(1)}, bf16[16,2,8,512]{3,2,0,1:T(8,128)(2,1)S(1)}, u32[]{:S(2)}, u32[]{:S(2)}) %collective-permute-start.39) | collective-permute-done | bytes 262176 | tf_op jit(solution)/shard_map/ppermute | solution.py:15
  135.2 1.3 collective-permute-start.40
  136.5 8.4 %collective-permute-done.40 = bf16[16,8,512]{2,1,0:T(8,128)(2,1)S(1)} collective-permute-done((bf16[16,8,512]{2,1,0:T(8,128)(2,1)S(1)}, bf16[16,8,512]{2,1,0:T(8,128)(2,1)S(1)}, u32[]{:S(2)}, u32[]{:S(2)}) %collective-permute-start.40) | collective-permute-done | bytes 131104 | tf_op jit(solution)/shard_map/ppermute | solution.py:15
  144.9 3.3 %shard_map.40 = bf16[128,512]{1,0:T(8,128)(2,1)S(1)} custom-call(s32[1]{0:T(128)} %bitcast.which.core, f32[4,4,2,4,8,128]{5,4,3,2,1,0:T(8,128)S(1)} %pad_maximum_fusion.2.mine_pairs, f32[4,4,2,4,8,128]{5,4,3,2,1,0:T(8,128)S(1)} %collective-permute-done.24.twin_pairs, bf16[4,4,128,512]{3,2,1,0:T(8,128)(2,1)S(1)} %bitcast.177, ...), custom_call_target="tpu_custom_call" | custom-call | flops 536870912 | bytes 3670020 | tf_op jit(solution)/shard_map/pallas_call | solution.py:96
  148.4 13.5 %all_to_all.5 = bf16[16,8,512]{2,1,0:T(8,128)(2,1)S(1)} all-to-all(bf16[16,8,512]{2,1,0:T(8,128)(2,1)S(1)} %bitcast.199), channel_id=1, replica_groups=mesh['zh'=2,'x'=4,'core'=2,'zl'=4,'y'=4] {'zl','y'}, dimensions={0} | all-to-all | bytes 262144 | tf_op jit(solution)/shard_map/all_to_all | solution.py:180
  162.1 1.2 collective-permute-done.41
  (103 shorter events, 9.9 us)
Async XLA Ops:
  0.0 8.9 %copy-start.5 = (bf16[4,16384]{1,0:T(4,128)(2,1)S(1)}, bf16[4,16384]{1,0:T(4,128)(2,1)}, u32[]{:S(2)}) copy-start(bf16[4,16384]{1,0:T(4,128)(2,1)} %param.3) | copy-start | bytes 393220
  0.0 9.2 %copy-start.6 = (bf16[4,16384]{1,0:T(4,128)(2,1)S(1)}, bf16[4,16384]{1,0:T(4,128)(2,1)}, u32[]{:S(2)}) copy-start(bf16[4,16384]{1,0:T(4,128)(2,1)} %param.4) | copy-start | bytes 393220
  0.0 1.6 collective-permute-start
  0.0 2.8 %collective-permute-start.1 = (bf16[4,16384]{1,0:T(4,128)(2,1)}, bf16[4,16384]{1,0:T(4,128)(2,1)S(1)}, u32[]{:S(2)}, u32[]{:S(2)}) collective-permute-start(bf16[4,16384]{1,0:T(4,128)(2,1)} %param.4), channel_id=1, source_target_pairs={{0,16},{16,0},{1,17},{17,1},{2,18},{18,2},{3,19},{19,3},{4,20},{20... | collective-permute-start | bytes 393224 | tf_op jit(solution)/shard_map/ppermute | solution.py:15
  4.1 5.3 %collective-permute-start.2 = (bf16[2,2,8,1024]{3,2,0,1:T(8,128)(2,1)S(1)}, bf16[2,2,8,1024]{3,2,0,1:T(8,128)(2,1)S(1)}, u32[]{:S(2)}, u32[]{:S(2)}) collective-permute-start(bf16[2,2,8,1024]{3,2,0,1:T(8,128)(2,1)S(1)} %get-tuple-element.16), channel_id=1, source_target_pairs={{0,32},{32,64},{64,96},{96,0},{1,33},{33,65},{65,97},{97,1},{2,34}... | collective-permute-start | bytes 196616 | tf_op jit(solution)/shard_map/ppermute | solution.py:15
  5.7 6.2 %collective-permute-start.3 = (bf16[2,2,8,1024]{3,2,0,1:T(8,128)(2,1)S(1)}, bf16[2,2,8,1024]{3,2,0,1:T(8,128)(2,1)S(1)}, u32[]{:S(2)}, u32[]{:S(2)}) collective-permute-start(bf16[2,2,8,1024]{3,2,0,1:T(8,128)(2,1)S(1)} %get-tuple-element.17), channel_id=1, source_target_pairs={{0,64},{32,96},{64,0},{96,32},{1,65},{33,97},{65,1},{97,33},{2,66}... | collective-permute-start | bytes 196616 | tf_op jit(solution)/shard_map/ppermute | solution.py:15
  8.5 4.3 %collective-permute-start.4 = (bf16[2,2,8,1024]{3,2,0,1:T(8,128)(2,1)S(1)}, bf16[2,2,8,1024]{3,2,0,1:T(8,128)(2,1)S(1)}, u32[]{:S(2)}, u32[]{:S(2)}) collective-permute-start(bf16[2,2,8,1024]{3,2,0,1:T(8,128)(2,1)S(1)} %get-tuple-element.15), channel_id=1, source_target_pairs={{0,96},{32,0},{64,32},{96,64},{1,97},{33,1},{65,33},{97,65},{2,98}... | collective-permute-start | bytes 196616 | tf_op jit(solution)/shard_map/ppermute | solution.py:15
  12.8 11.5 %collective-permute-start.5 = (bf16[4,2,8,1024]{3,2,0,1:T(8,128)(2,1)S(1)}, bf16[4,2,8,1024]{3,2,0,1:T(8,128)(2,1)S(1)}, u32[]{:S(2)}, u32[]{:S(2)}) collective-permute-start(bf16[4,2,8,1024]{3,2,0,1:T(8,128)(2,1)S(1)} %get-tuple-element.25), channel_id=1, source_target_pairs={{0,128},{128,0},{1,129},{129,1},{2,130},{130,2},{3,131},{131,3},{4... | collective-permute-start | bytes 393224 | tf_op jit(solution)/shard_map/ppermute | solution.py:15
  19.2 9.2 %collective-permute-start.25 = (bf16[4,2,8,512]{3,2,0,1:T(8,128)(2,1)S(1)}, bf16[4,2,8,512]{3,2,0,1:T(8,128)(2,1)S(1)}, u32[]{:S(2)}, u32[]{:S(2)}) collective-permute-start(bf16[4,2,8,512]{3,2,0,1:T(8,128)(2,1)S(1)} %get-tuple-element.11), channel_id=1, source_target_pairs={{0,4},{4,8},{8,12},{12,0},{1,5},{5,9},{9,13},{13,1},{2,6},{6,10},{... | collective-permute-start | bytes 196616 | tf_op jit(solution)/shard_map/ppermute | solution.py:15
  20.3 12.2 %collective-permute-start.26 = (bf16[4,2,8,512]{3,2,0,1:T(8,128)(2,1)S(1)}, bf16[4,2,8,512]{3,2,0,1:T(8,128)(2,1)S(1)}, u32[]{:S(2)}, u32[]{:S(2)}) collective-permute-start(bf16[4,2,8,512]{3,2,0,1:T(8,128)(2,1)S(1)} %get-tuple-element.10), channel_id=1, source_target_pairs={{0,8},{4,12},{8,0},{12,4},{1,9},{5,13},{9,1},{13,5},{2,10},{6,14},... | collective-permute-start | bytes 196616 | tf_op jit(solution)/shard_map/ppermute | solution.py:15
  21.8 10.7 %collective-permute-start.27 = (bf16[4,2,8,512]{3,2,0,1:T(8,128)(2,1)S(1)}, bf16[4,2,8,512]{3,2,0,1:T(8,128)(2,1)S(1)}, u32[]{:S(2)}, u32[]{:S(2)}) collective-permute-start(bf16[4,2,8,512]{3,2,0,1:T(8,128)(2,1)S(1)} %get-tuple-element.9), channel_id=1, source_target_pairs={{0,12},{4,0},{8,4},{12,8},{1,13},{5,1},{9,5},{13,9},{2,14},{6,2},{... | collective-permute-start | bytes 196616 | tf_op jit(solution)/shard_map/ppermute | solution.py:15
  24.4 12.8 %collective-permute-start.6 = (bf16[64,1024]{1,0:T(8,128)(2,1)S(1)}, bf16[64,1024]{1,0:T(8,128)(2,1)S(1)}, u32[]{:S(2)}, u32[]{:S(2)}) collective-permute-start(bf16[64,1024]{1,0:T(8,128)(2,1)S(1)} %bitcast.200), channel_id=1, source_target_pairs={{0,4},{4,8},{8,12},{12,0},{1,5},{5,9},{9,13},{13,1},{2,6},{6,10},{... | collective-permute-start | bytes 393224 | tf_op jit(solution)/shard_map/ppermute | solution.py:15
  28.2 10.6 %collective-permute-start.7 = (bf16[64,1024]{1,0:T(8,128)(2,1)S(1)}, bf16[64,1024]{1,0:T(8,128)(2,1)S(1)}, u32[]{:S(2)}, u32[]{:S(2)}) collective-permute-start(bf16[64,1024]{1,0:T(8,128)(2,1)S(1)} %bitcast.201), channel_id=1, source_target_pairs={{0,8},{4,12},{8,0},{12,4},{1,9},{5,13},{9,1},{13,5},{2,10},{6,14},... | collective-permute-start | bytes 393224 | tf_op jit(solution)/shard_map/ppermute | solution.py:15
  28.4 10.3 %collective-permute-start.8 = (bf16[64,1024]{1,0:T(8,128)(2,1)S(1)}, bf16[64,1024]{1,0:T(8,128)(2,1)S(1)}, u32[]{:S(2)}, u32[]{:S(2)}) collective-permute-start(bf16[64,1024]{1,0:T(8,128)(2,1)S(1)} %bitcast.202), channel_id=1, source_target_pairs={{0,12},{4,0},{8,4},{12,8},{1,13},{5,1},{9,5},{13,9},{2,14},{6,2},{... | collective-permute-start | bytes 393224 | tf_op jit(solution)/shard_map/ppermute | solution.py:15
  32.6 8.0 %collective-permute-start.28 = (bf16[4,2,8,512]{3,2,0,1:T(8,128)(2,1)S(1)}, bf16[4,2,8,512]{3,2,0,1:T(8,128)(2,1)S(1)}, u32[]{:S(2)}, u32[]{:S(2)}) collective-permute-start(bf16[4,2,8,512]{3,2,0,1:T(8,128)(2,1)S(1)} %get-tuple-element.21), channel_id=1, source_target_pairs={{0,1},{1,2},{2,3},{3,0},{4,5},{5,6},{6,7},{7,4},{8,9},{9,10},{10,1... | collective-permute-start | bytes 196616 | tf_op jit(solution)/shard_map/ppermute | solution.py:15
  34.3 6.4 %collective-permute-start.29 = (bf16[4,2,8,512]{3,2,0,1:T(8,128)(2,1)S(1)}, bf16[4,2,8,512]{3,2,0,1:T(8,128)(2,1)S(1)}, u32[]{:S(2)}, u32[]{:S(2)}) collective-permute-start(bf16[4,2,8,512]{3,2,0,1:T(8,128)(2,1)S(1)} %get-tuple-element.20), channel_id=1, source_target_pairs={{0,2},{1,3},{2,0},{3,1},{4,6},{5,7},{6,4},{7,5},{8,10},{9,11},{10,... | collective-permute-start | bytes 196616 | tf_op jit(solution)/shard_map/ppermute | solution.py:15
  37.2 4.3 %collective-permute-start.30 = (bf16[4,2,8,512]{3,2,0,1:T(8,128)(2,1)S(1)}, bf16[4,2,8,512]{3,2,0,1:T(8,128)(2,1)S(1)}, u32[]{:S(2)}, u32[]{:S(2)}) collective-permute-start(bf16[4,2,8,512]{3,2,0,1:T(8,128)(2,1)S(1)} %get-tuple-element.19), channel_id=1, source_target_pairs={{0,3},{1,0},{2,1},{3,2},{4,7},{5,4},{6,5},{7,6},{8,11},{9,8},{10,9... | collective-permute-start | bytes 196616 | tf_op jit(solution)/shard_map/ppermute | solution.py:15
  38.8 15.1 %collective-permute-start.9 = (bf16[4,64,1024]{2,1,0:T(8,128)(2,1)S(1)}, bf16[4,64,1024]{2,1,0:T(8,128)(2,1)S(1)}, u32[]{:S(2)}, u32[]{:S(2)}) collective-permute-start(bf16[4,64,1024]{2,1,0:T(8,128)(2,1)S(1)} %pad_maximum_fusion.1.a0), channel_id=1, source_target_pairs={{0,1},{1,2},{2,3},{3,0},{4,5},{5,6},{6,7},{7,4},{8,9},{9,10},{10,1... | collective-permute-start | bytes 1572872 | tf_op jit(solution)/shard_map/ppermute | solution.py:15
  42.2 16.8 %collective-permute-start.31 = (bf16[4,4,2,8,512]{4,3,1,0,2:T(8,128)(2,1)}, bf16[4,4,2,8,512]{4,3,1,0,2:T(8,128)(2,1)}, u32[]{:S(2)}, u32[]{:S(2)}) collective-permute-start(bf16[4,4,2,8,512]{4,3,1,0,2:T(8,128)(2,1)} %pad_maximum_fusion.8), channel_id=1, source_target_pairs={{0,128},{128,0},{1,129},{129,1},{2,130},{130,2},{3,131},{131,3},{4... | collective-permute-start | bytes 786440 | tf_op jit(solution)/shard_map/ppermute | solution.py:15
  47.0 15.8 %collective-permute-start.11 = (bf16[4,64,1024]{2,1,0:T(8,128)(2,1)S(1)}, bf16[4,64,1024]{2,1,0:T(8,128)(2,1)}, u32[]{:S(2)}, u32[]{:S(2)}) collective-permute-start(bf16[4,64,1024]{2,1,0:T(8,128)(2,1)S(1)} %pad_maximum_fusion.1.a0), channel_id=1, source_target_pairs={{0,3},{1,0},{2,1},{3,2},{4,7},{5,4},{6,5},{7,6},{8,11},{9,8},{10,9... | collective-permute-start | bytes 1572872 | tf_op jit(solution)/shard_map/ppermute | solution.py:15
  54.7 15.0 %collective-permute-start.10 = (bf16[2,64,1024]{2,1,0:T(8,128)(2,1)}, bf16[2,64,1024]{2,1,0:T(8,128)(2,1)}, u32[]{:S(2)}, u32[]{:S(2)}) collective-permute-start(bf16[2,64,1024]{2,1,0:T(8,128)(2,1)} %slice.78), channel_id=1, source_target_pairs={{0,1},{1,2},{2,3},{3,0},{4,5},{5,6},{6,7},{7,4},{8,9},{9,10},{10,1... | collective-permute-start | bytes 786440 | tf_op jit(solution)/shard_map/ppermute | solution.py:15
  63.8 8.1 %copy-start = (f32[1024,1024]{1,0:T(8,128)S(1)}, f32[1024,1024]{1,0:T(8,128)}, u32[]{:S(2)}) copy-start(f32[1024,1024]{1,0:T(8,128)} %kept.3) | copy-start | bytes 12582916
  63.8 6.9 %collective-permute-start.12 = (bf16[2,64,1024]{2,1,0:T(8,128)(2,1)S(1)}, bf16[2,64,1024]{2,1,0:T(8,128)(2,1)S(1)}, u32[]{:S(2)}, u32[]{:S(2)}) collective-permute-start(bf16[2,64,1024]{2,1,0:T(8,128)(2,1)S(1)} %slice.79), channel_id=1, source_target_pairs={{0,3},{1,0},{2,1},{3,2},{4,7},{5,4},{6,5},{7,6},{8,11},{9,8},{10,9... | collective-permute-start | bytes 786440 | tf_op jit(solution)/shard_map/ppermute | solution.py:15
  67.7 11.2 %collective-permute-start.32 = (bf16[4,2,4,2,8,512]{5,4,2,0,3,1:T(8,128)(2,1)}, bf16[4,2,4,2,8,512]{5,4,2,0,3,1:T(8,128)(2,1)}, u32[]{:S(2)}, u32[]{:S(2)}) collective-permute-start(bf16[4,2,4,2,8,512]{5,4,2,0,3,1:T(8,128)(2,1)} %fusion.3), channel_id=1, source_target_pairs={{0,32},{32,64},{64,96},{96,0},{1,33},{33,65},{65,97},{97,1},{2,34}... | collective-permute-start | bytes 1572872 | tf_op jit(solution)/shard_map/ppermute | solution.py:15
  69.2 12.3 %collective-permute-start.34 = (bf16[4,2,4,2,8,512]{5,4,2,0,3,1:T(8,128)(2,1)}, bf16[4,2,4,2,8,512]{5,4,2,0,3,1:T(8,128)(2,1)}, u32[]{:S(2)}, u32[]{:S(2)}) collective-permute-start(bf16[4,2,4,2,8,512]{5,4,2,0,3,1:T(8,128)(2,1)} %fusion.3), channel_id=1, source_target_pairs={{0,96},{32,0},{64,32},{96,64},{1,97},{33,1},{65,33},{97,65},{2,98}... | collective-permute-start | bytes 1572872 | tf_op jit(solution)/shard_map/ppermute | solution.py:15
  75.1 46.3 %collective-permute-start.36 = (f32[1024,512]{1,0:T(8,128)}, f32[1024,512]{1,0:T(8,128)}, u32[]{:S(2)}, u32[]{:S(2)}) collective-permute-start(f32[1024,512]{1,0:T(8,128)} %shard_map.39), channel_id=1, source_target_pairs={{0,16},{16,0},{1,17},{17,1},{2,18},{18,2},{3,19},{19,3},{4,20},{20... | collective-permute-start | bytes 6291464 | tf_op jit(solution)/shard_map/ppermute | solution.py:15
  77.0 5.5 %collective-permute-start.13 = (f32[2,4,2,4,8,128]{5,4,1,0,2,3:T(8,128)S(1)}, f32[2,4,2,4,8,128]{5,4,1,0,2,3:T(8,128)S(1)}, u32[]{:S(2)}, u32[]{:S(2)}) collective-permute-start(f32[2,4,2,4,8,128]{5,4,1,0,2,3:T(8,128)S(1)} %bitcast.204), channel_id=1, source_target_pairs={{0,16},{16,0},{1,17},{17,1},{2,18},{18,2},{3,19},{19,3},{4,20},{20... | collective-permute-start | bytes 786440 | tf_op jit(solution)/shard_map/ppermute | solution.py:15
  79.9 20.0 %collective-permute-start.33 = (bf16[2,2,4,2,8,512]{5,4,2,0,3,1:T(8,128)(2,1)S(1)}, bf16[2,2,4,2,8,512]{5,4,2,0,3,1:T(8,128)(2,1)S(1)}, u32[]{:S(2)}, u32[]{:S(2)}) collective-permute-start(bf16[2,2,4,2,8,512]{5,4,2,0,3,1:T(8,128)(2,1)S(1)} %slice.86), channel_id=1, source_target_pairs={{0,32},{32,64},{64,96},{96,0},{1,33},{33,65},{65,97},{97,1},{2,34}... | collective-permute-start | bytes 786440 | tf_op jit(solution)/shard_map/ppermute | solution.py:15
  82.5 11.8 %collective-permute-start.14 = (f32[2,4,2,8,128]{4,3,1,0,2:T(8,128)S(1)}, f32[2,4,2,8,128]{4,3,1,0,2:T(8,128)S(1)}, u32[]{:S(2)}, u32[]{:S(2)}) collective-permute-start(f32[2,4,2,8,128]{4,3,1,0,2:T(8,128)S(1)} %get-tuple-element.24), channel_id=1, source_target_pairs={{0,32},{32,64},{64,96},{96,0},{1,33},{33,65},{65,97},{97,1},{2,34}... | collective-permute-start | bytes 196616 | tf_op jit(solution)/shard_map/ppermute | solution.py:15
  84.6 10.3 %collective-permute-start.15 = (f32[2,4,2,8,128]{4,3,1,0,2:T(8,128)S(1)}, f32[2,4,2,8,128]{4,3,1,0,2:T(8,128)S(1)}, u32[]{:S(2)}, u32[]{:S(2)}) collective-permute-start(f32[2,4,2,8,128]{4,3,1,0,2:T(8,128)S(1)} %get-tuple-element.22), channel_id=1, source_target_pairs={{0,64},{32,96},{64,0},{96,32},{1,65},{33,97},{65,1},{97,33},{2,66}... | collective-permute-start | bytes 196616 | tf_op jit(solution)/shard_map/ppermute | solution.py:15
  86.2 8.7 %collective-permute-start.16 = (f32[2,4,2,8,128]{4,3,1,0,2:T(8,128)S(1)}, f32[2,4,2,8,128]{4,3,1,0,2:T(8,128)S(1)}, u32[]{:S(2)}, u32[]{:S(2)}) collective-permute-start(f32[2,4,2,8,128]{4,3,1,0,2:T(8,128)S(1)} %get-tuple-element.23), channel_id=1, source_target_pairs={{0,96},{32,0},{64,32},{96,64},{1,97},{33,1},{65,33},{97,65},{2,98}... | collective-permute-start | bytes 196616 | tf_op jit(solution)/shard_map/ppermute | solution.py:15
  88.7 2.2 %copy-start.1 = (f32[1024,1024]{1,0:T(8,128)S(1)}, f32[1024,1024]{1,0:T(8,128)}, u32[]{:S(2)}) copy-start(f32[1024,1024]{1,0:T(8,128)} %kept.3) | copy-start | bytes 12582916
  93.0 1.4 copy-start.2
  94.3 6.7 %collective-permute-start.35 = (bf16[2,2,4,2,8,512]{5,4,2,0,3,1:T(8,128)(2,1)S(1)}, bf16[2,2,4,2,8,512]{5,4,2,0,3,1:T(8,128)(2,1)S(1)}, u32[]{:S(2)}, u32[]{:S(2)}) collective-permute-start(bf16[2,2,4,2,8,512]{5,4,2,0,3,1:T(8,128)(2,1)S(1)} %slice.87), channel_id=1, source_target_pairs={{0,96},{32,0},{64,32},{96,64},{1,97},{33,1},{65,33},{97,65},{2,98}... | collective-permute-start | bytes 786440 | tf_op jit(solution)/shard_map/ppermute | solution.py:15
  94.9 8.2 %collective-permute-start.17 = (f32[2,4,8,128]{3,2,1,0:T(8,128)S(1)}, f32[2,4,8,128]{3,2,1,0:T(8,128)S(1)}, u32[]{:S(2)}, u32[]{:S(2)}) collective-permute-start(f32[2,4,8,128]{3,2,1,0:T(8,128)S(1)} %slice_bitcast_fusion.9), channel_id=1, source_target_pairs={{0,128},{128,0},{1,129},{129,1},{2,130},{130,2},{3,131},{131,3},{4... | collective-permute-start | bytes 98312 | tf_op jit(solution)/shard_map/ppermute | solution.py:15
  103.2 14.2 %collective-permute-start.18 = (f32[2,4,8,128]{3,2,1,0:T(8,128)S(1)}, f32[2,4,8,128]{3,2,1,0:T(8,128)S(1)}, u32[]{:S(2)}, u32[]{:S(2)}) collective-permute-start(f32[2,4,8,128]{3,2,1,0:T(8,128)S(1)} %fusion.22), channel_id=1, source_target_pairs={{0,4},{4,8},{8,12},{12,0},{1,5},{5,9},{9,13},{13,1},{2,6},{6,10},{... | collective-permute-start | bytes 98312 | tf_op jit(solution)/shard_map/ppermute | solution.py:15
  108.6 8.8 %collective-permute-start.19 = (f32[2,4,8,128]{3,2,1,0:T(8,128)S(1)}, f32[2,4,8,128]{3,2,1,0:T(8,128)S(1)}, u32[]{:S(2)}, u32[]{:S(2)}) collective-permute-start(f32[2,4,8,128]{3,2,1,0:T(8,128)S(1)} %fusion.22), channel_id=1, source_target_pairs={{0,8},{4,12},{8,0},{12,4},{1,9},{5,13},{9,1},{13,5},{2,10},{6,14},... | collective-permute-start | bytes 98312 | tf_op jit(solution)/shard_map/ppermute | solution.py:15
  108.6 8.8 %collective-permute-start.20 = (f32[2,4,8,128]{3,2,1,0:T(8,128)S(1)}, f32[2,4,8,128]{3,2,1,0:T(8,128)S(1)}, u32[]{:S(2)}, u32[]{:S(2)}) collective-permute-start(f32[2,4,8,128]{3,2,1,0:T(8,128)S(1)} %fusion.22), channel_id=1, source_target_pairs={{0,12},{4,0},{8,4},{12,8},{1,13},{5,1},{9,5},{13,9},{2,14},{6,2},{... | collective-permute-start | bytes 98312 | tf_op jit(solution)/shard_map/ppermute | solution.py:15
  114.0 7.3 %copy-start.3 = (f32[1024,512]{1,0:T(8,128)S(1)}, f32[1024,512]{1,0:T(8,128)}, u32[]{:S(2)}) copy-start(f32[1024,512]{1,0:T(8,128)} %copy-done.2) | copy-start | bytes 6291460
  117.4 8.5 %collective-permute-start.21 = (f32[4,2,4,8,128]{4,3,2,1,0:T(8,128)S(1)}, f32[4,2,4,8,128]{4,3,2,1,0:T(8,128)S(1)}, u32[]{:S(2)}, u32[]{:S(2)}) collective-permute-start(f32[4,2,4,8,128]{4,3,2,1,0:T(8,128)S(1)} %get-tuple-element.30), channel_id=1, source_target_pairs={{0,1},{1,2},{2,3},{3,0},{4,5},{5,6},{6,7},{7,4},{8,9},{9,10},{10,1... | collective-permute-start | bytes 393224 | tf_op jit(solution)/shard_map/ppermute | solution.py:15
  117.5 11.1 %collective-permute-start.22 = (f32[4,2,4,8,128]{4,3,2,1,0:T(8,128)S(1)}, f32[4,2,4,8,128]{4,3,2,1,0:T(8,128)S(1)}, u32[]{:S(2)}, u32[]{:S(2)}) collective-permute-start(f32[4,2,4,8,128]{4,3,2,1,0:T(8,128)S(1)} %get-tuple-element.30), channel_id=1, source_target_pairs={{0,2},{1,3},{2,0},{3,1},{4,6},{5,7},{6,4},{7,5},{8,10},{9,11},{10,... | collective-permute-start | bytes 393224 | tf_op jit(solution)/shard_map/ppermute | solution.py:15
  120.3 8.4 %collective-permute-start.23 = (f32[4,2,4,8,128]{4,3,2,1,0:T(8,128)S(1)}, f32[4,2,4,8,128]{4,3,2,1,0:T(8,128)S(1)}, u32[]{:S(2)}, u32[]{:S(2)}) collective-permute-start(f32[4,2,4,8,128]{4,3,2,1,0:T(8,128)S(1)} %get-tuple-element.30), channel_id=1, source_target_pairs={{0,3},{1,0},{2,1},{3,2},{4,7},{5,4},{6,5},{7,6},{8,11},{9,8},{10,9... | collective-permute-start | bytes 393224 | tf_op jit(solution)/shard_map/ppermute | solution.py:15
  121.4 6.2 %copy-start.4 = (bf16[4,4,2,4,2,8,512]{6,5,3,1,4,2,0:T(8,128)(2,1)S(1)}, bf16[4,4,2,4,2,8,512]{6,5,3,1,4,2,0:T(8,128)(2,1)}, u32[]{:S(2)}) copy-start(bf16[4,4,2,4,2,8,512]{6,5,3,1,4,2,0:T(8,128)(2,1)} %rev.31) | copy-start | bytes 6291460
  123.7 6.5 %collective-permute-start.37 = (bf16[16,2,8,512]{3,2,0,1:T(8,128)(2,1)S(1)}, bf16[16,2,8,512]{3,2,0,1:T(8,128)(2,1)S(1)}, u32[]{:S(2)}, u32[]{:S(2)}) collective-permute-start(bf16[16,2,8,512]{3,2,0,1:T(8,128)(2,1)S(1)} %get-tuple-element.5), channel_id=1, source_target_pairs={{0,32},{32,64},{64,96},{96,0},{1,33},{33,65},{65,97},{97,1},{2,34}... | collective-permute-start | bytes 786440 | tf_op jit(solution)/shard_map/ppermute | solution.py:15
  125.4 8.0 %collective-permute-start.38 = (bf16[16,2,8,512]{3,2,0,1:T(8,128)(2,1)S(1)}, bf16[16,2,8,512]{3,2,0,1:T(8,128)(2,1)S(1)}, u32[]{:S(2)}, u32[]{:S(2)}) collective-permute-start(bf16[16,2,8,512]{3,2,0,1:T(8,128)(2,1)S(1)} %get-tuple-element.7), channel_id=1, source_target_pairs={{0,64},{32,96},{64,0},{96,32},{1,65},{33,97},{65,1},{97,33},{2,66}... | collective-permute-start | bytes 786440 | tf_op jit(solution)/shard_map/ppermute | solution.py:15
  125.8 9.2 %collective-permute-start.39 = (bf16[16,2,8,512]{3,2,0,1:T(8,128)(2,1)S(1)}, bf16[16,2,8,512]{3,2,0,1:T(8,128)(2,1)S(1)}, u32[]{:S(2)}, u32[]{:S(2)}) collective-permute-start(bf16[16,2,8,512]{3,2,0,1:T(8,128)(2,1)S(1)} %get-tuple-element.6), channel_id=1, source_target_pairs={{0,96},{32,0},{64,32},{96,64},{1,97},{33,1},{65,33},{97,65},{2,98}... | collective-permute-start | bytes 786440 | tf_op jit(solution)/shard_map/ppermute | solution.py:15
  128.7 7.8 %collective-permute-start.24 = (f32[4,4,2,4,8,128]{5,4,3,2,1,0:T(8,128)S(1)}, f32[4,4,2,4,8,128]{5,4,3,2,1,0:T(8,128)S(1)}, u32[]{:S(2)}, u32[]{:S(2)}) collective-permute-start(f32[4,4,2,4,8,128]{5,4,3,2,1,0:T(8,128)S(1)} %pad_maximum_fusion.2.mine_pairs), channel_id=1, source_target_pairs={{0,16},{16,0},{1,17},{17,1},{2,18},{18,2},{3,19},{19,3},{4,20},{20... | collective-permute-start | bytes 1572872 | tf_op jit(solution)/shard_map/ppermute | solution.py:15
  135.2 9.7 %collective-permute-start.40 = (bf16[16,8,512]{2,1,0:T(8,128)(2,1)S(1)}, bf16[16,8,512]{2,1,0:T(8,128)(2,1)S(1)}, u32[]{:S(2)}, u32[]{:S(2)}) collective-permute-start(bf16[16,8,512]{2,1,0:T(8,128)(2,1)S(1)} %fusion.10), channel_id=1, source_target_pairs={{0,128},{128,0},{1,129},{129,1},{2,130},{130,2},{3,131},{131,3},{4... | collective-permute-start | bytes 393224 | tf_op jit(solution)/shard_map/ppermute | solution.py:15
  162.0 1.3 collective-permute-start.41
